TPU v7x, 32 devices: a whole 2x2x4 slice. The times are simulated.
32 devices in a mesh: grp: 2 (over y), slab: 4 (over z), head: 2 (over x), seq: 2 (over core).
Axes of the slice: x: 2, y: 2, z: 4, core: 2. Of those that a mesh axis runs over, the one named last changes fastest.
Arguments:
- queries: bfloat16 [1024, 5120], P(('grp', 'seq'), 'head'), parts along dimension 0, may hold values from -140 to 140
- query_gain: float32 [5120], P('head'), may hold values from 1.5 to 3
- cache_keys: bfloat16 [4096, 5120], P(('grp', 'slab'), 'head'), parts along dimension 0, may hold values from -120 to 120
- cache_values: bfloat16 [4096, 5120], P(('grp', 'slab'), 'head'), parts along dimension 0, may hold values from -6 to 6
- finished_keys: bfloat16 [1024, 5120], P(('grp', 'slab', 'seq'), 'head'), parts along dimension 0, may hold values from -6 to 6
- finished_values: bfloat16 [1024, 5120], P(('grp', 'slab', 'seq'), 'head'), parts along dimension 0, may hold values from -6 to 6
- new_keys: bfloat16 [1024, 5120], P(('grp', 'slab', 'seq'), 'head'), parts along dimension 0, may hold values from -6 to 6
- new_values: bfloat16 [1024, 5120], P(('grp', 'slab', 'seq'), 'head'), parts along dimension 0, may hold values from -6 to 6
- out_weight: bfloat16 [5120, 5120], P('head', 'slab'), may hold values from -0.25 to 0.25
- time_weight: float32 [256, 5120], P(None, ('slab', 'head')), may hold values from -0.375 to 0.375
- owner: int32 [2], P('grp'), parts along dimension 0, may hold values from 0 to 3
- step: int32 [2], P('grp'), parts along dimension 0, may hold values from 0 to 999
Outputs:
- branch: bfloat16 [1024, 5120], P(('grp', 'seq'), ('slab', 'head')), parts along dimension 0
There are 2 independent parts, one for each index of `grp`. A program takes and returns all parts, laid end to end along the dimension named above; an argument that names none is the same for every part. Nothing has to cross between parts.
All inputs are finite; a program needn't handle non-finite values.
Results may differ from a plain program's by a relative error of at most 0.012.
Values may be sent and summed in bfloat16 or wider, within the bound.
No kernel may reach another device: no remote copies, remote signals or barrier semaphores. Data moves between devices by JAX's collectives and lax.ppermute only.
A program may use at most 64 MiB of HBM per device.

v0:
```python
from functools import reduce

import jax
import jax.numpy as jnp
from jax import lax
from jax.sharding import PartitionSpec as P

HEADS = 40
HD = 128


EPSILON = 1e-06


def local(
    queries,
    query_gain,
    cache_keys,
    cache_values,
    finished_keys,
    finished_values,
    new_keys,
    new_values,
    out_weight,
    time_weight,
    owner,
    step,
):
    row_count = queries.shape[0]
    head_count = queries.shape[1] // HD
    query_float = queries.astype(jnp.float32)
    norm_total = lax.psum(jnp.sum(query_float * query_float, axis=1), "head")
    inverse = lax.rsqrt(norm_total / (HEADS * HD) + EPSILON)
    normed = (
        (query_float * inverse[:, None] * query_gain)
        .astype(jnp.bfloat16)
        .reshape(row_count, head_count, HD)
    )
    is_owner = lax.axis_index("slab") == owner[0]
    whole_keys, whole_values = (
        lax.all_gather(finished_keys, ("slab", "seq"), axis=0, tiled=True),
        lax.all_gather(finished_values, ("slab", "seq"), axis=0, tiled=True),
    )
    fresh_keys, fresh_values = (
        lax.all_gather(new_keys, "seq", axis=0, tiled=True),
        lax.all_gather(new_values, "seq", axis=0, tiled=True),
    )
    key_block = jnp.where(is_owner, whole_keys, cache_keys)
    value_block = jnp.where(is_owner, whole_values, cache_values)
    blocks = [
        (key_block, value_block, jnp.float32(0.0)),
        (fresh_keys, fresh_values, jnp.float32(0.0)),
    ]
    score_scale = 1.0 / HD**0.5
    score_list = []
    for key_block, value_block, penalty in blocks:
        key_heads = key_block.reshape(key_block.shape[0], head_count, HD)
        each_score = jnp.einsum(
            "rhd,khd->hrk", normed, key_heads, preferred_element_type=jnp.float32
        )
        score_list.append(each_score * score_scale)
    row_top = reduce(jnp.maximum, [jnp.max(each_score, axis=2) for each_score in score_list])
    row_mass = jnp.zeros_like(row_top)
    partial_value = jnp.zeros((head_count, row_count, HD), jnp.float32)
    for each_score, (key_block, value_block, penalty) in zip(score_list, blocks):
        raw_weights = jnp.exp(each_score - row_top[:, :, None])
        row_mass = row_mass + jnp.sum(raw_weights, axis=2)
        value_heads = value_block.reshape(value_block.shape[0], head_count, HD)
        partial_value = partial_value + jnp.einsum(
            "hrk,khd->hrd",
            raw_weights.astype(jnp.bfloat16),
            value_heads,
            preferred_element_type=jnp.float32,
        )
    global_top = lax.pmax(row_top, "slab")
    factor = jnp.exp(row_top - global_top)
    sum_share, mass_share = (
        lax.psum_scatter(
            partial_value * factor[:, :, None], "slab", scatter_dimension=1, tiled=True
        ),
        lax.psum_scatter(row_mass * factor, "slab", scatter_dimension=1, tiled=True),
    )
    row_share = (sum_share / mass_share[:, :, None]).astype(jnp.bfloat16)
    attended = lax.all_gather(row_share, "slab", axis=1, tiled=True)
    weight_heads = out_weight.reshape(head_count, HD, out_weight.shape[1])
    projected = jnp.einsum(
        "hrd,hdc->rc", attended, weight_heads, preferred_element_type=jnp.float32
    )
    summed = lax.psum_scatter(projected, "head", scatter_dimension=1, tiled=True)
    half = time_weight.shape[0] // 2
    frequency = jnp.exp(-jnp.log(10000.0) * jnp.arange(half, dtype=jnp.float32) / half)
    phases = step[0].astype(jnp.float32) * frequency
    embedding = jnp.concatenate([jnp.cos(phases), jnp.sin(phases)])
    time_gate = 1.0 + jnp.dot(embedding, time_weight, precision=lax.Precision.HIGHEST)
    return (time_gate * summed).astype(jnp.bfloat16)


def solution(mesh):
    in_specs = (
        P(("grp", "seq"), "head"),
        P("head"),
        P(("grp", "slab"), "head"),
        P(("grp", "slab"), "head"),
        P(("grp", "slab", "seq"), "head"),
        P(("grp", "slab", "seq"), "head"),
        P(("grp", "slab", "seq"), "head"),
        P(("grp", "slab", "seq"), "head"),
        P("head", "slab"),
        P(None, ("slab", "head")),
        P("grp"),
        P("grp"),
    )
    out_specs = P(("grp", "seq"), ("slab", "head"))
    return jax.shard_map(local, mesh=mesh, in_specs=in_specs, out_specs=out_specs, check_vma=False)
```

profile of v0, /device:TPU:0, one launch (start us, length us, event | category | flops | bytes accessed | tf_op | source)
XLA Modules:
  0.0 240.0 jit_solution(8406601955525841598)
XLA Ops:
  6.5 0.0 copy-start
  6.5 0.0 all-gather.4.cloned.1.call-start
  6.5 0.7 all-gather.4.cloned.1.call-update
  7.3 0.0 all-gather.6.cloned.1.call-start
  7.3 0.7 all-gather.6.cloned.1.call-update
  8.0 0.0 reduce-scatter.10.cloned.1.call-start
  8.1 0.0 copy-start.3
  8.1 4.5 %copy.36 = bf16[512,2560]{0,1:T(8,128)(2,1)} copy(bf16[512,2560]{1,0:T(8,128)(2,1)} %param.15) | data formatting | bytes 5242880 | tf_op args[3]
  13.3 0.0 copy-done.3
  13.3 0.6 copy.27
  13.9 0.0 copy-start.4
  13.9 0.0 copy-start.5
  13.9 4.5 %copy.29 = bf16[512,2560]{0,1:T(8,128)(2,1)} copy(bf16[512,2560]{1,0:T(8,128)(2,1)} %param.14) | data formatting | bytes 5242880 | tf_op args[2]
  18.4 0.0 copy-done.4
  18.4 2.7 %all_gather.16 = bf16[128,2560]{1,0:T(8,128)(2,1)S(1)} all-gather(bf16[64,2560]{1,0:T(8,128)(2,1)S(1)} %copy-done.4), channel_id=1, replica_groups=mesh['grp'=2,'slab'=4,'head'=2,'seq'=2] {'seq'}, dimensions={0}, use_global_device_ids=true | all-gather | bytes 983040 | tf_op jit(solution)/shard_map/all_gather | solution.py:45
  21.1 0.0 copy-start.6
  21.1 1.1 copy.32
  22.2 0.0 copy-done.5
  22.2 2.3 all_gather.18
  24.4 1.1 copy.38
  25.5 0.4 fusion.6
  25.9 5.5 %psum.7 = f32[256]{0:T(256)S(1)} all-reduce(f32[256]{0:T(256)S(1)} %fusion.6), channel_id=1, replica_groups=mesh['grp'=2,'slab'=4,'head'=2,'seq'=2] {'head'}, use_global_device_ids=true, to_apply=%region_1.0 | all-reduce | flops 256 | bytes 2048 | tf_op jit(solution)/shard_map/psum | solution.py:32
  31.5 0.0 copy-done.6
  31.5 0.4 fusion.8
  31.9 0.0 copy-start.1
  31.9 1.2 copy-done.1
  33.0 1.7 multiply_reduce_fusion.1
  34.7 10.7 %all-gather.4.cloned.1.call-done = bf16[512,2560]{1,0:T(8,128)(2,1)} async-done(((bf16[64,2560]{1,0:T(8,128)(2,1)}), bf16[512,2560]{1,0:T(8,128)(2,1)}) %all-gather.4.cloned.1.call-update) | async-done | bytes 2621456 | tf_op jit(solution)/shard_map/all_gather | solution.py:41
  45.4 4.4 %copy.28 = bf16[512,2560]{0,1:T(8,128)(2,1)} copy(bf16[512,2560]{1,0:T(8,128)(2,1)} %all-gather.4.cloned.1.call-done) | data formatting | bytes 5242880 | tf_op jit(solution)/shard_map/all_gather | solution.py:41
  49.8 0.0 copy-start.2
  49.8 2.1 broadcast_select_fusion.1
  52.0 0.0 copy-done.2
  52.0 5.7 %multiply_reduce_fusion = (f32[20,256]{1,0:T(8,128)S(1)}, f32[20,256,512]{2,1,0:T(8,128)}) fusion(bf16[256,20,128]{0,2,1:T(8,128)(2,1)S(1)} %bitcast.25, bf16[512,20,128]{0,2,1:T(8,128)(2,1)S(1)} %bitcast.27), kind=kOutput, calls=%fused_computation.1 | convolution fusion | flops 676326400 | bytes 14438400 | tf_op jit(solution)/shard_map/rhd,khd->hrk/dot_general | solution.py:58
  57.6 18.7 %pmax.7 = f32[20,256]{1,0:T(8,128)S(1)} all-reduce(f32[20,256]{1,0:T(8,128)S(1)} %max.9), channel_id=1, replica_groups=mesh['grp'=2,'slab'=4,'head'=2,'seq'=2] {'slab'}, use_global_device_ids=true, to_apply=%region_4.5 | all-reduce | flops 5120 | bytes 40960 | tf_op jit(solution)/shard_map/pmax | solution.py:75
  76.4 5.9 %fusion = f32[20,256]{1,0:T(8,128)S(1)} fusion(f32[20,256,512]{2,1,0:T(8,128)} %get-tuple-element.8, f32[20,256]{1,0:T(8,128)S(1)} %max.9), kind=kLoop, calls=%fused_computation.2 | loop fusion | flops 7859200 | bytes 10526720 | tf_op jit(solution)/shard_map/reduce_sum | solution.py:67
  82.2 0.0 all-gather.6.cloned.1.call-done
  82.3 4.4 %copy.35 = bf16[512,2560]{0,1:T(8,128)(2,1)} copy(bf16[512,2560]{1,0:T(8,128)(2,1)} %all-gather.6.cloned.1.call-done) | data formatting | bytes 5242880 | tf_op jit(solution)/shard_map/all_gather | solution.py:42
  86.7 2.0 broadcast_select_fusion
  88.7 7.7 %fusion.2 = f32[20,256,128]{2,1,0:T(8,128)} fusion(bf16[512,20,128]{0,2,1:T(8,128)(2,1)S(1)} %bitcast.26, f32[20,256,512]{2,1,0:T(8,128)} %get-tuple-element.8, f32[20,256]{1,0:T(8,128)S(1)} %max.9), kind=kOutput, calls=%fused_computation.4 | convolution fusion | flops 678952960 | bytes 15749120 | tf_op jit(solution)/shard_map/hrk,khd->hrd/dot_general | solution.py:69
  96.4 0.5 fusion.9
  96.9 0.8 copy.48
  97.6 0.0 reduce-scatter.10.cloned.1.call-update
  97.7 0.0 reduce-scatter.6.cloned.1.call-start
  97.7 4.1 %add_multiply_fusion = f32[20,256,128]{2,1,0:T(8,128)} fusion(f32[20,256,128]{2,1,0:T(8,128)} %fusion.2, bf16[128,20,128]{0,2,1:T(8,128)(2,1)} %bitcast.28, f32[20,256,128]{1,2,0:T(8,128)S(1)} %get-tuple-element.10, f32[20,256]{1,0:T(8,128)S(1)} %get-tuple-element.6, f32[20,256]{1,0:T(8,128)S(1)} %max.9), kind=kOutput, calls=%fused_computation.13 | convolution fusion | flops 171048960 | bytes 8560640 | tf_op jit(solution)/shard_map/hrk,khd->hrd/dot_general | solution.py:69
  101.8 0.0 reduce-scatter.6.cloned.1.call-update
  101.8 0.0 all-gather.8.cloned.1.call-start
  101.9 13.7 %reduce-scatter.10.cloned.1.call-done = f32[64,20]{1,0:T(8,128)} async-done(((f32[256,20]{1,0:T(8,128)}), f32[64,20]{1,0:T(8,128)}) %reduce-scatter.10.cloned.1.call-update) | async-done | bytes 5136
  115.6 0.8 copy.49
  116.4 51.8 %reduce-scatter.6.cloned.1.call-done = f32[20,64,128]{2,1,0:T(8,128)} async-done(((f32[20,256,128]{2,1,0:T(8,128)}), f32[20,64,128]{2,1,0:T(8,128)}) %reduce-scatter.6.cloned.1.call-update) | async-done | bytes 655376 | tf_op jit(solution)/shard_map/reduce_scatter | solution.py:78
  168.2 2.1 divide_convert_fusion
  170.3 0.0 all-gather.8.cloned.1.call-update
  170.3 0.0 reduce-scatter.8.cloned.1.call-start
  170.4 32.2 %all-gather.8.cloned.1.call-done = bf16[20,256,128]{2,1,0:T(8,128)(2,1)} async-done(((bf16[20,64,128]{2,1,0:T(8,128)(2,1)}), bf16[20,256,128]{2,1,0:T(8,128)(2,1)}) %all-gather.8.cloned.1.call-update) | async-done | bytes 1310736 | tf_op jit(solution)/shard_map/all_gather | solution.py:84
  202.5 6.2 %convolution_bitcast_fusion = f32[256,1280]{1,0:T(8,128)} fusion(bf16[20,256,128]{2,1,0:T(8,128)(2,1)} %all-gather.8.cloned.1.call-done, bf16[20,128,1280]{2,1,0:T(8,128)(2,1)} %bitcast.33), kind=kOutput, calls=%fused_computation.9 | convolution fusion | flops 1677721600 | bytes 9175040 | tf_op jit(solution)/shard_map/hrd,hdc->rc/dot_general | solution.py:86
  208.7 0.0 reduce-scatter.8.cloned.1.call-update
  209.5 0.0 copy-done
  209.5 0.4 convolution_reduce_fusion
  209.9 21.4 %reduce-scatter.8.cloned.1.call-done = f32[256,640]{1,0:T(8,128)} async-done(((f32[256,1280]{1,0:T(8,128)}), f32[256,640]{1,0:T(8,128)}) %reduce-scatter.8.cloned.1.call-update) | async-done | bytes 655376 | tf_op jit(solution)/shard_map/reduce_scatter | solution.py:89
  231.3 1.9 multiply_convert_fusion
  (6 shorter events, 0.1 us)
Async XLA Ops:
  6.5 202.9 %copy-start = (f32[256,640]{1,0:T(8,128)S(1)}, f32[256,640]{1,0:T(8,128)}, u32[]{:S(2)}) copy-start(f32[256,640]{1,0:T(8,128)} %param.21) | copy-start | bytes 1966084
  6.5 38.9 %all-gather.4.cloned.1.call-start = ((), (), s32[]{:S(2)}) async-start(), calls=%async_computation.3 | async-start | bytes 2949120 | tf_op jit(solution)/shard_map/all_gather | solution.py:41
  7.3 75.0 %all-gather.6.cloned.1.call-start = ((), (), s32[]{:S(2)}) async-start(), calls=%async_computation.4 | async-start | bytes 2949120 | tf_op jit(solution)/shard_map/all_gather | solution.py:42
  8.0 107.6 %reduce-scatter.10.cloned.1.call-start = ((), (), s32[]{:S(2)}) async-start(), calls=%async_computation.8 | async-start | bytes 163840
  8.1 5.2 %copy-start.3 = (bf16[256,2560]{1,0:T(8,128)(2,1)S(1)}, bf16[256,2560]{1,0:T(8,128)(2,1)}, u32[]{:S(2)}) copy-start(bf16[256,2560]{1,0:T(8,128)(2,1)} %param.12) | copy-start | bytes 3932164
  13.9 4.5 %copy-start.4 = (bf16[64,2560]{1,0:T(8,128)(2,1)S(1)}, bf16[64,2560]{1,0:T(8,128)(2,1)}, u32[]{:S(2)}) copy-start(bf16[64,2560]{1,0:T(8,128)(2,1)} %param.18) | copy-start | bytes 983044
  13.9 8.3 %copy-start.5 = (bf16[64,2560]{1,0:T(8,128)(2,1)S(1)}, bf16[64,2560]{1,0:T(8,128)(2,1)}, u32[]{:S(2)}) copy-start(bf16[64,2560]{1,0:T(8,128)(2,1)} %param.19) | copy-start | bytes 983044
  21.1 10.4 %copy-start.6 = (f32[2560]{0:T(1024)S(1)}, f32[2560]{0:T(1024)}, u32[]{:S(2)}) copy-start(f32[2560]{0:T(1024)} %param.13) | copy-start | bytes 30724
  31.9 1.2 copy-start.1
  49.8 2.1 copy-start.2
  97.7 70.6 %reduce-scatter.6.cloned.1.call-start = ((), (), s32[]{:S(2)}) async-start(), calls=%async_computation.5 | async-start | bytes 3276800 | tf_op jit(solution)/shard_map/reduce_scatter | solution.py:78
  101.8 100.7 %all-gather.8.cloned.1.call-start = ((), (), s32[]{:S(2)}) async-start(), calls=%async_computation.6 | async-start | bytes 1638400 | tf_op jit(solution)/shard_map/all_gather | solution.py:84
  170.3 61.0 %reduce-scatter.8.cloned.1.call-start = ((), (), s32[]{:S(2)}) async-start(), calls=%async_computation.7 | async-start | bytes 1966080 | tf_op jit(solution)/shard_map/reduce_scatter | solution.py:89
Sparse Core Ops, SparseCore 0:
  9.0 36.4 all-gather.3
  47.1 33.8 all-gather.5
  97.8 17.7 reduce-scatter.9
  117.7 50.4 reduce-scatter.5
  170.4 32.0 all-gather.7
  208.9 22.3 reduce-scatter.7
where the time goes:
time: 241 us; the launch traced here: 240 us
  waiting for transfers between devices  131 us (54%)
  blocking collectives  29.2 us (12%)
  matrix products  25.7 us (11%)
  local copies, waits for them, and re-layouts  23.4 us (10%)
  other arithmetic  15.2 us (6%)
  between operations  14.9 us (6%)
    reduce_scatter x1, waiting for transfers between devices, local(): lax.psum_scatter(partial_value * factor[:, :, None], 'slab', scatter_dime...  51.8 us
    all_gather x1, waiting for transfers between devices, local(): attended = lax.all_gather(row_share, 'slab', axis=1, tiled=True)  32.2 us
    reduce_scatter x1, waiting for transfers between devices, local(): lax.psum_scatter(projected, 'head', scatter_dimension=1, tiled=True)  21.4 us
    pmax x1, blocking collectives, local(): global_top = lax.pmax(row_top, 'slab')  18.7 us
    unnamed x7, waiting for transfers between devices  15.2 us
    unnamed x19, local copies, waits for them, and re-layouts  12.4 us
    dot_general x2, matrix products, local(): jnp.einsum('hrk,khd->hrd', raw_weights.astype(jnp.bfloat16), value_heads,...  11.8 us
    all_gather x1, waiting for transfers between devices, local(): lax.all_gather(finished_keys, ('slab', 'seq'), axis=0, tiled=True)  10.7 us
  transfers between devices with their start and end apart: 6, of which 5 were waited for; matrix products, arithmetic and copies ran while one was open for 16% of the time, Pallas kernels for 0%

commit v1 on v0

v1 whole, which is shorter than its diff:
```python
import functools

import jax
import jax.numpy as jnp
from jax import lax
from jax.experimental import pallas as pl
from jax.experimental.pallas import tpu as pltpu
from jax.sharding import PartitionSpec as P

HD = 128
EPSILON = 1e-06
LOG2E = 1.4426950408889634
OUT = -1e30
F32 = jnp.float32
BF16 = jnp.bfloat16
STATS = 16


def chunk_sizes(heads):
    if heads % 2 == 0 and heads >= 8:
        middle = heads - 4
        sizes = [2] + [4] * (middle // 4) + ([middle % 4] if middle % 4 else []) + [2]
        return sizes, 2
    return [1] * (heads % 2) + [2] * (heads // 2), 1


def square_kernel(q_ref, out_ref):
    heads = q_ref.shape[1] // HD
    total = None
    for h in range(heads):
        block = q_ref[:, h * HD : (h + 1) * HD].astype(F32)
        term = block * block
        total = term if total is None else total + term
    row = jnp.sum(total.T, axis=0, keepdims=True)
    out_ref[...] = jnp.broadcast_to(row, out_ref.shape)


def row_squares(queries):
    rows = queries.shape[0]
    return pl.pallas_call(
        square_kernel,
        out_shape=jax.ShapeDtypeStruct((8, rows), F32),
        cost_estimate=pl.CostEstimate(
            flops=2 * queries.size, bytes_accessed=2 * queries.size, transcendentals=0
        ),
        name="row_squares",
    )(queries)


def attend_kernel(
    unit, heads, width, owner_ref, q_ref, gain_ref, own_sq, far_sq, kc, vc, near, far,
    out_ref, inv_s, lse_s,
):
    step = pl.program_id(0)
    half = near.shape[0] // 2
    scale = LOG2E / HD**0.5

    @pl.when(step == 0)
    def _():
        total = own_sq[0:1, :] + far_sq[0:1, :]
        inverse = lax.rsqrt(total / width + EPSILON)
        inv_s[...] = jnp.broadcast_to(inverse, (HD, inverse.shape[1])).T
        lse_s[...] = jnp.zeros_like(lse_s)

    penalty = jnp.where(owner_ref[0] == 1, F32(OUT), F32(0.0))
    nt = (((1,), (1,)), ((), ()))
    tn = (((0,), (0,)), ((), ()))
    for j in range(unit):
        cols = slice(j * HD, (j + 1) * HD)
        normed = (q_ref[:, cols].astype(F32) * inv_s[...] * gain_ref[:, cols]).astype(BF16)
        parts = [
            (kc[:, cols], vc[:, cols], True),
            (near[:half, cols], near[half:, cols], False),
            (far[:half, cols], far[half:, cols], False),
        ]
        scores = [
            lax.dot_general(k, normed, nt, preferred_element_type=F32) for k, _, _ in parts
        ]
        top = None
        for s, (_, _, masked) in zip(scores, parts):
            t = jnp.max(s, axis=0, keepdims=True)
            if masked:
                t = t + penalty
            top = t if top is None else jnp.maximum(top, t)
        base = top * scale
        mass, value = None, None
        for s, (_, v, masked) in zip(scores, parts):
            shift = base - penalty if masked else base
            raw = jnp.exp2(s * scale - shift)
            part_mass = jnp.sum(raw, axis=0, keepdims=True)
            part = lax.dot_general(v, raw.astype(BF16), tn, preferred_element_type=F32)
            mass = part_mass if mass is None else mass + part_mass
            value = part if value is None else value + part
        at = step * unit + j
        out_ref[pl.ds(pl.multiple_of(at * HD, HD), HD), :] = (value * (1.0 / mass)).astype(BF16)
        lse_s[pl.ds(at, 1), :] = base + jnp.log2(mass)

    @pl.when(step == pl.num_programs(0) - 1)
    def _():
        lse = lse_s[0:heads, :]
        high = lse.astype(BF16).astype(F32)
        rest = lse - high
        mid = rest.astype(BF16).astype(F32)
        low = rest - mid
        pad = jnp.zeros((STATS - 3 * heads, lse.shape[1]), F32)
        out_ref[heads * HD :, :] = jnp.concatenate([high, mid, low, pad], axis=0).astype(BF16)


def attend(unit, start, heads, width, is_owner, queries, gain, own_sq, far_sq, kc, vc, near, far):
    rows = queries.shape[0]
    first = start // unit
    wide = unit * HD

    def col(array_rows):
        return pl.BlockSpec((array_rows, wide), lambda i, o: (0, first + i))

    def whole(shape):
        return pl.BlockSpec(shape, lambda i, o: (0, 0))

    keys = kc.shape[0] + near.shape[0]
    out_rows = heads * HD + STATS
    return pl.pallas_call(
        functools.partial(attend_kernel, unit, heads, width),
        out_shape=jax.ShapeDtypeStruct((out_rows, rows), BF16),
        grid_spec=pltpu.PrefetchScalarGridSpec(
            num_scalar_prefetch=1,
            grid=(heads // unit,),
            in_specs=[
                col(rows),
                col(1),
                whole(own_sq.shape),
                whole(far_sq.shape),
                col(kc.shape[0]),
                col(vc.shape[0]),
                col(near.shape[0]),
                col(far.shape[0]),
            ],
            out_specs=whole((out_rows, rows)),
            scratch_shapes=[pltpu.VMEM((rows, HD), F32), pltpu.VMEM((8, rows), F32)],
        ),
        cost_estimate=pl.CostEstimate(
            flops=16 * heads * rows * keys * HD,
            bytes_accessed=4 * heads * keys * HD,
            transcendentals=heads * rows * keys,
        ),
        name="attend",
    )(is_owner, queries, gain, own_sq, far_sq, kc, vc, near, far)


def decode(ref, heads):
    stats = ref[heads * HD :, :].astype(F32)
    return stats[:heads] + stats[heads : 2 * heads] + stats[2 * heads : 3 * heads]


def merge_kernel(heads, final, take_ref, own, got, out_ref):
    take = take_ref[0] == 1
    own_lse = decode(own, heads)
    got_lse = jnp.where(take, decode(got, heads), F32(OUT))
    top = jnp.maximum(own_lse, got_lse)
    own_w = jnp.exp2(own_lse - top)
    got_w = jnp.exp2(got_lse - top)
    mass = own_w + got_w
    share = 1.0 / mass
    own_w, got_w = own_w * share, got_w * share
    for h in range(heads):
        at = slice(h * HD, (h + 1) * HD)
        mixed = own[at, :].astype(F32) * own_w[h : h + 1] + got[at, :].astype(F32) * got_w[h : h + 1]
        out_ref[at, :] = mixed.astype(BF16)
    if not final:
        lse = top + jnp.log2(mass)
        high = lse.astype(BF16).astype(F32)
        rest = lse - high
        mid = rest.astype(BF16).astype(F32)
        low = rest - mid
        pad = jnp.zeros((STATS - 3 * heads, lse.shape[1]), F32)
        out_ref[heads * HD :, :] = jnp.concatenate([high, mid, low, pad], axis=0).astype(BF16)


def merge(heads, final, take, own, got):
    rows = own.shape[1]
    out_rows = heads * HD if final else heads * HD + STATS
    spec = pl.BlockSpec(memory_space=pltpu.VMEM)
    return pl.pallas_call(
        functools.partial(merge_kernel, heads, final),
        out_shape=jax.ShapeDtypeStruct((out_rows, rows), BF16),
        in_specs=[pl.BlockSpec(memory_space=pltpu.SMEM), spec, spec],
        out_specs=spec,
        cost_estimate=pl.CostEstimate(
            flops=4 * own.size, bytes_accessed=6 * own.size, transcendentals=0
        ),
        name="merge",
    )(take, own, got)


def local(
    n_slab, n_head, n_seq,
    queries, query_gain, cache_keys, cache_values, finished_keys, finished_values,
    new_keys, new_values, out_weight, time_weight, owner, step,
):
    heads = queries.shape[1] // HD
    width = queries.shape[1] * n_head
    slab = lax.axis_index("slab")

    near = jnp.concatenate([finished_keys, new_keys, finished_values, new_values], axis=0)
    if n_seq == 2:
        far = lax.ppermute(near, "seq", [(0, 1), (1, 0)])
    own_sq = row_squares(queries)
    if n_head == 2:
        far_sq = lax.ppermute(own_sq, "head", [(0, 1), (1, 0)])
    else:
        far_sq = lax.psum(own_sq, "head")
        own_sq = jnp.zeros_like(own_sq)
    is_owner = (slab == owner).astype(jnp.int32)
    gain = query_gain[None, :]

    sizes, unit = chunk_sizes(heads)
    starts = [sum(sizes[:c]) for c in range(len(sizes))]
    side = n_slab // 2
    projected = jnp.zeros((queries.shape[0], out_weight.shape[1]), F32)
    for start, size in zip(starts, sizes):
        own = attend(
            unit, start, size, width, is_owner, queries, gain, own_sq, far_sq,
            cache_keys, cache_values, near, far,
        )
        for j in range(side - 1):
            got = lax.ppermute(own, "slab", [(j, j + 1), (n_slab - 1 - j, n_slab - 2 - j)])
            take = ((slab == j + 1) | (slab == n_slab - 2 - j)).astype(jnp.int32)[None]
            own = merge(size, False, take, own, got)
        got = lax.ppermute(own, "slab", [(side - 1, side), (side, side - 1)])
        take = jnp.ones((1,), jnp.int32)
        attended = merge(size, True, take, own, got)
        for j in range(side - 2, -1, -1):
            got = lax.ppermute(attended, "slab", [(j + 1, j), (n_slab - 2 - j, n_slab - 1 - j)])
            attended = jnp.where((slab == j) | (slab == n_slab - 1 - j), got, attended)
        block = out_weight[start * HD : (start + size) * HD]
        projected = projected + lax.dot_general(
            attended, block, (((0,), (0,)), ((), ())), preferred_element_type=F32
        )

    half = time_weight.shape[0] // 2
    frequency = jnp.exp(-jnp.log(10000.0) * jnp.arange(half, dtype=F32) / half)
    phases = step[0].astype(F32) * frequency
    embedding = jnp.concatenate([jnp.cos(phases), jnp.sin(phases)])
    time_gate = 1.0 + jnp.dot(embedding, time_weight, precision=lax.Precision.HIGHEST)

    cols = time_weight.shape[1]
    if n_head == 2:
        me = lax.axis_index("head")
        left, right = projected[:, :cols], projected[:, cols:]
        kept = jnp.where(me == 0, left, right)
        sent = jnp.where(me == 0, right, left).astype(BF16)
        summed = kept + lax.ppermute(sent, "head", [(0, 1), (1, 0)]).astype(F32)
    else:
        summed = lax.psum_scatter(projected, "head", scatter_dimension=1, tiled=True)
    return (time_gate * summed).astype(BF16)


def solution(mesh):
    in_specs = (
        P(("grp", "seq"), "head"),
        P("head"),
        P(("grp", "slab"), "head"),
        P(("grp", "slab"), "head"),
        P(("grp", "slab", "seq"), "head"),
        P(("grp", "slab", "seq"), "head"),
        P(("grp", "slab", "seq"), "head"),
        P(("grp", "slab", "seq"), "head"),
        P("head", "slab"),
        P(None, ("slab", "head")),
        P("grp"),
        P("grp"),
    )
    out_specs = P(("grp", "seq"), ("slab", "head"))
    body = functools.partial(local, mesh.shape["slab"], mesh.shape["head"], mesh.shape["seq"])
    return jax.shard_map(body, mesh=mesh, in_specs=in_specs, out_specs=out_specs, check_vma=False)
```

time: 241 us -> 124 us (0.51)
  waiting for transfers between devices: 131 us -> 23.6 us
  Pallas kernels: 0 us -> 47.9 us
  starting transfers between devices: 0.2 us -> 30.4 us
  blocking collectives: 29.2 us -> 0 us
  local copies, waits for them, and re-layouts: 23.4 us -> 7.27 us
  matrix products: 25.7 us -> 11.1 us
  other arithmetic: 15.2 us -> 0.98 us
  between operations: 14.9 us -> 1.83 us
    reduce_scatter x2 -> x0, waiting for transfers between devices: 73.2 us -> none  [the longest x1 51.8 us: local(): lax.psum_scatter(partial_value * factor[:, :, None], 'slab', scatter_dime...]
    pallas_call x0 -> x19, Pallas kernels: none -> 47.9 us  [the longest x6 23.9 us: attend(): pl.pallas_call(functools.partial(attend_kernel, unit, heads, width), out_...]
    all_gather x3 -> x0, waiting for transfers between devices: 42.9 us -> none  [the longest x1 32.2 us: local(): attended = lax.all_gather(row_share, 'slab', axis=1, tiled=True)]
    ppermute x0 -> x21, starting transfers between devices: none -> 30.4 us  [the longest x6 13.2 us: local(): lax.ppermute(own, 'slab', [(j, j + 1), (n_slab - 1 - j, n_slab - 2 - j)])]
    ppermute x0 -> x21, waiting for transfers between devices: none -> 23.6 us  [the longest x6 16.9 us: local(): lax.ppermute(attended, 'slab', [(j + 1, j), (n_slab - 2 - j, n_slab - 1 -...]
    pmax x1 -> x0, blocking collectives: 18.7 us -> none  [local(): global_top = lax.pmax(row_top, 'slab')]
    unnamed x7 -> x0, waiting for transfers between devices: 15.2 us -> none
    dot_general x5 -> x6, matrix products: 25.3 us -> 10.6 us  [local(): lax.dot_general(attended, block, (((0,), (0,)), ((), ())), preferred_elem...]
  transfers between devices with their start and end apart: 6 -> 21, of which waited for: 5 -> 4; matrix products, arithmetic and copies ran while one was open for 16% -> 8% of each run, Pallas kernels for 0% -> 36%
where the time goes in v1:
time: 124 us; the launch traced here: 123 us
  Pallas kernels  47.9 us (39%)
  starting transfers between devices  30.4 us (25%)
  waiting for transfers between devices  23.6 us (19%)
  matrix products  11.1 us (9%)
  local copies, waits for them, and re-layouts  7.27 us (6%)
  between operations  1.83 us (1%)
    pallas_call x6, Pallas kernels, attend(): pl.pallas_call(functools.partial(attend_kernel, unit, heads, width), out_...  23.9 us
    pallas_call x12, Pallas kernels, merge(): pl.pallas_call(functools.partial(merge_kernel, heads, final), out_shape=j...  21.7 us
    ppermute x6, waiting for transfers between devices, local(): lax.ppermute(attended, 'slab', [(j + 1, j), (n_slab - 2 - j, n_slab - 1 -...  16.9 us
    ppermute x6, starting transfers between devices, local(): lax.ppermute(own, 'slab', [(j, j + 1), (n_slab - 1 - j, n_slab - 2 - j)])  13.2 us
    dot_general x6, matrix products, local(): lax.dot_general(attended, block, (((0,), (0,)), ((), ())), preferred_elem...  10.6 us
    ppermute x6, starting transfers between devices, local(): lax.ppermute(attended, 'slab', [(j + 1, j), (n_slab - 2 - j, n_slab - 1 -...  8 us
    unnamed x53, local copies, waits for them, and re-layouts  6.64 us
    ppermute x1, waiting for transfers between devices, local(): summed = kept + lax.ppermute(sent, 'head', [(0, 1), (1, 0)]).astype(F32)  6.04 us
  transfers between devices with their start and end apart: 21, of which 4 were waited for; matrix products, arithmetic and copies ran while one was open for 8% of the time, Pallas kernels for 36%

profile of v1, /device:TPU:0, one launch (start us, length us, event | category | flops | bytes accessed | tf_op | source)
XLA Modules:
  0.0 123.0 jit_solution(16442188629113789047)
XLA Ops:
  0.0 1.1 constant_dynamic-update-slice_fusion.3
  1.1 1.0 constant_dynamic-update-slice_fusion.2
  2.2 0.6 collective-permute-start.1
  2.8 2.2 %row_squares.1.own_sq = f32[8,256]{1,0:T(8,128)} custom-call(bf16[256,2560]{1,0:T(8,128)(2,1)} %q_ref.13), custom_call_target="tpu_custom_call" | custom-call | flops 1310720 | bytes 1310720 | tf_op jit(solution)/shard_map/row_squares/pallas_call | solution.py:40
  5.0 2.9 %collective-permute-start = (f32[8,256]{1,0:T(8,128)}, f32[8,256]{1,0:T(8,128)S(1)}, u32[]{:S(2)}, u32[]{:S(2)}) collective-permute-start(f32[8,256]{1,0:T(8,128)} %row_squares.1.own_sq), channel_id=1, source_target_pairs={{0,2},{2,0},{1,3},{3,1},{4,6},{6,4},{5,7},{7,5},{8,10},{10,8},{9,1... | collective-permute-start | bytes 24584 | tf_op jit(solution)/shard_map/ppermute | solution.py:209
  8.6 0.6 broadcast_in_dim.16.gain_ref
  9.2 0.6 collective-permute-done.far_sq
  9.8 0.6 copy-done.11
  10.3 1.1 copy-done.2
  11.4 3.1 %attend.6.own = bf16[272,256]{1,0:T(8,128)(2,1)} custom-call(s32[1]{0:T(128)S(6)} %convert_element_type.26.owner_ref, bf16[256,2560]{1,0:T(8,128)(2,1)} %q_ref.13, f32[1,2560]{1,0:T(1,128)} %broadcast_in_dim.16.gain_ref, f32[8,256]{1,0:T(8,128)} %row_squares.1.own_sq, f32[8,256]{1,0:T(8,128)} %copy-done.11, bf16[512,2560]{1,0:T(8,128)(2,1)} %kc.11, ...), custom_call_target="tpu_custom_call" | custom-call | flops 805306368 | bytes 786432 | tf_op jit(solution)/shard_map/attend/pallas_call | solution.py:122
  14.5 4.0 %collective-permute-start.2 = (bf16[272,256]{1,0:T(8,128)(2,1)}, bf16[272,256]{1,0:T(8,128)(2,1)S(1)}, u32[]{:S(2)}, u32[]{:S(2)}) collective-permute-start(bf16[272,256]{1,0:T(8,128)(2,1)} %attend.6.own), channel_id=1, source_target_pairs={{0,4},{12,8},{1,5},{13,9},{2,6},{14,10},{3,7},{15,11},{16,20},{28,... | collective-permute-start | bytes 417800 | tf_op jit(solution)/shard_map/ppermute | solution.py:226
  18.5 3.1 %attend.11.own = bf16[272,256]{1,0:T(8,128)(2,1)} custom-call(s32[1]{0:T(128)S(6)} %convert_element_type.26.owner_ref, bf16[256,2560]{1,0:T(8,128)(2,1)} %q_ref.13, f32[1,2560]{1,0:T(1,128)} %broadcast_in_dim.16.gain_ref, f32[8,256]{1,0:T(8,128)} %row_squares.1.own_sq, f32[8,256]{1,0:T(8,128)} %copy-done.11, bf16[512,2560]{1,0:T(8,128)(2,1)} %kc.11, ...), custom_call_target="tpu_custom_call" | custom-call | flops 805306368 | bytes 786432 | tf_op jit(solution)/shard_map/attend/pallas_call | solution.py:122
  21.7 1.3 %collective-permute-start.17 = (bf16[272,256]{1,0:T(8,128)(2,1)}, bf16[272,256]{1,0:T(8,128)(2,1)S(1)}, u32[]{:S(2)}, u32[]{:S(2)}) collective-permute-start(bf16[272,256]{1,0:T(8,128)(2,1)} %attend.11.own), channel_id=1, source_target_pairs={{0,4},{12,8},{1,5},{13,9},{2,6},{14,10},{3,7},{15,11},{16,20},{28,... | collective-permute-start | bytes 417800 | tf_op jit(solution)/shard_map/ppermute | solution.py:226
  23.0 4.4 %attend.7.own = bf16[528,256]{1,0:T(8,128)(2,1)} custom-call(s32[1]{0:T(128)S(6)} %convert_element_type.26.owner_ref, bf16[256,2560]{1,0:T(8,128)(2,1)} %q_ref.13, f32[1,2560]{1,0:T(1,128)} %broadcast_in_dim.16.gain_ref, f32[8,256]{1,0:T(8,128)} %row_squares.1.own_sq, f32[8,256]{1,0:T(8,128)} %copy-done.11, bf16[512,2560]{1,0:T(8,128)(2,1)} %kc.11, ...), custom_call_target="tpu_custom_call" | custom-call | flops 1610612736 | bytes 1572864 | tf_op jit(solution)/shard_map/attend/pallas_call | solution.py:122
  27.4 1.3 %collective-permute-start.5 = (bf16[528,256]{1,0:T(8,128)(2,1)}, bf16[528,256]{1,0:T(8,128)(2,1)S(1)}, u32[]{:S(2)}, u32[]{:S(2)}) collective-permute-start(bf16[528,256]{1,0:T(8,128)(2,1)} %attend.7.own), channel_id=1, source_target_pairs={{0,4},{12,8},{1,5},{13,9},{2,6},{14,10},{3,7},{15,11},{16,20},{28,... | collective-permute-start | bytes 811016 | tf_op jit(solution)/shard_map/ppermute | solution.py:226
  28.7 4.4 %attend.10.own = bf16[528,256]{1,0:T(8,128)(2,1)} custom-call(s32[1]{0:T(128)S(6)} %convert_element_type.26.owner_ref, bf16[256,2560]{1,0:T(8,128)(2,1)} %q_ref.13, f32[1,2560]{1,0:T(1,128)} %broadcast_in_dim.16.gain_ref, f32[8,256]{1,0:T(8,128)} %row_squares.1.own_sq, f32[8,256]{1,0:T(8,128)} %copy-done.11, bf16[512,2560]{1,0:T(8,128)(2,1)} %kc.11, ...), custom_call_target="tpu_custom_call" | custom-call | flops 1610612736 | bytes 1572864 | tf_op jit(solution)/shard_map/attend/pallas_call | solution.py:122
  33.1 1.3 %collective-permute-start.14 = (bf16[528,256]{1,0:T(8,128)(2,1)}, bf16[528,256]{1,0:T(8,128)(2,1)S(1)}, u32[]{:S(2)}, u32[]{:S(2)}) collective-permute-start(bf16[528,256]{1,0:T(8,128)(2,1)} %attend.10.own), channel_id=1, source_target_pairs={{0,4},{12,8},{1,5},{13,9},{2,6},{14,10},{3,7},{15,11},{16,20},{28,... | collective-permute-start | bytes 811016 | tf_op jit(solution)/shard_map/ppermute | solution.py:226
  34.4 4.4 %attend.8.own = bf16[528,256]{1,0:T(8,128)(2,1)} custom-call(s32[1]{0:T(128)S(6)} %convert_element_type.26.owner_ref, bf16[256,2560]{1,0:T(8,128)(2,1)} %q_ref.13, f32[1,2560]{1,0:T(1,128)} %broadcast_in_dim.16.gain_ref, f32[8,256]{1,0:T(8,128)} %row_squares.1.own_sq, f32[8,256]{1,0:T(8,128)} %copy-done.11, bf16[512,2560]{1,0:T(8,128)(2,1)} %kc.11, ...), custom_call_target="tpu_custom_call" | custom-call | flops 1610612736 | bytes 1572864 | tf_op jit(solution)/shard_map/attend/pallas_call | solution.py:122
  38.8 1.3 %collective-permute-start.8 = (bf16[528,256]{1,0:T(8,128)(2,1)}, bf16[528,256]{1,0:T(8,128)(2,1)S(1)}, u32[]{:S(2)}, u32[]{:S(2)}) collective-permute-start(bf16[528,256]{1,0:T(8,128)(2,1)} %attend.8.own), channel_id=1, source_target_pairs={{0,4},{12,8},{1,5},{13,9},{2,6},{14,10},{3,7},{15,11},{16,20},{28,... | collective-permute-start | bytes 811016 | tf_op jit(solution)/shard_map/ppermute | solution.py:226
  40.1 0.7 copy-done.23
  40.8 1.7 %merge.22.own = bf16[272,256]{1,0:T(8,128)(2,1)} custom-call(s32[1]{0:T(128)} %bitcast.2.take_ref, bf16[272,256]{1,0:T(8,128)(2,1)} %attend.11.own, bf16[272,256]{1,0:T(8,128)(2,1)} %copy-done.23), custom_call_target="tpu_custom_call" | custom-call | flops 278528 | bytes 417792 | tf_op jit(solution)/shard_map/merge/pallas_call | solution.py:183
  42.5 0.7 collective-permute-start.18
  43.1 4.4 %attend.9.own = bf16[528,256]{1,0:T(8,128)(2,1)} custom-call(s32[1]{0:T(128)S(6)} %convert_element_type.26.owner_ref, bf16[256,2560]{1,0:T(8,128)(2,1)} %q_ref.13, f32[1,2560]{1,0:T(1,128)} %broadcast_in_dim.16.gain_ref, f32[8,256]{1,0:T(8,128)} %row_squares.1.own_sq, f32[8,256]{1,0:T(8,128)} %copy-done.11, bf16[512,2560]{1,0:T(8,128)(2,1)} %kc.11, ...), custom_call_target="tpu_custom_call" | custom-call | flops 1610612736 | bytes 1572864 | tf_op jit(solution)/shard_map/attend/pallas_call | solution.py:122
  47.6 4.1 %collective-permute-start.11 = (bf16[528,256]{1,0:T(8,128)(2,1)}, bf16[528,256]{1,0:T(8,128)(2,1)S(1)}, u32[]{:S(2)}, u32[]{:S(2)}) collective-permute-start(bf16[528,256]{1,0:T(8,128)(2,1)} %attend.9.own), channel_id=1, source_target_pairs={{0,4},{12,8},{1,5},{13,9},{2,6},{14,10},{3,7},{15,11},{16,20},{28,... | collective-permute-start | bytes 811016 | tf_op jit(solution)/shard_map/ppermute | solution.py:226
  51.7 1.9 %merge.20.own = bf16[528,256]{1,0:T(8,128)(2,1)} custom-call(s32[1]{0:T(128)} %bitcast.2.take_ref, bf16[528,256]{1,0:T(8,128)(2,1)} %attend.10.own, bf16[528,256]{1,0:T(8,128)(2,1)} %copy-done.19), custom_call_target="tpu_custom_call" | custom-call | flops 540672 | bytes 811008 | tf_op jit(solution)/shard_map/merge/pallas_call | solution.py:183
  53.5 0.7 collective-permute-start.15
  54.9 1.7 %merge.12.own = bf16[272,256]{1,0:T(8,128)(2,1)} custom-call(s32[1]{0:T(128)} %bitcast.2.take_ref, bf16[272,256]{1,0:T(8,128)(2,1)} %attend.6.own, bf16[272,256]{1,0:T(8,128)(2,1)} %copy-done.21), custom_call_target="tpu_custom_call" | custom-call | flops 278528 | bytes 417792 | tf_op jit(solution)/shard_map/merge/pallas_call | solution.py:183
  56.6 0.7 collective-permute-start.3
  57.3 1.7 %merge.23 = bf16[256,256]{1,0:T(8,128)(2,1)} custom-call(s32[1]{0:T(128)} %constant.23.clone.1.take_ref, bf16[272,256]{1,0:T(8,128)(2,1)} %merge.22.own, bf16[272,256]{1,0:T(8,128)(2,1)} %copy-done.22), custom_call_target="tpu_custom_call" | custom-call | flops 278528 | bytes 417792 | tf_op jit(solution)/shard_map/merge/pallas_call | solution.py:183
  58.9 1.3 %collective-permute-start.19 = (bf16[256,256]{1,0:T(8,128)(2,1)}, bf16[256,256]{1,0:T(8,128)(2,1)S(1)}, u32[]{:S(2)}, u32[]{:S(2)}) collective-permute-start(bf16[256,256]{1,0:T(8,128)(2,1)} %merge.23), channel_id=1, source_target_pairs={{4,0},{8,12},{5,1},{9,13},{6,2},{10,14},{7,3},{11,15},{20,16},{24,... | collective-permute-start | bytes 393224 | tf_op jit(solution)/shard_map/ppermute | solution.py:233
  60.2 0.1 fusion.27
  60.3 1.9 %merge.14.own = bf16[528,256]{1,0:T(8,128)(2,1)} custom-call(s32[1]{0:T(128)} %bitcast.2.take_ref, bf16[528,256]{1,0:T(8,128)(2,1)} %attend.7.own, bf16[528,256]{1,0:T(8,128)(2,1)} %copy-done.12), custom_call_target="tpu_custom_call" | custom-call | flops 540672 | bytes 811008 | tf_op jit(solution)/shard_map/merge/pallas_call | solution.py:183
  62.2 0.8 collective-permute-start.6
  63.1 1.9 %merge.16.own = bf16[528,256]{1,0:T(8,128)(2,1)} custom-call(s32[1]{0:T(128)} %bitcast.2.take_ref, bf16[528,256]{1,0:T(8,128)(2,1)} %attend.8.own, bf16[528,256]{1,0:T(8,128)(2,1)} %copy-done.13), custom_call_target="tpu_custom_call" | custom-call | flops 540672 | bytes 811008 | tf_op jit(solution)/shard_map/merge/pallas_call | solution.py:183
  64.9 0.7 collective-permute-start.9
  65.6 0.0 copy-done.15
  65.6 1.9 %merge.18.own = bf16[528,256]{1,0:T(8,128)(2,1)} custom-call(s32[1]{0:T(128)} %bitcast.2.take_ref, bf16[528,256]{1,0:T(8,128)(2,1)} %attend.9.own, bf16[528,256]{1,0:T(8,128)(2,1)} %copy-done.15), custom_call_target="tpu_custom_call" | custom-call | flops 540672 | bytes 811008 | tf_op jit(solution)/shard_map/merge/pallas_call | solution.py:183
  67.5 0.7 collective-permute-start.12
  68.2 1.7 %merge.13 = bf16[256,256]{1,0:T(8,128)(2,1)} custom-call(s32[1]{0:T(128)} %constant.23.clone.1.take_ref, bf16[272,256]{1,0:T(8,128)(2,1)} %merge.12.own, bf16[272,256]{1,0:T(8,128)(2,1)} %copy-done.20), custom_call_target="tpu_custom_call" | custom-call | flops 278528 | bytes 417792 | tf_op jit(solution)/shard_map/merge/pallas_call | solution.py:183
  69.9 1.3 %collective-permute-start.4 = (bf16[256,256]{1,0:T(8,128)(2,1)}, bf16[256,256]{1,0:T(8,128)(2,1)S(1)}, u32[]{:S(2)}, u32[]{:S(2)}) collective-permute-start(bf16[256,256]{1,0:T(8,128)(2,1)} %merge.13), channel_id=1, source_target_pairs={{4,0},{8,12},{5,1},{9,13},{6,2},{10,14},{7,3},{11,15},{20,16},{24,... | collective-permute-start | bytes 393224 | tf_op jit(solution)/shard_map/ppermute | solution.py:233
  71.2 1.9 %merge.21 = bf16[512,256]{1,0:T(8,128)(2,1)} custom-call(s32[1]{0:T(128)} %constant.23.clone.1.take_ref, bf16[528,256]{1,0:T(8,128)(2,1)} %merge.20.own, bf16[528,256]{1,0:T(8,128)(2,1)} %copy-done.14), custom_call_target="tpu_custom_call" | custom-call | flops 540672 | bytes 811008 | tf_op jit(solution)/shard_map/merge/pallas_call | solution.py:183
  73.1 1.3 %collective-permute-start.16 = (bf16[512,256]{1,0:T(8,128)(2,1)}, bf16[512,256]{1,0:T(8,128)(2,1)S(1)}, u32[]{:S(2)}, u32[]{:S(2)}) collective-permute-start(bf16[512,256]{1,0:T(8,128)(2,1)} %merge.21), channel_id=1, source_target_pairs={{4,0},{8,12},{5,1},{9,13},{6,2},{10,14},{7,3},{11,15},{20,16},{24,... | collective-permute-start | bytes 786440 | tf_op jit(solution)/shard_map/ppermute | solution.py:233
  74.4 1.5 %fusion.12 = f32[256,1280]{1,0:T(8,128)S(1)} fusion(bf16[2560,1280]{1,0:T(8,128)(2,1)} %param.20, bf16[256,256]{1,0:T(8,128)(2,1)S(1)} %collective-permute-done.19, bf16[256,256]{1,0:T(8,128)(2,1)S(1)} %copy-done.8, pred[]{:T(512)S(6)} %or.4), kind=kOutput, calls=%fused_computation.16 | convolution fusion | flops 167837696 | bytes 2228225 | tf_op jit(solution)/shard_map/dot_general | solution.py:236
  75.9 0.7 copy-done.16
  76.6 1.8 %merge.15 = bf16[512,256]{1,0:T(8,128)(2,1)} custom-call(s32[1]{0:T(128)} %constant.23.clone.1.take_ref, bf16[528,256]{1,0:T(8,128)(2,1)} %merge.14.own, bf16[528,256]{1,0:T(8,128)(2,1)} %copy-done.16), custom_call_target="tpu_custom_call" | custom-call | flops 540672 | bytes 811008 | tf_op jit(solution)/shard_map/merge/pallas_call | solution.py:183
  78.4 1.3 %collective-permute-start.7 = (bf16[512,256]{1,0:T(8,128)(2,1)}, bf16[512,256]{1,0:T(8,128)(2,1)S(1)}, u32[]{:S(2)}, u32[]{:S(2)}) collective-permute-start(bf16[512,256]{1,0:T(8,128)(2,1)} %merge.15), channel_id=1, source_target_pairs={{4,0},{8,12},{5,1},{9,13},{6,2},{10,14},{7,3},{11,15},{20,16},{24,... | collective-permute-start | bytes 786440 | tf_op jit(solution)/shard_map/ppermute | solution.py:233
  79.7 0.7 copy-done.17
  80.4 1.9 %merge.17 = bf16[512,256]{1,0:T(8,128)(2,1)} custom-call(s32[1]{0:T(128)} %constant.23.clone.1.take_ref, bf16[528,256]{1,0:T(8,128)(2,1)} %merge.16.own, bf16[528,256]{1,0:T(8,128)(2,1)} %copy-done.17), custom_call_target="tpu_custom_call" | custom-call | flops 540672 | bytes 811008 | tf_op jit(solution)/shard_map/merge/pallas_call | solution.py:183
  82.3 1.3 %collective-permute-start.10 = (bf16[512,256]{1,0:T(8,128)(2,1)}, bf16[512,256]{1,0:T(8,128)(2,1)S(1)}, u32[]{:S(2)}, u32[]{:S(2)}) collective-permute-start(bf16[512,256]{1,0:T(8,128)(2,1)} %merge.17), channel_id=1, source_target_pairs={{4,0},{8,12},{5,1},{9,13},{6,2},{10,14},{7,3},{11,15},{20,16},{24,... | collective-permute-start | bytes 786440 | tf_op jit(solution)/shard_map/ppermute | solution.py:233
  83.6 0.7 copy-done.18
  84.3 1.9 %merge.19 = bf16[512,256]{1,0:T(8,128)(2,1)} custom-call(s32[1]{0:T(128)} %constant.23.clone.1.take_ref, bf16[528,256]{1,0:T(8,128)(2,1)} %merge.18.own, bf16[528,256]{1,0:T(8,128)(2,1)} %copy-done.18), custom_call_target="tpu_custom_call" | custom-call | flops 540672 | bytes 811008 | tf_op jit(solution)/shard_map/merge/pallas_call | solution.py:183
  86.2 1.6 %collective-permute-start.13 = (bf16[512,256]{1,0:T(8,128)(2,1)}, bf16[512,256]{1,0:T(8,128)(2,1)S(1)}, u32[]{:S(2)}, u32[]{:S(2)}) collective-permute-start(bf16[512,256]{1,0:T(8,128)(2,1)} %merge.19), channel_id=1, source_target_pairs={{4,0},{8,12},{5,1},{9,13},{6,2},{10,14},{7,3},{11,15},{20,16},{24,... | collective-permute-start | bytes 786440 | tf_op jit(solution)/shard_map/ppermute | solution.py:233
  87.8 3.6 %collective-permute-done.16 = bf16[512,256]{1,0:T(8,128)(2,1)S(1)} collective-permute-done((bf16[512,256]{1,0:T(8,128)(2,1)}, bf16[512,256]{1,0:T(8,128)(2,1)S(1)}, u32[]{:S(2)}, u32[]{:S(2)}) %collective-permute-start.16) | collective-permute-done | bytes 262176 | tf_op jit(solution)/shard_map/ppermute | solution.py:233
  91.4 1.9 %fusion.4 = f32[256,1280]{1,0:T(8,128)S(1)} fusion(bf16[2560,1280]{1,0:T(8,128)(2,1)} %param.20, bf16[512,256]{1,0:T(8,128)(2,1)S(1)} %collective-permute-done.16, bf16[512,256]{1,0:T(8,128)(2,1)S(1)} %copy-done.4, pred[]{:T(512)S(6)} %or.4), kind=kOutput, calls=%fused_computation.5 | convolution fusion | flops 335675392 | bytes 3145729 | tf_op jit(solution)/shard_map/dot_general | solution.py:236
  93.3 13.3 %collective-permute-done.13 = bf16[512,256]{1,0:T(8,128)(2,1)S(1)} collective-permute-done((bf16[512,256]{1,0:T(8,128)(2,1)}, bf16[512,256]{1,0:T(8,128)(2,1)S(1)}, u32[]{:S(2)}, u32[]{:S(2)}) %collective-permute-start.13) | collective-permute-done | bytes 262176 | tf_op jit(solution)/shard_map/ppermute | solution.py:233
  106.6 1.9 %fusion.6 = f32[256,1280]{1,0:T(8,128)S(1)} fusion(bf16[2560,1280]{1,0:T(8,128)(2,1)} %param.20, bf16[512,256]{1,0:T(8,128)(2,1)S(1)} %collective-permute-done.13, bf16[512,256]{1,0:T(8,128)(2,1)S(1)} %copy-done.6, pred[]{:T(512)S(6)} %or.4), kind=kOutput, calls=%fused_computation.7 | convolution fusion | flops 335675392 | bytes 3145729 | tf_op jit(solution)/shard_map/dot_general | solution.py:236
  108.5 1.9 %fusion.8 = f32[256,1280]{1,0:T(8,128)S(1)} fusion(bf16[2560,1280]{1,0:T(8,128)(2,1)} %param.20, bf16[512,256]{1,0:T(8,128)(2,1)S(1)} %collective-permute-done.10, bf16[512,256]{1,0:T(8,128)(2,1)S(1)} %copy-done.5, pred[]{:T(512)S(6)} %or.4), kind=kOutput, calls=%fused_computation.9 | convolution fusion | flops 335675392 | bytes 3145729 | tf_op jit(solution)/shard_map/dot_general | solution.py:236
  110.4 1.9 %fusion.10 = f32[256,1280]{1,0:T(8,128)S(1)} fusion(bf16[2560,1280]{1,0:T(8,128)(2,1)} %param.20, bf16[512,256]{1,0:T(8,128)(2,1)S(1)} %collective-permute-done.7, bf16[512,256]{1,0:T(8,128)(2,1)S(1)} %copy-done.3, pred[]{:T(512)S(6)} %or.4), kind=kOutput, calls=%fused_computation.11 | convolution fusion | flops 335675392 | bytes 3145729 | tf_op jit(solution)/shard_map/dot_general | solution.py:236
  112.3 1.7 %fusion.3 = f32[256,1280]{1,0:T(8,128)S(1)} fusion(f32[256,1280]{1,0:T(8,128)S(1)} %fusion.12, f32[256,1280]{1,0:T(8,128)S(1)} %fusion.4, f32[256,1280]{1,0:T(8,128)S(1)} %fusion.6, f32[256,1280]{1,0:T(8,128)S(1)} %fusion.8, f32[256,1280]{1,0:T(8,128)S(1)} %fusion.10, bf16[2560,1280]{1,0:T(8,128)(2,1)} %param.20, ...), kind=kOutput, calls=%fused_computation.4 | convolution fusion | flops 169476096 | bytes 8781825 | tf_op jit(solution)/shard_map/dot_general | solution.py:236
  114.0 0.1 select_convert_fusion
  114.1 1.6 %collective-permute-start.20 = (bf16[256,640]{1,0:T(8,128)(2,1)S(1)}, bf16[256,640]{1,0:T(8,128)(2,1)S(1)}, u32[]{:S(2)}, u32[]{:S(2)}) collective-permute-start(bf16[256,640]{1,0:T(8,128)(2,1)S(1)} %select_convert_fusion), channel_id=1, source_target_pairs={{0,2},{2,0},{1,3},{3,1},{4,6},{6,4},{5,7},{7,5},{8,10},{10,8},{9,1... | collective-permute-start | bytes 983048 | tf_op jit(solution)/shard_map/ppermute | solution.py:252
  115.6 0.4 convolution_reduce_fusion
  116.1 6.0 %collective-permute-done.20 = bf16[256,640]{1,0:T(8,128)(2,1)S(1)} collective-permute-done((bf16[256,640]{1,0:T(8,128)(2,1)S(1)}, bf16[256,640]{1,0:T(8,128)(2,1)S(1)}, u32[]{:S(2)}, u32[]{:S(2)}) %collective-permute-start.20) | collective-permute-done | bytes 327712 | tf_op jit(solution)/shard_map/ppermute | solution.py:252
  122.1 0.8 multiply_convert_fusion
  (64 shorter events, 0.2 us)
Async XLA Ops:
  0.0 115.6 %copy-start = (f32[256,640]{1,0:T(8,128)S(1)}, f32[256,640]{1,0:T(8,128)}, u32[]{:S(2)}) copy-start(f32[256,640]{1,0:T(8,128)} %param.21) | copy-start | bytes 1966084
  0.0 2.1 %copy-start.9 = (bf16[64,2560]{1,0:T(8,128)(2,1)S(1)}, bf16[64,2560]{1,0:T(8,128)(2,1)}, u32[]{:S(2)}) copy-start(bf16[64,2560]{1,0:T(8,128)(2,1)} %param.17) | copy-start | bytes 983044
  0.0 2.2 %copy-start.10 = (bf16[64,2560]{1,0:T(8,128)(2,1)S(1)}, bf16[64,2560]{1,0:T(8,128)(2,1)}, u32[]{:S(2)}) copy-start(bf16[64,2560]{1,0:T(8,128)(2,1)} %param.19) | copy-start | bytes 983044
  2.1 6.4 %copy-start.24 = (f32[2560]{0:T(1024)S(1)}, f32[2560]{0:T(1024)}, u32[]{:S(2)}) copy-start(f32[2560]{0:T(1024)} %param.13) | copy-start | bytes 30724
  2.2 7.5 %copy-start.1 = (bf16[256,2560]{1,0:T(8,128)(2,1)}, bf16[256,2560]{1,0:T(8,128)(2,1)S(1)}, u32[]{:S(2)}) copy-start(bf16[256,2560]{1,0:T(8,128)(2,1)S(1)} %constant_dynamic-update-slice_fusion.near) | copy-start | bytes 3932164
  2.2 7.5 %collective-permute-start.1 = (bf16[256,2560]{1,0:T(8,128)(2,1)S(1)}, bf16[256,2560]{1,0:T(8,128)(2,1)S(1)}, u32[]{:S(2)}, u32[]{:S(2)}) collective-permute-start(bf16[256,2560]{1,0:T(8,128)(2,1)S(1)} %constant_dynamic-update-slice_fusion.near), channel_id=1, source_target_pairs={{0,1},{1,0},{2,3},{3,2},{4,5},{5,4},{6,7},{7,6},{8,9},{9,8},{10,11... | collective-permute-start | bytes 3932168 | tf_op jit(solution)/shard_map/ppermute | solution.py:206
  5.0 4.7 %collective-permute-start = (f32[8,256]{1,0:T(8,128)}, f32[8,256]{1,0:T(8,128)S(1)}, u32[]{:S(2)}, u32[]{:S(2)}) collective-permute-start(f32[8,256]{1,0:T(8,128)} %row_squares.1.own_sq), channel_id=1, source_target_pairs={{0,2},{2,0},{1,3},{3,1},{4,6},{6,4},{5,7},{7,5},{8,10},{10,8},{9,1... | collective-permute-start | bytes 24584 | tf_op jit(solution)/shard_map/ppermute | solution.py:209
  9.7 0.6 copy-start.11
  10.3 1.1 copy-start.2
  14.5 39.0 %collective-permute-start.2 = (bf16[272,256]{1,0:T(8,128)(2,1)}, bf16[272,256]{1,0:T(8,128)(2,1)S(1)}, u32[]{:S(2)}, u32[]{:S(2)}) collective-permute-start(bf16[272,256]{1,0:T(8,128)(2,1)} %attend.6.own), channel_id=1, source_target_pairs={{0,4},{12,8},{1,5},{13,9},{2,6},{14,10},{3,7},{15,11},{16,20},{28,... | collective-permute-start | bytes 417800 | tf_op jit(solution)/shard_map/ppermute | solution.py:226
  21.7 18.4 %collective-permute-start.17 = (bf16[272,256]{1,0:T(8,128)(2,1)}, bf16[272,256]{1,0:T(8,128)(2,1)S(1)}, u32[]{:S(2)}, u32[]{:S(2)}) collective-permute-start(bf16[272,256]{1,0:T(8,128)(2,1)} %attend.11.own), channel_id=1, source_target_pairs={{0,4},{12,8},{1,5},{13,9},{2,6},{14,10},{3,7},{15,11},{16,20},{28,... | collective-permute-start | bytes 417800 | tf_op jit(solution)/shard_map/ppermute | solution.py:226
  27.4 31.6 %collective-permute-start.5 = (bf16[528,256]{1,0:T(8,128)(2,1)}, bf16[528,256]{1,0:T(8,128)(2,1)S(1)}, u32[]{:S(2)}, u32[]{:S(2)}) collective-permute-start(bf16[528,256]{1,0:T(8,128)(2,1)} %attend.7.own), channel_id=1, source_target_pairs={{0,4},{12,8},{1,5},{13,9},{2,6},{14,10},{3,7},{15,11},{16,20},{28,... | collective-permute-start | bytes 811016 | tf_op jit(solution)/shard_map/ppermute | solution.py:226
  33.1 14.5 %collective-permute-start.14 = (bf16[528,256]{1,0:T(8,128)(2,1)}, bf16[528,256]{1,0:T(8,128)(2,1)S(1)}, u32[]{:S(2)}, u32[]{:S(2)}) collective-permute-start(bf16[528,256]{1,0:T(8,128)(2,1)} %attend.10.own), channel_id=1, source_target_pairs={{0,4},{12,8},{1,5},{13,9},{2,6},{14,10},{3,7},{15,11},{16,20},{28,... | collective-permute-start | bytes 811016 | tf_op jit(solution)/shard_map/ppermute | solution.py:226
  38.8 23.4 %collective-permute-start.8 = (bf16[528,256]{1,0:T(8,128)(2,1)}, bf16[528,256]{1,0:T(8,128)(2,1)S(1)}, u32[]{:S(2)}, u32[]{:S(2)}) collective-permute-start(bf16[528,256]{1,0:T(8,128)(2,1)} %attend.8.own), channel_id=1, source_target_pairs={{0,4},{12,8},{1,5},{13,9},{2,6},{14,10},{3,7},{15,11},{16,20},{28,... | collective-permute-start | bytes 811016 | tf_op jit(solution)/shard_map/ppermute | solution.py:226
  40.1 0.7 copy-start.23
  42.5 14.1 %collective-permute-start.18 = (bf16[272,256]{1,0:T(8,128)(2,1)}, bf16[272,256]{1,0:T(8,128)(2,1)S(1)}, u32[]{:S(2)}, u32[]{:S(2)}) collective-permute-start(bf16[272,256]{1,0:T(8,128)(2,1)} %merge.22.own), channel_id=1, source_target_pairs={{4,8},{8,4},{5,9},{9,5},{6,10},{10,6},{7,11},{11,7},{20,24},{24,20... | collective-permute-start | bytes 417800 | tf_op jit(solution)/shard_map/ppermute | solution.py:229
  47.6 4.1 %copy-start.19 = (bf16[528,256]{1,0:T(8,128)(2,1)}, bf16[528,256]{1,0:T(8,128)(2,1)S(1)}, u32[]{:S(2)}) copy-start(bf16[528,256]{1,0:T(8,128)(2,1)S(1)} %collective-permute-done.14.got) | copy-start | bytes 811012
  47.6 17.4 %collective-permute-start.11 = (bf16[528,256]{1,0:T(8,128)(2,1)}, bf16[528,256]{1,0:T(8,128)(2,1)S(1)}, u32[]{:S(2)}, u32[]{:S(2)}) collective-permute-start(bf16[528,256]{1,0:T(8,128)(2,1)} %attend.9.own), channel_id=1, source_target_pairs={{0,4},{12,8},{1,5},{13,9},{2,6},{14,10},{3,7},{15,11},{16,20},{28,... | collective-permute-start | bytes 811016 | tf_op jit(solution)/shard_map/ppermute | solution.py:226
  53.5 1.3 %copy-start.21 = (bf16[272,256]{1,0:T(8,128)(2,1)}, bf16[272,256]{1,0:T(8,128)(2,1)S(1)}, u32[]{:S(2)}) copy-start(bf16[272,256]{1,0:T(8,128)(2,1)S(1)} %collective-permute-done.2.got) | copy-start | bytes 417796
  53.5 16.4 %collective-permute-start.15 = (bf16[528,256]{1,0:T(8,128)(2,1)}, bf16[528,256]{1,0:T(8,128)(2,1)S(1)}, u32[]{:S(2)}, u32[]{:S(2)}) collective-permute-start(bf16[528,256]{1,0:T(8,128)(2,1)} %merge.20.own), channel_id=1, source_target_pairs={{4,8},{8,4},{5,9},{9,5},{6,10},{10,6},{7,11},{11,7},{20,24},{24,20... | collective-permute-start | bytes 811016 | tf_op jit(solution)/shard_map/ppermute | solution.py:229
  56.6 0.7 copy-start.22
  56.6 11.0 %collective-permute-start.3 = (bf16[272,256]{1,0:T(8,128)(2,1)}, bf16[272,256]{1,0:T(8,128)(2,1)S(1)}, u32[]{:S(2)}, u32[]{:S(2)}) collective-permute-start(bf16[272,256]{1,0:T(8,128)(2,1)} %merge.12.own), channel_id=1, source_target_pairs={{4,8},{8,4},{5,9},{9,5},{6,10},{10,6},{7,11},{11,7},{20,24},{24,20... | collective-permute-start | bytes 417800 | tf_op jit(solution)/shard_map/ppermute | solution.py:229
  58.9 1.4 %copy-start.12 = (bf16[528,256]{1,0:T(8,128)(2,1)}, bf16[528,256]{1,0:T(8,128)(2,1)S(1)}, u32[]{:S(2)}) copy-start(bf16[528,256]{1,0:T(8,128)(2,1)S(1)} %collective-permute-done.5.got) | copy-start | bytes 811012
  58.9 14.1 %collective-permute-start.19 = (bf16[256,256]{1,0:T(8,128)(2,1)}, bf16[256,256]{1,0:T(8,128)(2,1)S(1)}, u32[]{:S(2)}, u32[]{:S(2)}) collective-permute-start(bf16[256,256]{1,0:T(8,128)(2,1)} %merge.23), channel_id=1, source_target_pairs={{4,0},{8,12},{5,1},{9,13},{6,2},{10,14},{7,3},{11,15},{20,16},{24,... | collective-permute-start | bytes 393224 | tf_op jit(solution)/shard_map/ppermute | solution.py:233
  62.2 12.1 %copy-start.8 = (bf16[256,256]{1,0:T(8,128)(2,1)S(1)}, bf16[256,256]{1,0:T(8,128)(2,1)}, u32[]{:S(2)}) copy-start(bf16[256,256]{1,0:T(8,128)(2,1)} %merge.23) | copy-start | bytes 393220
  62.2 0.8 copy-start.13
  62.2 13.6 %collective-permute-start.6 = (bf16[528,256]{1,0:T(8,128)(2,1)}, bf16[528,256]{1,0:T(8,128)(2,1)S(1)}, u32[]{:S(2)}, u32[]{:S(2)}) collective-permute-start(bf16[528,256]{1,0:T(8,128)(2,1)} %merge.14.own), channel_id=1, source_target_pairs={{4,8},{8,4},{5,9},{9,5},{6,10},{10,6},{7,11},{11,7},{20,24},{24,20... | collective-permute-start | bytes 811016 | tf_op jit(solution)/shard_map/ppermute | solution.py:229
  64.9 0.7 copy-start.15
  64.9 14.8 %collective-permute-start.9 = (bf16[528,256]{1,0:T(8,128)(2,1)}, bf16[528,256]{1,0:T(8,128)(2,1)S(1)}, u32[]{:S(2)}, u32[]{:S(2)}) collective-permute-start(bf16[528,256]{1,0:T(8,128)(2,1)} %merge.16.own), channel_id=1, source_target_pairs={{4,8},{8,4},{5,9},{9,5},{6,10},{10,6},{7,11},{11,7},{20,24},{24,20... | collective-permute-start | bytes 811016 | tf_op jit(solution)/shard_map/ppermute | solution.py:229
  67.5 0.7 copy-start.20
  67.5 16.1 %collective-permute-start.12 = (bf16[528,256]{1,0:T(8,128)(2,1)}, bf16[528,256]{1,0:T(8,128)(2,1)S(1)}, u32[]{:S(2)}, u32[]{:S(2)}) collective-permute-start(bf16[528,256]{1,0:T(8,128)(2,1)} %merge.18.own), channel_id=1, source_target_pairs={{4,8},{8,4},{5,9},{9,5},{6,10},{10,6},{7,11},{11,7},{20,24},{24,20... | collective-permute-start | bytes 811016 | tf_op jit(solution)/shard_map/ppermute | solution.py:229
  69.9 1.3 %copy-start.14 = (bf16[528,256]{1,0:T(8,128)(2,1)}, bf16[528,256]{1,0:T(8,128)(2,1)S(1)}, u32[]{:S(2)}) copy-start(bf16[528,256]{1,0:T(8,128)(2,1)S(1)} %collective-permute-done.15.got) | copy-start | bytes 811012
  69.9 42.4 %collective-permute-start.4 = (bf16[256,256]{1,0:T(8,128)(2,1)}, bf16[256,256]{1,0:T(8,128)(2,1)S(1)}, u32[]{:S(2)}, u32[]{:S(2)}) collective-permute-start(bf16[256,256]{1,0:T(8,128)(2,1)} %merge.13), channel_id=1, source_target_pairs={{4,0},{8,12},{5,1},{9,13},{6,2},{10,14},{7,3},{11,15},{20,16},{24,... | collective-permute-start | bytes 393224 | tf_op jit(solution)/shard_map/ppermute | solution.py:233
  73.1 18.3 %collective-permute-start.16 = (bf16[512,256]{1,0:T(8,128)(2,1)}, bf16[512,256]{1,0:T(8,128)(2,1)S(1)}, u32[]{:S(2)}, u32[]{:S(2)}) collective-permute-start(bf16[512,256]{1,0:T(8,128)(2,1)} %merge.21), channel_id=1, source_target_pairs={{4,0},{8,12},{5,1},{9,13},{6,2},{10,14},{7,3},{11,15},{20,16},{24,... | collective-permute-start | bytes 786440 | tf_op jit(solution)/shard_map/ppermute | solution.py:233
  75.9 15.5 %copy-start.4 = (bf16[512,256]{1,0:T(8,128)(2,1)S(1)}, bf16[512,256]{1,0:T(8,128)(2,1)}, u32[]{:S(2)}) copy-start(bf16[512,256]{1,0:T(8,128)(2,1)} %merge.21) | copy-start | bytes 786436
  75.9 0.7 copy-start.16
  78.4 32.0 %collective-permute-start.7 = (bf16[512,256]{1,0:T(8,128)(2,1)}, bf16[512,256]{1,0:T(8,128)(2,1)S(1)}, u32[]{:S(2)}, u32[]{:S(2)}) collective-permute-start(bf16[512,256]{1,0:T(8,128)(2,1)} %merge.15), channel_id=1, source_target_pairs={{4,0},{8,12},{5,1},{9,13},{6,2},{10,14},{7,3},{11,15},{20,16},{24,... | collective-permute-start | bytes 786440 | tf_op jit(solution)/shard_map/ppermute | solution.py:233
  79.7 0.7 copy-start.17
  82.3 26.1 %collective-permute-start.10 = (bf16[512,256]{1,0:T(8,128)(2,1)}, bf16[512,256]{1,0:T(8,128)(2,1)S(1)}, u32[]{:S(2)}, u32[]{:S(2)}) collective-permute-start(bf16[512,256]{1,0:T(8,128)(2,1)} %merge.17), channel_id=1, source_target_pairs={{4,0},{8,12},{5,1},{9,13},{6,2},{10,14},{7,3},{11,15},{20,16},{24,... | collective-permute-start | bytes 786440 | tf_op jit(solution)/shard_map/ppermute | solution.py:233
  83.6 0.7 copy-start.18
  86.2 20.4 %copy-start.6 = (bf16[512,256]{1,0:T(8,128)(2,1)S(1)}, bf16[512,256]{1,0:T(8,128)(2,1)}, u32[]{:S(2)}) copy-start(bf16[512,256]{1,0:T(8,128)(2,1)} %merge.19) | copy-start | bytes 786436
  86.2 20.4 %collective-permute-start.13 = (bf16[512,256]{1,0:T(8,128)(2,1)}, bf16[512,256]{1,0:T(8,128)(2,1)S(1)}, u32[]{:S(2)}, u32[]{:S(2)}) collective-permute-start(bf16[512,256]{1,0:T(8,128)(2,1)} %merge.19), channel_id=1, source_target_pairs={{4,0},{8,12},{5,1},{9,13},{6,2},{10,14},{7,3},{11,15},{20,16},{24,... | collective-permute-start | bytes 786440 | tf_op jit(solution)/shard_map/ppermute | solution.py:233
  93.3 15.2 %copy-start.5 = (bf16[512,256]{1,0:T(8,128)(2,1)S(1)}, bf16[512,256]{1,0:T(8,128)(2,1)}, u32[]{:S(2)}) copy-start(bf16[512,256]{1,0:T(8,128)(2,1)} %merge.17) | copy-start | bytes 786436
  108.4 1.9 %copy-start.3 = (bf16[512,256]{1,0:T(8,128)(2,1)S(1)}, bf16[512,256]{1,0:T(8,128)(2,1)}, u32[]{:S(2)}) copy-start(bf16[512,256]{1,0:T(8,128)(2,1)} %merge.15) | copy-start | bytes 786436
  110.4 1.9 %copy-start.7 = (bf16[256,256]{1,0:T(8,128)(2,1)S(1)}, bf16[256,256]{1,0:T(8,128)(2,1)}, u32[]{:S(2)}) copy-start(bf16[256,256]{1,0:T(8,128)(2,1)} %merge.13) | copy-start | bytes 393220
  114.1 8.0 %collective-permute-start.20 = (bf16[256,640]{1,0:T(8,128)(2,1)S(1)}, bf16[256,640]{1,0:T(8,128)(2,1)S(1)}, u32[]{:S(2)}, u32[]{:S(2)}) collective-permute-start(bf16[256,640]{1,0:T(8,128)(2,1)S(1)} %select_convert_fusion), channel_id=1, source_target_pairs={{0,2},{2,0},{1,3},{3,1},{4,6},{6,4},{5,7},{7,5},{8,10},{10,8},{9,1... | collective-permute-start | bytes 983048 | tf_op jit(solution)/shard_map/ppermute | solution.py:252

commit v2 on v1

v2 whole, which is shorter than its diff:
```python
import functools

import jax
import jax.numpy as jnp
from jax import lax
from jax.experimental import pallas as pl
from jax.experimental.pallas import tpu as pltpu
from jax.sharding import PartitionSpec as P

HD = 128
EPSILON = 1e-06
LOG2E = 1.4426950408889634
OUT = -1e30
F32 = jnp.float32
BF16 = jnp.bfloat16
STATS = 16


def chunk_sizes(heads):
    count = -(-heads // 4)
    return [heads // count + (c < heads % count) for c in range(count)]


def in_order(value, *earlier):
    return lax.optimization_barrier((value, *earlier))[0]


def vmem():
    return pl.BlockSpec(memory_space=pltpu.VMEM)


def hbm():
    return pl.BlockSpec(memory_space=pltpu.HBM)


def in_hbm(*arrays):
    return [pltpu.with_memory_space_constraint(array, pltpu.HBM) for array in arrays]


def prepare_kernel(q_hbm, fk, nk, fv, nv, squares_ref, near_ref, q_ref, sems):
    rows = fk.shape[0]
    copies = [pltpu.make_async_copy(q_hbm, q_ref, sems.at[0])] + [
        pltpu.make_async_copy(src, near_ref.at[pl.ds(n * rows, rows), :], sems.at[n + 1])
        for n, src in enumerate((fk, nk, fv, nv))
    ]
    for copy in copies:
        copy.start()
    copies[0].wait()
    total = None
    for h in range(q_ref.shape[1] // HD):
        block = q_ref[:, h * HD : (h + 1) * HD].astype(F32)
        term = block * block
        total = term if total is None else total + term
    row = jnp.sum(total.T, axis=0, keepdims=True)
    squares_ref[...] = jnp.broadcast_to(row, squares_ref.shape)
    for copy in copies[1:]:
        copy.wait()


def prepare(queries, fk, nk, fv, nv):
    rows = queries.shape[0]
    return pl.pallas_call(
        prepare_kernel,
        out_shape=(
            jax.ShapeDtypeStruct((8, rows), F32),
            jax.ShapeDtypeStruct((4 * fk.shape[0], fk.shape[1]), BF16),
        ),
        in_specs=[hbm()] * 5,
        out_specs=(vmem(), vmem()),
        scratch_shapes=[pltpu.VMEM(queries.shape, BF16), pltpu.SemaphoreType.DMA((5,))],
        cost_estimate=pl.CostEstimate(
            flops=2 * queries.size, bytes_accessed=8 * queries.size, transcendentals=0
        ),
        compiler_params=pltpu.CompilerParams(vmem_limit_bytes=8 << 20),
        name="prepare",
    )(queries, fk, nk, fv, nv)


NT = (((1,), (1,)), ((), ()))
TN = (((0,), (0,)), ((), ()))


def attend_kernel(
    start, heads, width, owner_ref, gain_hbm, own_hbm, far_sq_hbm, q_hbm, kc_hbm, vc_hbm, near_hbm,
    far_hbm, out_ref, lse_s, s_a, s_b, p_a, p_b, gain_ref, own_sq, far_sq, q_ref, kc, vc, near,
    far, small_sems, sems,
):
    half = near.shape[0] // 2
    cached = kc.shape[0]
    scale = LOG2E / HD**0.5
    sources = (q_hbm, kc_hbm, near_hbm, far_hbm, vc_hbm)
    mine = slice(start * HD, (start + heads) * HD)
    small = [
        pltpu.make_async_copy(own_hbm, own_sq, small_sems.at[0]),
        pltpu.make_async_copy(far_sq_hbm, far_sq, small_sems.at[1]),
        pltpu.make_async_copy(gain_hbm.at[:, mine], gain_ref, small_sems.at[2]),
    ]
    for copy in small:
        copy.start()
    copies = []
    for h in range(heads):
        here, there = slice(h * HD, (h + 1) * HD), slice((start + h) * HD, (start + h + 1) * HD)
        copies.append(
            [
                pltpu.make_async_copy(src.at[:, there], dst.at[:, here], sems.at[h, n])
                for n, (src, dst) in enumerate(zip(sources, (q_ref, kc, near, far, vc)))
            ]
        )
        for copy in copies[h]:
            copy.start()
    for copy in small:
        copy.wait()
    total = own_sq[0:1, :] + far_sq[0:1, :]
    inverse = lax.rsqrt(total / width + EPSILON)
    inverse = jnp.broadcast_to(inverse, (HD, inverse.shape[1])).T
    penalty = jnp.where(owner_ref[0] == 1, F32(OUT), F32(0.0))
    s_refs, p_refs = (s_a, s_b), (p_a, p_b)
    spans = [(0, cached), (cached, half), (cached + half, half)]
    masses = {}

    def score(h):
        for copy in copies[h]:
            copy.wait()
        cols = slice(h * HD, (h + 1) * HD)
        normed = (q_ref[:, cols].astype(F32) * inverse * gain_ref[:, cols]).astype(BF16)
        for (at, size), k in zip(spans, (kc[:, cols], near[:half, cols], far[:half, cols])):
            s_refs[h % 2][at : at + size, :] = lax.dot_general(
                k, normed, NT, preferred_element_type=F32
            )

    def soften(h):
        s_ref, p_ref = s_refs[h % 2], p_refs[h % 2]
        top = jnp.max(s_ref[:cached, :], axis=0, keepdims=True) + penalty
        top = jnp.maximum(top, jnp.max(s_ref[cached:, :], axis=0, keepdims=True))
        base = top * scale
        old = jnp.exp2(s_ref[:cached, :] * scale - (base - penalty))
        p_ref[:cached, :] = old.astype(BF16)
        new = jnp.exp2(s_ref[cached:, :] * scale - base)
        p_ref[cached:, :] = new.astype(BF16)
        mass = jnp.sum(old, axis=0, keepdims=True) + jnp.sum(new, axis=0, keepdims=True)
        masses[h] = mass
        lse_s[h : h + 1, :] = base + jnp.log2(mass)

    def gather(h):
        cols = slice(h * HD, (h + 1) * HD)
        value = None
        for (at, size), v in zip(spans, (vc[:, cols], near[half:, cols], far[half:, cols])):
            part = lax.dot_general(
                v, p_refs[h % 2][at : at + size, :], TN, preferred_element_type=F32
            )
            value = part if value is None else value + part
        out_ref[h * HD : (h + 1) * HD, :] = (value * (1.0 / masses[h])).astype(BF16)

    for t in range(heads + 2):
        if 0 <= t - 2:
            gather(t - 2)
        if 0 <= t - 1 < heads:
            soften(t - 1)
        if t < heads:
            score(t)
    out_ref[heads * HD :, :] = split(lse_s[0:heads, :])


def split(lse):
    high = lse.astype(BF16).astype(F32)
    rest = lse - high
    mid = rest.astype(BF16).astype(F32)
    low = rest - mid
    pad = jnp.zeros((STATS - 3 * lse.shape[0], lse.shape[1]), F32)
    return jnp.concatenate([high, mid, low, pad], axis=0).astype(BF16)


def attend(start, heads, width, is_owner, queries, gain, own_sq, far_sq, kc, vc, near, far):
    rows = queries.shape[0]
    keys = kc.shape[0] + near.shape[0]
    wide = heads * HD
    return pl.pallas_call(
        functools.partial(attend_kernel, start, heads, width),
        out_shape=jax.ShapeDtypeStruct((wide + STATS, rows), BF16),
        in_specs=[pl.BlockSpec(memory_space=pltpu.SMEM)] + [hbm()] * 8,
        out_specs=vmem(),
        scratch_shapes=[pltpu.VMEM((8, rows), F32)]
        + [pltpu.VMEM((keys, rows), F32)] * 2
        + [pltpu.VMEM((keys, rows), BF16)] * 2
        + [pltpu.VMEM((1, wide), F32), pltpu.VMEM((8, rows), F32), pltpu.VMEM((8, rows), F32)]
        + [pltpu.VMEM((array.shape[0], wide), BF16) for array in (queries, kc, vc, near, far)]
        + [pltpu.SemaphoreType.DMA((3,))]
        + [pltpu.SemaphoreType.DMA((heads, 5))],
        cost_estimate=pl.CostEstimate(
            flops=16 * heads * rows * keys * HD,
            bytes_accessed=4 * heads * keys * HD,
            transcendentals=heads * rows * keys,
        ),
        compiler_params=pltpu.CompilerParams(vmem_limit_bytes=12 << 20),
        name="attend",
    )(is_owner, gain, own_sq, far_sq, queries, kc, vc, near, far)


def stats_of(ref, heads):
    stats = ref[heads * HD :, :].astype(F32)
    return stats[:heads] + stats[heads : 2 * heads] + stats[2 * heads : 3 * heads]


def merge_kernel(heads, guarded, *refs):
    own, got, out_ref = refs[-3:]
    own_lse, got_lse = stats_of(own, heads), stats_of(got, heads)
    if guarded:
        got_lse = jnp.where(refs[0][0] == 1, got_lse, F32(OUT))
    top = jnp.maximum(own_lse, got_lse)
    own_w, got_w = jnp.exp2(own_lse - top), jnp.exp2(got_lse - top)
    mass = own_w + got_w
    share = 1.0 / mass
    own_w, got_w = own_w * share, got_w * share
    for h in range(heads):
        at = slice(h * HD, (h + 1) * HD)
        mixed = own[at, :].astype(F32) * own_w[h : h + 1] + got[at, :].astype(F32) * got_w[h : h + 1]
        out_ref[at, :] = mixed.astype(BF16)
    out_ref[heads * HD :, :] = split(top + jnp.log2(mass))


def merge(heads, take, own, got):
    guard = [] if take is None else [take.astype(jnp.int32)[None]]
    return pl.pallas_call(
        functools.partial(merge_kernel, heads, bool(guard)),
        out_shape=jax.ShapeDtypeStruct(own.shape, BF16),
        in_specs=[pl.BlockSpec(memory_space=pltpu.SMEM)] * len(guard) + [vmem()] * 2,
        out_specs=vmem(),
        cost_estimate=pl.CostEstimate(
            flops=4 * own.size, bytes_accessed=6 * own.size, transcendentals=0
        ),
        compiler_params=pltpu.CompilerParams(vmem_limit_bytes=4 << 20),
        name="merge",
    )(*guard, own, got)


def local(
    n_slab, n_head, n_seq,
    queries, query_gain, cache_keys, cache_values, finished_keys, finished_values,
    new_keys, new_values, out_weight, time_weight, owner, step,
):
    queries, cache_keys, cache_values, finished_keys, finished_values, new_keys, new_values = in_hbm(
        queries, cache_keys, cache_values, finished_keys, finished_values, new_keys, new_values
    )
    heads = queries.shape[1] // HD
    width = queries.shape[1] * n_head
    slab = lax.axis_index("slab")

    own_sq, near = prepare(queries, finished_keys, new_keys, finished_values, new_values)
    if n_head == 2:
        far_sq = lax.ppermute(own_sq, "head", [(0, 1), (1, 0)])
    else:
        far_sq = lax.psum(own_sq, "head")
        own_sq = jnp.zeros_like(own_sq)
    far = lax.ppermute(near, "seq", [(0, 1), (1, 0)])
    is_owner = (slab == owner).astype(jnp.int32)
    gain = query_gain[None, :]
    gain, own_sq, far_sq, near, far = in_hbm(gain, own_sq, far_sq, near, far)

    sizes = chunk_sizes(heads)
    starts = [sum(sizes[:c]) for c in range(len(sizes))]
    count = len(sizes)
    side = n_slab // 2
    lag = 3
    outer = functools.reduce(jnp.logical_or, [(slab < side - 1), (slab > side)])
    inward = [
        [(j, j + 1), (n_slab - 1 - j, n_slab - 2 - j)] for j in range(side - 1)
    ]
    outward = [[(b, a) for a, b in pairs] for pairs in inward]
    own, got_in, folded, crossed, total, final = {}, {}, {}, {}, {}, {}
    last = []

    def run(value):
        last[:] = [value]
        return value

    def attention(c):
        own[c] = run(
            attend(
                starts[c], sizes[c], width, in_order(is_owner, *last), queries, gain, own_sq,
                far_sq, cache_keys, cache_values, near, far,
            )
        )

    def send_in(c):
        sent = own[c]
        for j in range(side - 2):
            got = lax.ppermute(sent, "slab", inward[j])
            take = (slab == j + 1) | (slab == n_slab - 2 - j)
            sent = merge(sizes[c], take, sent, got)
        own[c] = sent
        got_in[c] = lax.ppermute(sent, "slab", inward[side - 2]) if side > 1 else sent

    def fold(c):
        take = ((slab == side - 1) | (slab == side)) if side != 2 else None
        folded[c] = run(merge(sizes[c], take, own[c], in_order(got_in[c], *last)))
        crossed[c] = lax.ppermute(folded[c], "slab", [(side - 1, side), (side, side - 1)])

    def cross(c):
        total[c] = run(merge(sizes[c], None, folded[c], in_order(crossed[c], *last)))

    def send_out(c):
        attended = total[c][: sizes[c] * HD]
        for j in range(side - 2, -1, -1):
            got = lax.ppermute(attended, "slab", outward[j])
            attended = jnp.where((slab == j) | (slab == n_slab - 1 - j), got, attended)
        final[c] = attended

    for t in range(count):
        attention(t)
        back = t - lag
        if back >= 0:
            cross(back)
        if side == 2 and back >= 0 and sizes[t] == sizes[back]:
            sent = jnp.where(outer, own[t], total[back])
            got = lax.ppermute(sent, "slab", inward[0] + outward[0])
            got_in[t] = got
            final[back] = jnp.where(outer, got, sent)[: sizes[back] * HD]
        else:
            send_in(t)
            if back >= 0:
                send_out(back)
        if t >= 1:
            fold(t - 1)
    fold(count - 1)
    for c in range(max(0, count - lag), count):
        cross(c)
        send_out(c)
    attended = jnp.concatenate([final[c] for c in range(count)], axis=0)
    projected = lax.dot_general(attended, out_weight, TN, preferred_element_type=F32)

    half = time_weight.shape[0] // 2
    frequency = jnp.exp(-jnp.log(10000.0) * jnp.arange(half, dtype=F32) / half)
    phases = step[0].astype(F32) * frequency
    embedding = jnp.concatenate([jnp.cos(phases), jnp.sin(phases)])
    time_gate = 1.0 + jnp.dot(embedding, time_weight, precision=lax.Precision.HIGHEST)

    cols = time_weight.shape[1]
    if n_head == 2:
        me = lax.axis_index("head")
        left, right = projected[:, :cols], projected[:, cols:]
        kept = jnp.where(me == 0, left, right)
        sent = jnp.where(me == 0, right, left).astype(BF16)
        summed = kept + lax.ppermute(sent, "head", [(0, 1), (1, 0)]).astype(F32)
    else:
        summed = lax.psum_scatter(projected, "head", scatter_dimension=1, tiled=True)
    return (time_gate * summed).astype(BF16)


def solution(mesh):
    in_specs = (
        P(("grp", "seq"), "head"),
        P("head"),
        P(("grp", "slab"), "head"),
        P(("grp", "slab"), "head"),
        P(("grp", "slab", "seq"), "head"),
        P(("grp", "slab", "seq"), "head"),
        P(("grp", "slab", "seq"), "head"),
        P(("grp", "slab", "seq"), "head"),
        P("head", "slab"),
        P(None, ("slab", "head")),
        P("grp"),
        P("grp"),
    )
    out_specs = P(("grp", "seq"), ("slab", "head"))
    body = functools.partial(local, mesh.shape["slab"], mesh.shape["head"], mesh.shape["seq"])
    return jax.shard_map(body, mesh=mesh, in_specs=in_specs, out_specs=out_specs, check_vma=False)
```

time: 124 us -> 86.7 us (0.70)
  Pallas kernels: 47.9 us -> 22.4 us
  local copies, waits for them, and re-layouts: 7.27 us -> 1.26 us
  matrix products: 11.1 us -> 5.2 us
  waiting for transfers between devices: 23.6 us -> 27.4 us
  starting transfers between devices: 30.4 us -> 26.8 us
    pallas_call x19 -> x16, Pallas kernels: 47.9 us -> 22.4 us  [the longest x5 19.4 us: attend(): pl.pallas_call(functools.partial(attend_kernel, start, heads, width), out...]
    unnamed x53 -> x10, local copies, waits for them, and re-layouts: 6.64 us -> 0.6 us
    dot_general x6 -> x1, matrix products: 10.6 us -> 4.77 us  [local(): lax.dot_general(attended, out_weight, TN, preferred_element_type=F32)]
    ppermute x18 -> x13, waiting for transfers between devices: 17 us -> 21.9 us  [the longest x3 14.2 us: send_out(): got = lax.ppermute(attended, 'slab', outward[j])]
    ppermute x18 -> x13, starting transfers between devices: 25.4 us -> 22.1 us  [the longest x3 12.5 us: send_in(): lax.ppermute(sent, 'slab', inward[side - 2])]
  transfers between devices with their start and end apart: 21 -> 16, of which waited for: 4 -> 8; matrix products, arithmetic and copies ran while one was open for 8% -> 2% of each run, Pallas kernels for 36% -> 19%
where the time goes in v2:
time: 86.7 us; the launch traced here: 86.2 us
  waiting for transfers between devices  27.4 us (32%)
  starting transfers between devices  26.8 us (31%)
  Pallas kernels  22.4 us (26%)
  matrix products  5.2 us (6%)
  between operations  1.72 us (2%)
  other arithmetic  1.39 us (2%)
  local copies, waits for them, and re-layouts  1.26 us (1%)
    pallas_call x5, Pallas kernels, attend(): pl.pallas_call(functools.partial(attend_kernel, start, heads, width), out...  19.4 us
    ppermute x3, waiting for transfers between devices, send_out(): got = lax.ppermute(attended, 'slab', outward[j])  14.2 us
    ppermute x3, starting transfers between devices, send_in(): lax.ppermute(sent, 'slab', inward[side - 2])  12.5 us
    ppermute x2, waiting for transfers between devices, local(): got = lax.ppermute(sent, 'slab', inward[0] + outward[0])  7.09 us
    ppermute x1, waiting for transfers between devices, local(): summed = kept + lax.ppermute(sent, 'head', [(0, 1), (1, 0)]).astype(F32)  5.13 us
    dot_general x1, matrix products, local(): lax.dot_general(attended, out_weight, TN, preferred_element_type=F32)  4.77 us
    ppermute x3, starting transfers between devices, send_out(): got = lax.ppermute(attended, 'slab', outward[j])  4.06 us
    ppermute x5, starting transfers between devices, fold(): lax.ppermute(folded[c], 'slab', [(side - 1, side), (side, side - 1)])  3.38 us
  transfers between devices with their start and end apart: 16, of which 8 were waited for; matrix products, arithmetic and copies ran while one was open for 2% of the time, Pallas kernels for 19%

profile of v2, /device:TPU:0, one launch (start us, length us, event | category | flops | bytes accessed | tf_op | source)
XLA Modules:
  0.0 86.2 jit_solution(3360431872864385143)
XLA Ops:
  0.0 0.0 copy-start
  0.0 1.8 %prepare.1 = (f32[8,256]{1,0:T(8,128)S(1)}, bf16[256,2560]{1,0:T(8,128)(2,1)S(1)}) custom-call(bf16[256,2560]{1,0:T(8,128)(2,1)} %q_hbm.11, bf16[64,2560]{1,0:T(8,128)(2,1)} %fk.1, bf16[64,2560]{1,0:T(8,128)(2,1)} %nk.1, bf16[64,2560]{1,0:T(8,128)(2,1)} %fv.1, bf16[64,2560]{1,0:T(8,128)(2,1)} %nv.1), custom_call_target="tpu_custom_call" | custom-call | flops 1310720 | bytes 5242880 | tf_op jit(solution)/shard_map/prepare/pallas_call | solution.py:62
  1.8 0.0 copy-start.1
  1.8 0.0 copy-start.2
  1.8 0.6 collective-permute-start.1
  2.4 2.6 %collective-permute-start = (f32[8,256]{1,0:T(8,128)S(1)}, f32[8,256]{1,0:T(8,128)S(1)}, u32[]{:S(2)}, u32[]{:S(2)}) collective-permute-start(f32[8,256]{1,0:T(8,128)S(1)} %get-tuple-element.21.own_hbm), channel_id=1, source_target_pairs={{0,2},{2,0},{1,3},{3,1},{4,6},{6,4},{5,7},{7,5},{8,10},{10,8},{9,1... | collective-permute-start | bytes 24584 | tf_op jit(solution)/shard_map/ppermute | solution.py:250
  5.6 0.6 broadcast_in_dim.4.gain_hbm
  6.2 0.4 collective-permute-done.far_sq_hbm
  6.6 0.0 collective-permute-done.1.far_hbm
  6.6 0.0 copy-done.1
  6.6 0.0 copy-done.2
  6.6 0.6 copy-done.3
  7.2 3.9 %attend.5.refs_0_ = bf16[528,256]{1,0:T(8,128)(2,1)S(1)} custom-call(s32[1]{0:T(128)S(6)} %convert_element_type.20.owner_ref, f32[1,2560]{1,0:T(1,128)} %broadcast_in_dim.4.gain_hbm, f32[8,256]{1,0:T(8,128)} %copy-done.2, f32[8,256]{1,0:T(8,128)} %copy-done.3, bf16[256,2560]{1,0:T(8,128)(2,1)} %q_hbm.11, bf16[512,2560]{1,0:T(8,128)(2,1)} %kc_hbm.9, ...), custom_call_target="tpu_custom_call" | custom-call | flops 1610612736 | bytes 1572864 | tf_op jit(solution)/shard_map/attend/pallas_call | solution.py:177
  11.0 4.0 %collective-permute-start.3 = (bf16[528,256]{1,0:T(8,128)(2,1)S(1)}, bf16[528,256]{1,0:T(8,128)(2,1)S(1)}, u32[]{:S(2)}, u32[]{:S(2)}) collective-permute-start(bf16[528,256]{1,0:T(8,128)(2,1)S(1)} %attend.5.refs_0_), channel_id=1, source_target_pairs={{0,4},{12,8},{1,5},{13,9},{2,6},{14,10},{3,7},{15,11},{16,20},{28,... | collective-permute-start | bytes 811016 | tf_op jit(solution)/shard_map/ppermute | solution.py:291
  15.1 3.9 %attend.6.refs_0_ = bf16[528,256]{1,0:T(8,128)(2,1)S(1)} custom-call(s32[1]{0:T(128)S(6)} %convert_element_type.20.owner_ref, f32[1,2560]{1,0:T(1,128)} %broadcast_in_dim.4.gain_hbm, f32[8,256]{1,0:T(8,128)} %copy-done.2, f32[8,256]{1,0:T(8,128)} %copy-done.3, bf16[256,2560]{1,0:T(8,128)(2,1)} %q_hbm.11, bf16[512,2560]{1,0:T(8,128)(2,1)} %kc_hbm.9, ...), custom_call_target="tpu_custom_call" | custom-call | flops 1610612736 | bytes 1572864 | tf_op jit(solution)/shard_map/attend/pallas_call | solution.py:177
  19.0 1.3 %collective-permute-start.2 = (bf16[528,256]{1,0:T(8,128)(2,1)S(1)}, bf16[528,256]{1,0:T(8,128)(2,1)S(1)}, u32[]{:S(2)}, u32[]{:S(2)}) collective-permute-start(bf16[528,256]{1,0:T(8,128)(2,1)S(1)} %attend.6.refs_0_), channel_id=1, source_target_pairs={{0,4},{12,8},{1,5},{13,9},{2,6},{14,10},{3,7},{15,11},{16,20},{28,... | collective-permute-start | bytes 811016 | tf_op jit(solution)/shard_map/ppermute | solution.py:291
  20.3 0.6 collective-permute-done.3.refs_1_
  20.8 0.1 merge.10.refs_0_
  21.0 0.7 collective-permute-start.4
  21.6 3.9 %attend.7.refs_0_ = bf16[528,256]{1,0:T(8,128)(2,1)S(1)} custom-call(s32[1]{0:T(128)S(6)} %convert_element_type.20.owner_ref, f32[1,2560]{1,0:T(1,128)} %broadcast_in_dim.4.gain_hbm, f32[8,256]{1,0:T(8,128)} %copy-done.2, f32[8,256]{1,0:T(8,128)} %copy-done.3, bf16[256,2560]{1,0:T(8,128)(2,1)} %q_hbm.11, bf16[512,2560]{1,0:T(8,128)(2,1)} %kc_hbm.9, ...), custom_call_target="tpu_custom_call" | custom-call | flops 1610612736 | bytes 1572864 | tf_op jit(solution)/shard_map/attend/pallas_call | solution.py:177
  25.5 7.2 %collective-permute-start.6 = (bf16[528,256]{1,0:T(8,128)(2,1)S(1)}, bf16[528,256]{1,0:T(8,128)(2,1)S(1)}, u32[]{:S(2)}, u32[]{:S(2)}) collective-permute-start(bf16[528,256]{1,0:T(8,128)(2,1)S(1)} %attend.7.refs_0_), channel_id=1, source_target_pairs={{0,4},{12,8},{1,5},{13,9},{2,6},{14,10},{3,7},{15,11},{16,20},{28,... | collective-permute-start | bytes 811016 | tf_op jit(solution)/shard_map/ppermute | solution.py:291
  32.7 0.0 collective-permute-done.2.refs_1_
  32.7 0.1 merge.11.refs_0_
  32.9 0.7 collective-permute-start.7
  33.6 3.9 %attend.8.refs_0_ = bf16[528,256]{1,0:T(8,128)(2,1)S(1)} custom-call(s32[1]{0:T(128)S(6)} %convert_element_type.20.owner_ref, f32[1,2560]{1,0:T(1,128)} %broadcast_in_dim.4.gain_hbm, f32[8,256]{1,0:T(8,128)} %copy-done.2, f32[8,256]{1,0:T(8,128)} %copy-done.3, bf16[256,2560]{1,0:T(8,128)(2,1)} %q_hbm.11, bf16[512,2560]{1,0:T(8,128)(2,1)} %kc_hbm.9, ...), custom_call_target="tpu_custom_call" | custom-call | flops 1610612736 | bytes 1572864 | tf_op jit(solution)/shard_map/attend/pallas_call | solution.py:177
  37.5 0.0 collective-permute-done.4.refs_1_
  37.5 0.1 merge.12
  37.6 0.0 collective-permute-done.6.refs_1_
  37.6 0.1 merge.13.refs_0_
  37.7 3.9 %attend.9.refs_0_ = bf16[528,256]{1,0:T(8,128)(2,1)S(1)} custom-call(s32[1]{0:T(128)S(6)} %convert_element_type.20.owner_ref, f32[1,2560]{1,0:T(1,128)} %broadcast_in_dim.4.gain_hbm, f32[8,256]{1,0:T(8,128)} %copy-done.2, f32[8,256]{1,0:T(8,128)} %copy-done.3, bf16[256,2560]{1,0:T(8,128)(2,1)} %q_hbm.11, bf16[512,2560]{1,0:T(8,128)(2,1)} %kc_hbm.9, ...), custom_call_target="tpu_custom_call" | custom-call | flops 1610612736 | bytes 1572864 | tf_op jit(solution)/shard_map/attend/pallas_call | solution.py:177
  41.6 0.0 collective-permute-done.7.refs_1_
  41.6 0.1 merge.14
  41.8 1.6 %collective-permute-start.5 = (bf16[528,256]{1,0:T(8,128)(2,1)S(1)}, bf16[528,256]{1,0:T(8,128)(2,1)S(1)}, u32[]{:S(2)}, u32[]{:S(2)}) collective-permute-start(bf16[528,256]{1,0:T(8,128)(2,1)S(1)} %broadcast_select_fusion.1), channel_id=1, source_target_pairs={{0,4},{12,8},{4,0},{8,12},{1,5},{13,9},{5,1},{9,13},{2,6},{14,10},... | collective-permute-start | bytes 811016 | tf_op jit(solution)/shard_map/ppermute | solution.py:315
  43.5 0.5 collective-permute-start.8
  44.0 0.7 collective-permute-start.9
  45.4 5.0 %collective-permute-done.5.refs_1_ = bf16[528,256]{1,0:T(8,128)(2,1)S(1)} collective-permute-done((bf16[528,256]{1,0:T(8,128)(2,1)S(1)}, bf16[528,256]{1,0:T(8,128)(2,1)S(1)}, u32[]{:S(2)}, u32[]{:S(2)}) %collective-permute-start.5) | collective-permute-done | bytes 270368 | tf_op jit(solution)/shard_map/ppermute | solution.py:315
  50.4 0.1 merge.15.refs_0_
  50.6 0.7 collective-permute-start.11
  51.3 2.0 %collective-permute-done.8.refs_1_ = bf16[528,256]{1,0:T(8,128)(2,1)S(1)} collective-permute-done((bf16[528,256]{1,0:T(8,128)(2,1)S(1)}, bf16[528,256]{1,0:T(8,128)(2,1)S(1)}, u32[]{:S(2)}, u32[]{:S(2)}) %collective-permute-start.8) | collective-permute-done | bytes 270368 | tf_op jit(solution)/shard_map/ppermute | solution.py:315
  53.3 0.1 merge.16.refs_0_
  53.5 0.7 collective-permute-start.13
  54.2 0.0 collective-permute-done.9.refs_1_
  54.2 0.1 merge.17
  54.3 1.5 %collective-permute-start.10 = (bf16[512,256]{1,0:T(8,128)(2,1)S(1)}, bf16[512,256]{1,0:T(8,128)(2,1)S(1)}, u32[]{:S(2)}, u32[]{:S(2)}) collective-permute-start(bf16[512,256]{1,0:T(8,128)(2,1)S(1)} %slice.32), channel_id=1, source_target_pairs={{4,0},{8,12},{5,1},{9,13},{6,2},{10,14},{7,3},{11,15},{20,16},{24,... | collective-permute-start | bytes 786440 | tf_op jit(solution)/shard_map/ppermute | solution.py:304
  55.8 0.1 fusion.1
  55.9 0.0 collective-permute-done.11.refs_1_
  55.9 0.1 merge.18
  56.1 1.3 %collective-permute-start.12 = (bf16[512,256]{1,0:T(8,128)(2,1)S(1)}, bf16[512,256]{1,0:T(8,128)(2,1)S(1)}, u32[]{:S(2)}, u32[]{:S(2)}) collective-permute-start(bf16[512,256]{1,0:T(8,128)(2,1)S(1)} %slice.33), channel_id=1, source_target_pairs={{4,0},{8,12},{5,1},{9,13},{6,2},{10,14},{7,3},{11,15},{20,16},{24,... | collective-permute-start | bytes 786440 | tf_op jit(solution)/shard_map/ppermute | solution.py:304
  57.4 0.1 fusion
  57.4 0.0 collective-permute-done.13.refs_1_
  57.4 0.1 merge.19
  57.6 1.3 %collective-permute-start.14 = (bf16[512,256]{1,0:T(8,128)(2,1)S(1)}, bf16[512,256]{1,0:T(8,128)(2,1)S(1)}, u32[]{:S(2)}, u32[]{:S(2)}) collective-permute-start(bf16[512,256]{1,0:T(8,128)(2,1)S(1)} %slice.34), channel_id=1, source_target_pairs={{4,0},{8,12},{5,1},{9,13},{6,2},{10,14},{7,3},{11,15},{20,16},{24,... | collective-permute-start | bytes 786440 | tf_op jit(solution)/shard_map/ppermute | solution.py:304
  58.9 7.5 %collective-permute-done.10 = bf16[512,256]{1,0:T(8,128)(2,1)S(1)} collective-permute-done((bf16[512,256]{1,0:T(8,128)(2,1)S(1)}, bf16[512,256]{1,0:T(8,128)(2,1)S(1)}, u32[]{:S(2)}, u32[]{:S(2)}) %collective-permute-start.10) | collective-permute-done | bytes 262176 | tf_op jit(solution)/shard_map/ppermute | solution.py:304
  66.5 0.1 select_dynamic-update-slice_fusion.2
  66.5 4.0 %collective-permute-done.12 = bf16[512,256]{1,0:T(8,128)(2,1)S(1)} collective-permute-done((bf16[512,256]{1,0:T(8,128)(2,1)S(1)}, bf16[512,256]{1,0:T(8,128)(2,1)S(1)}, u32[]{:S(2)}, u32[]{:S(2)}) %collective-permute-start.12) | collective-permute-done | bytes 262176 | tf_op jit(solution)/shard_map/ppermute | solution.py:304
  70.5 0.1 select_dynamic-update-slice_fusion.1
  70.6 2.7 %collective-permute-done.14 = bf16[512,256]{1,0:T(8,128)(2,1)S(1)} collective-permute-done((bf16[512,256]{1,0:T(8,128)(2,1)S(1)}, bf16[512,256]{1,0:T(8,128)(2,1)S(1)}, u32[]{:S(2)}, u32[]{:S(2)}) %collective-permute-start.14) | collective-permute-done | bytes 262176 | tf_op jit(solution)/shard_map/ppermute | solution.py:304
  73.3 0.1 select_dynamic-update-slice_fusion
  73.4 4.8 %fusion.4 = f32[256,1280]{1,0:T(8,128)S(1)} fusion(bf16[2560,256]{1,0:T(8,128)(2,1)S(1)} %select_dynamic-update-slice_fusion, bf16[2560,1280]{1,0:T(8,128)(2,1)} %param.20), kind=kOutput, calls=%fused_computation.17 | convolution fusion | flops 1677721600 | bytes 9175040 | tf_op jit(solution)/shard_map/dot_general | solution.py:329
  78.1 0.1 select_convert_fusion
  78.2 1.6 %collective-permute-start.15 = (bf16[256,640]{1,0:T(8,128)(2,1)S(1)}, bf16[256,640]{1,0:T(8,128)(2,1)S(1)}, u32[]{:S(2)}, u32[]{:S(2)}) collective-permute-start(bf16[256,640]{1,0:T(8,128)(2,1)S(1)} %select_convert_fusion), channel_id=1, source_target_pairs={{0,2},{2,0},{1,3},{3,1},{4,6},{6,4},{5,7},{7,5},{8,10},{10,8},{9,1... | collective-permute-start | bytes 983048 | tf_op jit(solution)/shard_map/ppermute | solution.py:343
  79.8 0.4 convolution_reduce_fusion
  80.2 5.1 %collective-permute-done.15 = bf16[256,640]{1,0:T(8,128)(2,1)S(1)} collective-permute-done((bf16[256,640]{1,0:T(8,128)(2,1)S(1)}, bf16[256,640]{1,0:T(8,128)(2,1)S(1)}, u32[]{:S(2)}, u32[]{:S(2)}) %collective-permute-start.15) | collective-permute-done | bytes 327712 | tf_op jit(solution)/shard_map/ppermute | solution.py:343
  85.4 0.8 multiply_convert_fusion
  (12 shorter events, 0.2 us)
Async XLA Ops:
  0.0 79.8 %copy-start = (f32[256,640]{1,0:T(8,128)S(1)}, f32[256,640]{1,0:T(8,128)}, u32[]{:S(2)}) copy-start(f32[256,640]{1,0:T(8,128)} %param.21) | copy-start | bytes 1966084
  0.0 5.6 %copy-start.4 = (f32[2560]{0:T(1024)S(1)}, f32[2560]{0:T(1024)}, u32[]{:S(2)}) copy-start(f32[2560]{0:T(1024)} %param.13) | copy-start | bytes 30724
  1.8 4.8 %copy-start.1 = (bf16[256,2560]{1,0:T(8,128)(2,1)}, bf16[256,2560]{1,0:T(8,128)(2,1)S(1)}, u32[]{:S(2)}) copy-start(bf16[256,2560]{1,0:T(8,128)(2,1)S(1)} %get-tuple-element.22.near_hbm) | copy-start | bytes 3932164
  1.8 4.8 %copy-start.2 = (f32[8,256]{1,0:T(8,128)}, f32[8,256]{1,0:T(8,128)S(1)}, u32[]{:S(2)}) copy-start(f32[8,256]{1,0:T(8,128)S(1)} %get-tuple-element.21.own_hbm) | copy-start | bytes 24580
  1.8 4.7 %collective-permute-start.1 = (bf16[256,2560]{1,0:T(8,128)(2,1)S(1)}, bf16[256,2560]{1,0:T(8,128)(2,1)}, u32[]{:S(2)}, u32[]{:S(2)}) collective-permute-start(bf16[256,2560]{1,0:T(8,128)(2,1)S(1)} %get-tuple-element.22.near_hbm), channel_id=1, source_target_pairs={{0,1},{1,0},{2,3},{3,2},{4,5},{5,4},{6,7},{7,6},{8,9},{9,8},{10,11... | collective-permute-start | bytes 3932168 | tf_op jit(solution)/shard_map/ppermute | solution.py:254
  2.4 4.2 %collective-permute-start = (f32[8,256]{1,0:T(8,128)S(1)}, f32[8,256]{1,0:T(8,128)S(1)}, u32[]{:S(2)}, u32[]{:S(2)}) collective-permute-start(f32[8,256]{1,0:T(8,128)S(1)} %get-tuple-element.21.own_hbm), channel_id=1, source_target_pairs={{0,2},{2,0},{1,3},{3,1},{4,6},{6,4},{5,7},{7,5},{8,10},{10,8},{9,1... | collective-permute-start | bytes 24584 | tf_op jit(solution)/shard_map/ppermute | solution.py:250
  6.6 0.6 copy-start.3
  11.0 9.8 %collective-permute-start.3 = (bf16[528,256]{1,0:T(8,128)(2,1)S(1)}, bf16[528,256]{1,0:T(8,128)(2,1)S(1)}, u32[]{:S(2)}, u32[]{:S(2)}) collective-permute-start(bf16[528,256]{1,0:T(8,128)(2,1)S(1)} %attend.5.refs_0_), channel_id=1, source_target_pairs={{0,4},{12,8},{1,5},{13,9},{2,6},{14,10},{3,7},{15,11},{16,20},{28,... | collective-permute-start | bytes 811016 | tf_op jit(solution)/shard_map/ppermute | solution.py:291
  19.0 13.8 %collective-permute-start.2 = (bf16[528,256]{1,0:T(8,128)(2,1)S(1)}, bf16[528,256]{1,0:T(8,128)(2,1)S(1)}, u32[]{:S(2)}, u32[]{:S(2)}) collective-permute-start(bf16[528,256]{1,0:T(8,128)(2,1)S(1)} %attend.6.refs_0_), channel_id=1, source_target_pairs={{0,4},{12,8},{1,5},{13,9},{2,6},{14,10},{3,7},{15,11},{16,20},{28,... | collective-permute-start | bytes 811016 | tf_op jit(solution)/shard_map/ppermute | solution.py:291
  21.0 16.5 %collective-permute-start.4 = (bf16[528,256]{1,0:T(8,128)(2,1)S(1)}, bf16[528,256]{1,0:T(8,128)(2,1)S(1)}, u32[]{:S(2)}, u32[]{:S(2)}) collective-permute-start(bf16[528,256]{1,0:T(8,128)(2,1)S(1)} %merge.10.refs_0_), channel_id=1, source_target_pairs={{4,8},{8,4},{5,9},{9,5},{6,10},{10,6},{7,11},{11,7},{20,24},{24,20... | collective-permute-start | bytes 811016 | tf_op jit(solution)/shard_map/ppermute | solution.py:296
  25.5 12.1 %collective-permute-start.6 = (bf16[528,256]{1,0:T(8,128)(2,1)S(1)}, bf16[528,256]{1,0:T(8,128)(2,1)S(1)}, u32[]{:S(2)}, u32[]{:S(2)}) collective-permute-start(bf16[528,256]{1,0:T(8,128)(2,1)S(1)} %attend.7.refs_0_), channel_id=1, source_target_pairs={{0,4},{12,8},{1,5},{13,9},{2,6},{14,10},{3,7},{15,11},{16,20},{28,... | collective-permute-start | bytes 811016 | tf_op jit(solution)/shard_map/ppermute | solution.py:291
  32.9 8.7 %collective-permute-start.7 = (bf16[528,256]{1,0:T(8,128)(2,1)S(1)}, bf16[528,256]{1,0:T(8,128)(2,1)S(1)}, u32[]{:S(2)}, u32[]{:S(2)}) collective-permute-start(bf16[528,256]{1,0:T(8,128)(2,1)S(1)} %merge.11.refs_0_), channel_id=1, source_target_pairs={{4,8},{8,4},{5,9},{9,5},{6,10},{10,6},{7,11},{11,7},{20,24},{24,20... | collective-permute-start | bytes 811016 | tf_op jit(solution)/shard_map/ppermute | solution.py:296
  41.8 8.6 %collective-permute-start.5 = (bf16[528,256]{1,0:T(8,128)(2,1)S(1)}, bf16[528,256]{1,0:T(8,128)(2,1)S(1)}, u32[]{:S(2)}, u32[]{:S(2)}) collective-permute-start(bf16[528,256]{1,0:T(8,128)(2,1)S(1)} %broadcast_select_fusion.1), channel_id=1, source_target_pairs={{0,4},{12,8},{4,0},{8,12},{1,5},{13,9},{5,1},{9,13},{2,6},{14,10},... | collective-permute-start | bytes 811016 | tf_op jit(solution)/shard_map/ppermute | solution.py:315
  43.5 9.9 %collective-permute-start.8 = (bf16[528,256]{1,0:T(8,128)(2,1)S(1)}, bf16[528,256]{1,0:T(8,128)(2,1)S(1)}, u32[]{:S(2)}, u32[]{:S(2)}) collective-permute-start(bf16[528,256]{1,0:T(8,128)(2,1)S(1)} %broadcast_select_fusion), channel_id=1, source_target_pairs={{0,4},{12,8},{4,0},{8,12},{1,5},{13,9},{5,1},{9,13},{2,6},{14,10},... | collective-permute-start | bytes 811016 | tf_op jit(solution)/shard_map/ppermute | solution.py:315
  44.0 10.1 %collective-permute-start.9 = (bf16[528,256]{1,0:T(8,128)(2,1)S(1)}, bf16[528,256]{1,0:T(8,128)(2,1)S(1)}, u32[]{:S(2)}, u32[]{:S(2)}) collective-permute-start(bf16[528,256]{1,0:T(8,128)(2,1)S(1)} %merge.13.refs_0_), channel_id=1, source_target_pairs={{4,8},{8,4},{5,9},{9,5},{6,10},{10,6},{7,11},{11,7},{20,24},{24,20... | collective-permute-start | bytes 811016 | tf_op jit(solution)/shard_map/ppermute | solution.py:296
  50.6 5.3 %collective-permute-start.11 = (bf16[528,256]{1,0:T(8,128)(2,1)S(1)}, bf16[528,256]{1,0:T(8,128)(2,1)S(1)}, u32[]{:S(2)}, u32[]{:S(2)}) collective-permute-start(bf16[528,256]{1,0:T(8,128)(2,1)S(1)} %merge.15.refs_0_), channel_id=1, source_target_pairs={{4,8},{8,4},{5,9},{9,5},{6,10},{10,6},{7,11},{11,7},{20,24},{24,20... | collective-permute-start | bytes 811016 | tf_op jit(solution)/shard_map/ppermute | solution.py:296
  53.5 4.0 %collective-permute-start.13 = (bf16[528,256]{1,0:T(8,128)(2,1)S(1)}, bf16[528,256]{1,0:T(8,128)(2,1)S(1)}, u32[]{:S(2)}, u32[]{:S(2)}) collective-permute-start(bf16[528,256]{1,0:T(8,128)(2,1)S(1)} %merge.16.refs_0_), channel_id=1, source_target_pairs={{4,8},{8,4},{5,9},{9,5},{6,10},{10,6},{7,11},{11,7},{20,24},{24,20... | collective-permute-start | bytes 811016 | tf_op jit(solution)/shard_map/ppermute | solution.py:296
  54.3 12.1 %collective-permute-start.10 = (bf16[512,256]{1,0:T(8,128)(2,1)S(1)}, bf16[512,256]{1,0:T(8,128)(2,1)S(1)}, u32[]{:S(2)}, u32[]{:S(2)}) collective-permute-start(bf16[512,256]{1,0:T(8,128)(2,1)S(1)} %slice.32), channel_id=1, source_target_pairs={{4,0},{8,12},{5,1},{9,13},{6,2},{10,14},{7,3},{11,15},{20,16},{24,... | collective-permute-start | bytes 786440 | tf_op jit(solution)/shard_map/ppermute | solution.py:304
  56.1 14.4 %collective-permute-start.12 = (bf16[512,256]{1,0:T(8,128)(2,1)S(1)}, bf16[512,256]{1,0:T(8,128)(2,1)S(1)}, u32[]{:S(2)}, u32[]{:S(2)}) collective-permute-start(bf16[512,256]{1,0:T(8,128)(2,1)S(1)} %slice.33), channel_id=1, source_target_pairs={{4,0},{8,12},{5,1},{9,13},{6,2},{10,14},{7,3},{11,15},{20,16},{24,... | collective-permute-start | bytes 786440 | tf_op jit(solution)/shard_map/ppermute | solution.py:304
  57.6 15.7 %collective-permute-start.14 = (bf16[512,256]{1,0:T(8,128)(2,1)S(1)}, bf16[512,256]{1,0:T(8,128)(2,1)S(1)}, u32[]{:S(2)}, u32[]{:S(2)}) collective-permute-start(bf16[512,256]{1,0:T(8,128)(2,1)S(1)} %slice.34), channel_id=1, source_target_pairs={{4,0},{8,12},{5,1},{9,13},{6,2},{10,14},{7,3},{11,15},{20,16},{24,... | collective-permute-start | bytes 786440 | tf_op jit(solution)/shard_map/ppermute | solution.py:304
  78.2 7.1 %collective-permute-start.15 = (bf16[256,640]{1,0:T(8,128)(2,1)S(1)}, bf16[256,640]{1,0:T(8,128)(2,1)S(1)}, u32[]{:S(2)}, u32[]{:S(2)}) collective-permute-start(bf16[256,640]{1,0:T(8,128)(2,1)S(1)} %select_convert_fusion), channel_id=1, source_target_pairs={{0,2},{2,0},{1,3},{3,1},{4,6},{6,4},{5,7},{7,5},{8,10},{10,8},{9,1... | collective-permute-start | bytes 983048 | tf_op jit(solution)/shard_map/ppermute | solution.py:343

commit v3 on v2

--- a/solution.py
+++ b/solution.py
@@ -6,6 +6,7 @@
 from jax.experimental import pallas as pl
 from jax.experimental.pallas import tpu as pltpu
 from jax.sharding import PartitionSpec as P
+
 
 HD = 128
 EPSILON = 1e-06
@@ -17,8 +18,20 @@
 
 
 def chunk_sizes(heads):
-    count = -(-heads // 4)
+    count = -(-heads // 5) if heads > 5 else 2
     return [heads // count + (c < heads % count) for c in range(count)]
+
+
+def order_of(count):
+    if count < 3:
+        steps = [(kind, c) for c in range(count) for kind in "AI"]
+        steps += [("F", c) for c in range(count)]
+        return steps + [(kind, c) for c in range(count) for kind in "CO"]
+    steps = [(kind, c) for c in range(count - 1) for kind in "AI"]
+    steps += [("F", 0), ("A", count - 1), ("F", 1), ("C", 0), ("X", 0)]
+    for c in range(2, count):
+        steps += [("F", c), ("C", c - 1), ("O", c - 1)]
+    return steps + [("C", count - 1), ("O", count - 1)]
 
 
 def in_order(value, *earlier):
@@ -80,84 +93,103 @@
 TN = (((0,), (0,)), ((), ()))
 
 
+def tiles_of(keys, cached, size=256):
+    tiles, at = [], 0
+    for end in (cached, keys):
+        while at < end:
+            step = min(size, end - at)
+            tiles.append((at, step, end == cached))
+            at += step
+    return tiles
+
+
+def by_eight(op, array):
+    return op(array.reshape(array.shape[0] // 8, 8, array.shape[1]), axis=0)
+
+
 def attend_kernel(
-    start, heads, width, owner_ref, gain_hbm, own_hbm, far_sq_hbm, q_hbm, kc_hbm, vc_hbm, near_hbm,
-    far_hbm, out_ref, lse_s, s_a, s_b, p_a, p_b, gain_ref, own_sq, far_sq, q_ref, kc, vc, near,
-    far, small_sems, sems,
+    start, heads, width, owner_ref, own_sq, far_sq, gain_hbm, q_hbm, kc_hbm, vc_hbm, near_hbm,
+    far_hbm, out_ref, lse_s, s_a, s_b, p_a, p_b, gain_ref, q_ref, k_ref, v_ref, sems,
 ):
-    half = near.shape[0] // 2
-    cached = kc.shape[0]
+    half = near_hbm.shape[0] // 2
+    cached, keys = kc_hbm.shape[0], k_ref.shape[0]
     scale = LOG2E / HD**0.5
-    sources = (q_hbm, kc_hbm, near_hbm, far_hbm, vc_hbm)
-    mine = slice(start * HD, (start + heads) * HD)
-    small = [
-        pltpu.make_async_copy(own_hbm, own_sq, small_sems.at[0]),
-        pltpu.make_async_copy(far_sq_hbm, far_sq, small_sems.at[1]),
-        pltpu.make_async_copy(gain_hbm.at[:, mine], gain_ref, small_sems.at[2]),
+    moves = [
+        (gain_hbm, 0, gain_hbm.shape[0], gain_ref, 0),
+        (q_hbm, 0, q_hbm.shape[0], q_ref, 0),
+        (kc_hbm, 0, cached, k_ref, 0),
+        (near_hbm, 0, half, k_ref, cached),
+        (far_hbm, 0, half, k_ref, cached + half),
+        (vc_hbm, 0, cached, v_ref, 0),
+        (near_hbm, half, half, v_ref, cached),
+        (far_hbm, half, half, v_ref, cached + half),
     ]
-    for copy in small:
-        copy.start()
+    groups = [(0, 1), (1, heads)] if heads > 1 else [(0, 1)]
     copies = []
-    for h in range(heads):
-        here, there = slice(h * HD, (h + 1) * HD), slice((start + h) * HD, (start + h + 1) * HD)
+    for g, (low, high) in enumerate(groups):
+        here = slice(low * HD, high * HD)
+        there = slice((start + low) * HD, (start + high) * HD)
         copies.append(
             [
-                pltpu.make_async_copy(src.at[:, there], dst.at[:, here], sems.at[h, n])
-                for n, (src, dst) in enumerate(zip(sources, (q_ref, kc, near, far, vc)))
+                pltpu.make_async_copy(
+                    src.at[at : at + size, there], dst.at[to : to + size, here], sems.at[g, n]
+                )
+                for n, (src, at, size, dst, to) in enumerate(moves)
             ]
         )
-        for copy in copies[h]:
+        for copy in copies[g]:
             copy.start()
-    for copy in small:
-        copy.wait()
     total = own_sq[0:1, :] + far_sq[0:1, :]
     inverse = lax.rsqrt(total / width + EPSILON)
     inverse = jnp.broadcast_to(inverse, (HD, inverse.shape[1])).T
     penalty = jnp.where(owner_ref[0] == 1, F32(OUT), F32(0.0))
     s_refs, p_refs = (s_a, s_b), (p_a, p_b)
-    spans = [(0, cached), (cached, half), (cached + half, half)]
-    masses = {}
-
-    def score(h):
-        for copy in copies[h]:
-            copy.wait()
-        cols = slice(h * HD, (h + 1) * HD)
-        normed = (q_ref[:, cols].astype(F32) * inverse * gain_ref[:, cols]).astype(BF16)
-        for (at, size), k in zip(spans, (kc[:, cols], near[:half, cols], far[:half, cols])):
-            s_refs[h % 2][at : at + size, :] = lax.dot_general(
-                k, normed, NT, preferred_element_type=F32
-            )
-
-    def soften(h):
-        s_ref, p_ref = s_refs[h % 2], p_refs[h % 2]
-        top = jnp.max(s_ref[:cached, :], axis=0, keepdims=True) + penalty
-        top = jnp.maximum(top, jnp.max(s_ref[cached:, :], axis=0, keepdims=True))
-        base = top * scale
-        old = jnp.exp2(s_ref[:cached, :] * scale - (base - penalty))
-        p_ref[:cached, :] = old.astype(BF16)
-        new = jnp.exp2(s_ref[cached:, :] * scale - base)
-        p_ref[cached:, :] = new.astype(BF16)
-        mass = jnp.sum(old, axis=0, keepdims=True) + jnp.sum(new, axis=0, keepdims=True)
-        masses[h] = mass
-        lse_s[h : h + 1, :] = base + jnp.log2(mass)
-
-    def gather(h):
-        cols = slice(h * HD, (h + 1) * HD)
-        value = None
-        for (at, size), v in zip(spans, (vc[:, cols], near[half:, cols], far[half:, cols])):
-            part = lax.dot_general(
-                v, p_refs[h % 2][at : at + size, :], TN, preferred_element_type=F32
-            )
-            value = part if value is None else value + part
-        out_ref[h * HD : (h + 1) * HD, :] = (value * (1.0 / masses[h])).astype(BF16)
-
+    tiles = tiles_of(keys, cached)
+    bases, masses = {}, {}
     for t in range(heads + 2):
-        if 0 <= t - 2:
-            gather(t - 2)
-        if 0 <= t - 1 < heads:
-            soften(t - 1)
-        if t < heads:
-            score(t)
+        to_score, to_soften, to_gather = t, t - 1, t - 2
+        scoring, softening, gathering = t < heads, 0 <= t - 1 < heads, t - 2 >= 0
+        if t < len(groups):
+            for copy in copies[t]:
+                copy.wait()
+        if scoring:
+            cols = slice(to_score * HD, (to_score + 1) * HD)
+            normed = (q_ref[:, cols].astype(F32) * inverse * gain_ref[:, cols]).astype(BF16)
+            top = None
+        value, mass = None, None
+        for at, size, masked in tiles:
+            span = slice(at, at + size)
+            if gathering:
+                part = lax.dot_general(
+                    v_ref[span, to_gather * HD : (to_gather + 1) * HD],
+                    p_refs[to_gather % 2][span, :],
+                    TN,
+                    preferred_element_type=F32,
+                )
+                value = part if value is None else value + part
+            if scoring:
+                scores = lax.dot_general(k_ref[span, cols], normed, NT, preferred_element_type=F32)
+                s_refs[to_score % 2][span, :] = scores
+                most = by_eight(jnp.max, scores)
+                if masked:
+                    most = most + penalty
+                top = most if top is None else jnp.maximum(top, most)
+            if softening:
+                base = bases[to_soften]
+                shift = base - penalty if masked else base
+                raw = jnp.exp2(s_refs[to_soften % 2][span, :] * scale - shift)
+                p_refs[to_soften % 2][span, :] = raw.astype(BF16)
+                sums = by_eight(jnp.sum, raw)
+                mass = sums if mass is None else mass + sums
+        if gathering:
+            at = slice(to_gather * HD, (to_gather + 1) * HD)
+            out_ref[at, :] = (value * (1.0 / masses[to_gather])).astype(BF16)
+        if softening:
+            mass = jnp.sum(mass, axis=0, keepdims=True)
+            masses[to_soften] = mass
+            lse_s[to_soften : to_soften + 1, :] = bases[to_soften] + jnp.log2(mass)
+        if scoring:
+            bases[to_score] = jnp.max(top, axis=0, keepdims=True) * scale
     out_ref[heads * HD :, :] = split(lse_s[0:heads, :])
 
 
@@ -177,15 +209,14 @@
     return pl.pallas_call(
         functools.partial(attend_kernel, start, heads, width),
         out_shape=jax.ShapeDtypeStruct((wide + STATS, rows), BF16),
-        in_specs=[pl.BlockSpec(memory_space=pltpu.SMEM)] + [hbm()] * 8,
+        in_specs=[pl.BlockSpec(memory_space=pltpu.SMEM)] + [vmem()] * 2 + [hbm()] * 6,
         out_specs=vmem(),
         scratch_shapes=[pltpu.VMEM((8, rows), F32)]
         + [pltpu.VMEM((keys, rows), F32)] * 2
         + [pltpu.VMEM((keys, rows), BF16)] * 2
-        + [pltpu.VMEM((1, wide), F32), pltpu.VMEM((8, rows), F32), pltpu.VMEM((8, rows), F32)]
-        + [pltpu.VMEM((array.shape[0], wide), BF16) for array in (queries, kc, vc, near, far)]
-        + [pltpu.SemaphoreType.DMA((3,))]
-        + [pltpu.SemaphoreType.DMA((heads, 5))],
+        + [pltpu.VMEM((1, wide), F32), pltpu.VMEM((rows, wide), BF16)]
+        + [pltpu.VMEM((keys, wide), BF16)] * 2
+        + [pltpu.SemaphoreType.DMA((2, 8))],
         cost_estimate=pl.CostEstimate(
             flops=16 * heads * rows * keys * HD,
             bytes_accessed=4 * heads * keys * HD,
@@ -193,7 +224,7 @@
         ),
         compiler_params=pltpu.CompilerParams(vmem_limit_bytes=12 << 20),
         name="attend",
-    )(is_owner, gain, own_sq, far_sq, queries, kc, vc, near, far)
+    )(is_owner, own_sq, far_sq, gain, queries, kc, vc, near, far)
 
 
 def stats_of(ref, heads):
@@ -254,17 +285,14 @@
     far = lax.ppermute(near, "seq", [(0, 1), (1, 0)])
     is_owner = (slab == owner).astype(jnp.int32)
     gain = query_gain[None, :]
-    gain, own_sq, far_sq, near, far = in_hbm(gain, own_sq, far_sq, near, far)
+    gain, near, far = in_hbm(gain, near, far)
 
     sizes = chunk_sizes(heads)
     starts = [sum(sizes[:c]) for c in range(len(sizes))]
     count = len(sizes)
     side = n_slab // 2
-    lag = 3
     outer = functools.reduce(jnp.logical_or, [(slab < side - 1), (slab > side)])
-    inward = [
-        [(j, j + 1), (n_slab - 1 - j, n_slab - 2 - j)] for j in range(side - 1)
-    ]
+    inward = [[(j, j + 1), (n_slab - 1 - j, n_slab - 2 - j)] for j in range(side - 1)]
     outward = [[(b, a) for a, b in pairs] for pairs in inward]
     own, got_in, folded, crossed, total, final = {}, {}, {}, {}, {}, {}
     last = []
@@ -274,9 +302,10 @@
         return value
 
     def attention(c):
+        flag = in_order(is_owner, *last)
         own[c] = run(
             attend(
-                starts[c], sizes[c], width, in_order(is_owner, *last), queries, gain, own_sq,
+                starts[c], sizes[c], width, flag, queries, gain, own_sq,
                 far_sq, cache_keys, cache_values, near, far,
             )
         )
@@ -292,11 +321,13 @@
 
     def fold(c):
         take = ((slab == side - 1) | (slab == side)) if side != 2 else None
-        folded[c] = run(merge(sizes[c], take, own[c], in_order(got_in[c], *last)))
+        got = in_order(got_in[c], *last)
+        folded[c] = run(merge(sizes[c], take, own[c], got))
         crossed[c] = lax.ppermute(folded[c], "slab", [(side - 1, side), (side, side - 1)])
 
     def cross(c):
-        total[c] = run(merge(sizes[c], None, folded[c], in_order(crossed[c], *last)))
+        got = in_order(crossed[c], *last)
+        total[c] = run(merge(sizes[c], None, folded[c], got))
 
     def send_out(c):
         attended = total[c][: sizes[c] * HD]
@@ -305,28 +336,29 @@
             attended = jnp.where((slab == j) | (slab == n_slab - 1 - j), got, attended)
         final[c] = attended
 
-    for t in range(count):
-        attention(t)
-        back = t - lag
-        if back >= 0:
-            cross(back)
-        if side == 2 and back >= 0 and sizes[t] == sizes[back]:
-            sent = jnp.where(outer, own[t], total[back])
-            got = lax.ppermute(sent, "slab", inward[0] + outward[0])
-            got_in[t] = got
-            final[back] = jnp.where(outer, got, sent)[: sizes[back] * HD]
-        else:
-            send_in(t)
-            if back >= 0:
-                send_out(back)
-        if t >= 1:
-            fold(t - 1)
-    fold(count - 1)
-    for c in range(max(0, count - lag), count):
-        cross(c)
-        send_out(c)
-    attended = jnp.concatenate([final[c] for c in range(count)], axis=0)
-    projected = lax.dot_general(attended, out_weight, TN, preferred_element_type=F32)
+    def send_both(c):
+        if side != 2 or sizes[c] != sizes[-1]:
+            send_in(count - 1)
+            send_out(c)
+            return
+        sent = run(jnp.where(outer, own[count - 1], total[c]))
+        got = lax.ppermute(sent, "slab", inward[0] + outward[0])
+        got_in[count - 1] = got
+        final[c] = jnp.where(outer, got, sent)[: sizes[c] * HD]
+
+    steps = {"A": attention, "I": send_in, "F": fold, "C": cross, "O": send_out, "X": send_both}
+    for kind, c in order_of(count):
+        steps[kind](c)
+    projected = None
+    for first, stop in ((0, count - 1), (count - 1, count)):
+        attended = jnp.concatenate([final[c] for c in range(first, stop)], axis=0)
+        if projected is not None:
+            attended = in_order(attended, projected)
+        at = starts[first] * HD
+        term = lax.dot_general(
+            attended, out_weight[at : at + attended.shape[0]], TN, preferred_element_type=F32
+        )
+        projected = term if projected is None else projected + term
 
     half = time_weight.shape[0] // 2
     frequency = jnp.exp(-jnp.log(10000.0) * jnp.arange(half, dtype=F32) / half)
@@ -362,5 +394,9 @@
         P("grp"),
     )
     out_specs = P(("grp", "seq"), ("slab", "head"))
-    body = functools.partial(local, mesh.shape["slab"], mesh.shape["head"], mesh.shape["seq"])
+
+    def body(*arrays):
+        return local(*sizes, *arrays)
+
+    sizes = mesh.shape["slab"], mesh.shape["head"], mesh.shape["seq"]
     return jax.shard_map(body, mesh=mesh, in_specs=in_specs, out_specs=out_specs, check_vma=False)

time: 86.7 us -> 79.9 us (0.922)
  Pallas kernels: 22.4 us -> 16.1 us
  waiting for transfers between devices: 27.4 us -> 25.4 us
  starting transfers between devices: 26.8 us -> 25.1 us
  other arithmetic: 1.39 us -> 2.86 us
  matrix products: 5.2 us -> 6.52 us
    pallas_call x5 -> x4, Pallas kernels: 19.4 us -> 13 us  [attend(): pl.pallas_call(functools.partial(attend_kernel, start, heads, width), out...]
    ppermute x2 -> x1, waiting for transfers between devices: 7.09 us -> 4.76 us  [send_both(): got = lax.ppermute(sent, 'slab', inward[0] + outward[0])]
    select_n x2 -> x5, other arithmetic: 0.07 us -> 1.91 us  [the longest x1 1.02 us: send_both(): final[c] = jnp.where(outer, got, sent)[:sizes[c] * HD]]
    dot_general x1 -> x2, matrix products: 4.77 us -> 6.09 us  [local(): lax.dot_general(attended, out_weight[at:at + attended.shape[0]], TN, pref...]
    ppermute x2 -> x1, starting transfers between devices: 2.16 us -> 1.13 us  [send_both(): got = lax.ppermute(sent, 'slab', inward[0] + outward[0])]
    ppermute x5 -> x4, starting transfers between devices: 3.38 us -> 2.73 us  [fold(): lax.ppermute(folded[c], 'slab', [(side - 1, side), (side, side - 1)])]
  transfers between devices with their start and end apart: 16 -> 14, of which waited for: 8 -> 8; matrix products, arithmetic and copies ran while one was open for 2% -> 9% of each run, Pallas kernels for 19% -> 14%
where the time goes in v3:
time: 79.9 us; the launch traced here: 79.4 us
  waiting for transfers between devices  25.4 us (32%)
  starting transfers between devices  25.1 us (31%)
  Pallas kernels  16.1 us (20%)
  matrix products  6.52 us (8%)
  other arithmetic  2.86 us (4%)
  local copies, waits for them, and re-layouts  1.76 us (2%)
  between operations  1.65 us (2%)
    ppermute x3, waiting for transfers between devices, send_out(): got = lax.ppermute(attended, 'slab', outward[j])  14.6 us
    pallas_call x4, Pallas kernels, attend(): pl.pallas_call(functools.partial(attend_kernel, start, heads, width), out...  13 us
    ppermute x3, starting transfers between devices, send_in(): lax.ppermute(sent, 'slab', inward[side - 2])  12.6 us
    dot_general x2, matrix products, local(): lax.dot_general(attended, out_weight[at:at + attended.shape[0]], TN, pref...  6.09 us
    ppermute x1, waiting for transfers between devices, local(): summed = kept + lax.ppermute(sent, 'head', [(0, 1), (1, 0)]).astype(F32)  5.12 us
    ppermute x1, waiting for transfers between devices, send_both(): got = lax.ppermute(sent, 'slab', inward[0] + outward[0])  4.76 us
    ppermute x3, starting transfers between devices, send_out(): got = lax.ppermute(attended, 'slab', outward[j])  4.06 us
    ppermute x4, starting transfers between devices, fold(): lax.ppermute(folded[c], 'slab', [(side - 1, side), (side, side - 1)])  2.73 us
  transfers between devices with their start and end apart: 14, of which 8 were waited for; matrix products, arithmetic and copies ran while one was open for 9% of the time, Pallas kernels for 14%

profile of v3, /device:TPU:0, one launch (start us, length us, event | category | flops | bytes accessed | tf_op | source)
XLA Modules:
  0.0 79.4 jit_solution(10887482992534679180)
XLA Ops:
  0.0 0.0 copy-start
  0.0 0.0 copy-start.3
  0.0 1.8 %prepare.1 = (f32[8,256]{1,0:T(8,128)S(1)}, bf16[256,2560]{1,0:T(8,128)(2,1)S(1)}) custom-call(bf16[256,2560]{1,0:T(8,128)(2,1)} %q_hbm.9, bf16[64,2560]{1,0:T(8,128)(2,1)} %fk.1, bf16[64,2560]{1,0:T(8,128)(2,1)} %nk.1, bf16[64,2560]{1,0:T(8,128)(2,1)} %fv.1, bf16[64,2560]{1,0:T(8,128)(2,1)} %nv.1), custom_call_target="tpu_custom_call" | custom-call | flops 1310720 | bytes 5242880 | tf_op jit(solution)/shard_map/prepare/pallas_call | solution.py:75
  1.8 0.0 copy-start.1
  1.8 0.6 collective-permute-start.1
  2.4 2.6 %collective-permute-start = (f32[8,256]{1,0:T(8,128)S(1)}, f32[8,256]{1,0:T(8,128)S(1)}, u32[]{:S(2)}, u32[]{:S(2)}) collective-permute-start(f32[8,256]{1,0:T(8,128)S(1)} %get-tuple-element.19.own_sq), channel_id=1, source_target_pairs={{0,2},{2,0},{1,3},{3,1},{4,6},{6,4},{5,7},{7,5},{8,10},{10,8},{9,1... | collective-permute-start | bytes 24584 | tf_op jit(solution)/shard_map/ppermute | solution.py:281
  5.6 0.0 copy-done.3
  5.6 0.6 broadcast_in_dim.4.gain_hbm
  6.2 0.4 collective-permute-done.far_sq
  6.6 0.0 collective-permute-done.1.far_hbm
  6.6 0.0 copy-done.1
  6.6 0.0 copy-start.2
  6.6 1.1 %copy-done.2 = bf16[256,2560]{1,0:T(8,128)(2,1)} copy-done((bf16[256,2560]{1,0:T(8,128)(2,1)}, bf16[256,2560]{1,0:T(8,128)(2,1)S(1)}, u32[]{:S(2)}) %copy-start.2) | copy-done | bytes 1310744
  7.6 3.3 %attend.4.refs_0_ = bf16[656,256]{1,0:T(8,128)(2,1)S(1)} custom-call(s32[1]{0:T(128)S(6)} %convert_element_type.20.owner_ref, f32[8,256]{1,0:T(8,128)S(1)} %get-tuple-element.19.own_sq, f32[8,256]{1,0:T(8,128)S(1)} %collective-permute-done.far_sq, f32[1,2560]{1,0:T(1,128)} %broadcast_in_dim.4.gain_hbm, bf16[256,2560]{1,0:T(8,128)(2,1)} %q_hbm.9, ...), custom_call_target="tpu_custom_call" | custom-call | flops 2013265920 | bytes 1966080 | tf_op jit(solution)/shard_map/attend/pallas_call | solution.py:209
  10.9 4.0 %collective-permute-start.2 = (bf16[656,256]{1,0:T(8,128)(2,1)S(1)}, bf16[656,256]{1,0:T(8,128)(2,1)S(1)}, u32[]{:S(2)}, u32[]{:S(2)}) collective-permute-start(bf16[656,256]{1,0:T(8,128)(2,1)S(1)} %attend.4.refs_0_), channel_id=1, source_target_pairs={{0,4},{12,8},{1,5},{13,9},{2,6},{14,10},{3,7},{15,11},{16,20},{28,... | collective-permute-start | bytes 1007624 | tf_op jit(solution)/shard_map/ppermute | solution.py:320
  14.9 3.3 %attend.5.refs_0_ = bf16[656,256]{1,0:T(8,128)(2,1)S(1)} custom-call(s32[1]{0:T(128)S(6)} %convert_element_type.20.owner_ref, f32[8,256]{1,0:T(8,128)S(1)} %get-tuple-element.19.own_sq, f32[8,256]{1,0:T(8,128)S(1)} %collective-permute-done.far_sq, f32[1,2560]{1,0:T(1,128)} %broadcast_in_dim.4.gain_hbm, bf16[256,2560]{1,0:T(8,128)(2,1)} %q_hbm.9, ...), custom_call_target="tpu_custom_call" | custom-call | flops 2013265920 | bytes 1966080 | tf_op jit(solution)/shard_map/attend/pallas_call | solution.py:209
  18.2 1.3 %collective-permute-start.4 = (bf16[656,256]{1,0:T(8,128)(2,1)S(1)}, bf16[656,256]{1,0:T(8,128)(2,1)S(1)}, u32[]{:S(2)}, u32[]{:S(2)}) collective-permute-start(bf16[656,256]{1,0:T(8,128)(2,1)S(1)} %attend.5.refs_0_), channel_id=1, source_target_pairs={{0,4},{12,8},{1,5},{13,9},{2,6},{14,10},{3,7},{15,11},{16,20},{28,... | collective-permute-start | bytes 1007624 | tf_op jit(solution)/shard_map/ppermute | solution.py:320
  19.5 3.3 %attend.6.refs_0_ = bf16[656,256]{1,0:T(8,128)(2,1)S(1)} custom-call(s32[1]{0:T(128)S(6)} %convert_element_type.20.owner_ref, f32[8,256]{1,0:T(8,128)S(1)} %get-tuple-element.19.own_sq, f32[8,256]{1,0:T(8,128)S(1)} %collective-permute-done.far_sq, f32[1,2560]{1,0:T(1,128)} %broadcast_in_dim.4.gain_hbm, bf16[256,2560]{1,0:T(8,128)(2,1)} %q_hbm.9, ...), custom_call_target="tpu_custom_call" | custom-call | flops 2013265920 | bytes 1966080 | tf_op jit(solution)/shard_map/attend/pallas_call | solution.py:209
  22.8 0.4 collective-permute-done.2.refs_1_
  23.2 0.2 merge.8.refs_0_
  23.3 0.7 collective-permute-start.3
  24.0 7.2 %collective-permute-start.7 = (bf16[656,256]{1,0:T(8,128)(2,1)S(1)}, bf16[656,256]{1,0:T(8,128)(2,1)S(1)}, u32[]{:S(2)}, u32[]{:S(2)}) collective-permute-start(bf16[656,256]{1,0:T(8,128)(2,1)S(1)} %attend.6.refs_0_), channel_id=1, source_target_pairs={{0,4},{12,8},{1,5},{13,9},{2,6},{14,10},{3,7},{15,11},{16,20},{28,... | collective-permute-start | bytes 1007624 | tf_op jit(solution)/shard_map/ppermute | solution.py:320
  31.2 3.3 %attend.7.refs_0_ = bf16[656,256]{1,0:T(8,128)(2,1)S(1)} custom-call(s32[1]{0:T(128)S(6)} %convert_element_type.20.owner_ref, f32[8,256]{1,0:T(8,128)S(1)} %get-tuple-element.19.own_sq, f32[8,256]{1,0:T(8,128)S(1)} %collective-permute-done.far_sq, f32[1,2560]{1,0:T(1,128)} %broadcast_in_dim.4.gain_hbm, bf16[256,2560]{1,0:T(8,128)(2,1)} %q_hbm.9, ...), custom_call_target="tpu_custom_call" | custom-call | flops 2013265920 | bytes 1966080 | tf_op jit(solution)/shard_map/attend/pallas_call | solution.py:209
  34.5 0.0 collective-permute-done.4.refs_1_
  34.5 0.2 merge.9.refs_0_
  34.7 0.7 collective-permute-start.6
  35.4 0.0 collective-permute-done.3.refs_1_
  35.4 0.2 merge.10
  35.6 0.8 broadcast_select_fusion
  36.3 1.1 %collective-permute-start.5 = (bf16[656,256]{1,0:T(8,128)(2,1)}, bf16[656,256]{1,0:T(8,128)(2,1)S(1)}, u32[]{:S(2)}, u32[]{:S(2)}) collective-permute-start(bf16[656,256]{1,0:T(8,128)(2,1)} %broadcast_select_fusion), channel_id=1, source_target_pairs={{0,4},{12,8},{4,0},{8,12},{1,5},{13,9},{5,1},{9,13},{2,6},{14,10},... | collective-permute-start | bytes 1007624 | tf_op jit(solution)/shard_map/ppermute | solution.py:345
  37.5 0.1 collective-permute-done.7.refs_1_
  37.5 0.2 merge.11.refs_0_
  37.7 0.7 collective-permute-start.9
  38.4 0.0 collective-permute-done.6.refs_1_
  38.4 0.2 merge.12
  38.6 1.3 %collective-permute-start.8 = (bf16[640,256]{1,0:T(8,128)(2,1)S(1)}, bf16[640,256]{1,0:T(8,128)(2,1)S(1)}, u32[]{:S(2)}, u32[]{:S(2)}) collective-permute-start(bf16[640,256]{1,0:T(8,128)(2,1)S(1)} %slice.34), channel_id=1, source_target_pairs={{4,0},{8,12},{5,1},{9,13},{6,2},{10,14},{7,3},{11,15},{20,16},{24,... | collective-permute-start | bytes 983048 | tf_op jit(solution)/shard_map/ppermute | solution.py:335
  40.6 4.8 %collective-permute-done.5.refs_1_ = bf16[656,256]{1,0:T(8,128)(2,1)S(1)} collective-permute-done((bf16[656,256]{1,0:T(8,128)(2,1)}, bf16[656,256]{1,0:T(8,128)(2,1)S(1)}, u32[]{:S(2)}, u32[]{:S(2)}) %collective-permute-start.5) | collective-permute-done | bytes 335904 | tf_op jit(solution)/shard_map/ppermute | solution.py:345
  45.4 0.2 merge.13.refs_0_
  45.6 0.0 collective-permute-done.9.refs_1_
  45.6 0.2 merge.14
  45.8 1.3 %collective-permute-start.10 = (bf16[640,256]{1,0:T(8,128)(2,1)S(1)}, bf16[640,256]{1,0:T(8,128)(2,1)S(1)}, u32[]{:S(2)}, u32[]{:S(2)}) collective-permute-start(bf16[640,256]{1,0:T(8,128)(2,1)S(1)} %slice.35), channel_id=1, source_target_pairs={{4,0},{8,12},{5,1},{9,13},{6,2},{10,14},{7,3},{11,15},{20,16},{24,... | collective-permute-start | bytes 983048 | tf_op jit(solution)/shard_map/ppermute | solution.py:335
  47.1 6.6 %collective-permute-done.8 = bf16[640,256]{1,0:T(8,128)(2,1)S(1)} collective-permute-done((bf16[640,256]{1,0:T(8,128)(2,1)S(1)}, bf16[640,256]{1,0:T(8,128)(2,1)S(1)}, u32[]{:S(2)}, u32[]{:S(2)}) %collective-permute-start.8) | collective-permute-done | bytes 327712 | tf_op jit(solution)/shard_map/ppermute | solution.py:335
  53.7 0.7 collective-permute-start.11
  54.4 1.0 %slice_select_fusion = bf16[640,256]{1,0:T(8,128)(2,1)S(1)} fusion(bf16[656,256]{1,0:T(8,128)(2,1)} %broadcast_select_fusion, bf16[656,256]{1,0:T(8,128)(2,1)S(1)} %collective-permute-done.5.refs_1_, pred[]{:T(512)S(6)} %or.8), kind=kLoop, calls=%fused_computation.13 | loop fusion | flops 163840 | bytes 983041 | tf_op jit(solution)/shard_map/jit(_where)/select_n | solution.py:347
  55.4 3.5 %collective-permute-done.10 = bf16[640,256]{1,0:T(8,128)(2,1)S(1)} collective-permute-done((bf16[640,256]{1,0:T(8,128)(2,1)S(1)}, bf16[640,256]{1,0:T(8,128)(2,1)S(1)}, u32[]{:S(2)}, u32[]{:S(2)}) %collective-permute-start.10) | collective-permute-done | bytes 327712 | tf_op jit(solution)/shard_map/ppermute | solution.py:335
  59.0 0.0 collective-permute-done.11.refs_1_
  59.0 0.2 merge.15
  59.2 1.5 %collective-permute-start.12 = (bf16[640,256]{1,0:T(8,128)(2,1)S(1)}, bf16[640,256]{1,0:T(8,128)(2,1)S(1)}, u32[]{:S(2)}, u32[]{:S(2)}) collective-permute-start(bf16[640,256]{1,0:T(8,128)(2,1)S(1)} %slice.36), channel_id=1, source_target_pairs={{4,0},{8,12},{5,1},{9,13},{6,2},{10,14},{7,3},{11,15},{20,16},{24,... | collective-permute-start | bytes 983048 | tf_op jit(solution)/shard_map/ppermute | solution.py:335
  60.7 3.9 %fusion = f32[256,1280]{1,0:T(8,128)S(1)} fusion(bf16[2560,1280]{1,0:T(8,128)(2,1)} %param.20, bf16[640,256]{1,0:T(8,128)(2,1)S(1)} %broadcast_select_fusion.2, bf16[640,256]{1,0:T(8,128)(2,1)S(1)} %broadcast_select_fusion.3, bf16[640,256]{1,0:T(8,128)(2,1)S(1)} %slice_select_fusion), kind=kOutput, calls=%fused_computation | convolution fusion | flops 1261240320 | bytes 7208960 | tf_op jit(solution)/shard_map/dot_general | solution.py:358
  64.7 4.5 %collective-permute-done.12 = bf16[640,256]{1,0:T(8,128)(2,1)S(1)} collective-permute-done((bf16[640,256]{1,0:T(8,128)(2,1)S(1)}, bf16[640,256]{1,0:T(8,128)(2,1)S(1)}, u32[]{:S(2)}, u32[]{:S(2)}) %collective-permute-start.12) | collective-permute-done | bytes 327712 | tf_op jit(solution)/shard_map/ppermute | solution.py:335
  69.2 2.1 %convolution_add_fusion = f32[256,1280]{1,0:T(8,128)S(1)} fusion(f32[256,1280]{1,0:T(8,128)S(1)} %fusion, bf16[640,256]{1,0:T(8,128)(2,1)S(1)} %broadcast_select_fusion.1, bf16[2560,1280]{1,0:T(8,128)(2,1)} %param.20), kind=kOutput, calls=%fused_computation.2 | convolution fusion | flops 419758080 | bytes 4587520 | tf_op jit(solution)/shard_map/dot_general | solution.py:358
  71.3 0.1 select_convert_fusion
  71.4 1.6 %collective-permute-start.13 = (bf16[256,640]{1,0:T(8,128)(2,1)S(1)}, bf16[256,640]{1,0:T(8,128)(2,1)S(1)}, u32[]{:S(2)}, u32[]{:S(2)}) collective-permute-start(bf16[256,640]{1,0:T(8,128)(2,1)S(1)} %select_convert_fusion), channel_id=1, source_target_pairs={{0,2},{2,0},{1,3},{3,1},{4,6},{6,4},{5,7},{7,5},{8,10},{10,8},{9,1... | collective-permute-start | bytes 983048 | tf_op jit(solution)/shard_map/ppermute | solution.py:375
  72.9 0.0 copy-done
  73.0 0.4 convolution_reduce_fusion
  73.4 5.1 %collective-permute-done.13 = bf16[256,640]{1,0:T(8,128)(2,1)S(1)} collective-permute-done((bf16[256,640]{1,0:T(8,128)(2,1)S(1)}, bf16[256,640]{1,0:T(8,128)(2,1)S(1)}, u32[]{:S(2)}, u32[]{:S(2)}) %collective-permute-start.13) | collective-permute-done | bytes 327712 | tf_op jit(solution)/shard_map/ppermute | solution.py:375
  78.5 0.8 %multiply_convert_fusion = bf16[256,640]{1,0:T(8,128)(2,1)} fusion(bf16[256,640]{1,0:T(8,128)(2,1)S(1)} %collective-permute-done.13, f32[256,1280]{1,0:T(8,128)S(1)} %convolution_add_fusion, f32[640]{0:T(1024)S(1)} %broadcast_add_fusion, pred[]{:T(512)S(6)} %eq.20), kind=kLoop, calls=%fused_computation.10 | loop fusion | flops 819200 | bytes 1968641 | tf_op jit(solution)/shard_map/convert_element_type | solution.py:378
  (9 shorter events, 0.2 us)
Async XLA Ops:
  0.0 73.0 %copy-start = (f32[256,640]{1,0:T(8,128)S(1)}, f32[256,640]{1,0:T(8,128)}, u32[]{:S(2)}) copy-start(f32[256,640]{1,0:T(8,128)} %param.21) | copy-start | bytes 1966084
  0.0 5.6 %copy-start.3 = (f32[2560]{0:T(1024)S(1)}, f32[2560]{0:T(1024)}, u32[]{:S(2)}) copy-start(f32[2560]{0:T(1024)} %param.13) | copy-start | bytes 30724
  1.8 4.8 %copy-start.1 = (bf16[256,2560]{1,0:T(8,128)(2,1)}, bf16[256,2560]{1,0:T(8,128)(2,1)S(1)}, u32[]{:S(2)}) copy-start(bf16[256,2560]{1,0:T(8,128)(2,1)S(1)} %get-tuple-element.20.near_hbm) | copy-start | bytes 3932164
  1.8 4.7 %collective-permute-start.1 = (bf16[256,2560]{1,0:T(8,128)(2,1)S(1)}, bf16[256,2560]{1,0:T(8,128)(2,1)S(1)}, u32[]{:S(2)}, u32[]{:S(2)}) collective-permute-start(bf16[256,2560]{1,0:T(8,128)(2,1)S(1)} %get-tuple-element.20.near_hbm), channel_id=1, source_target_pairs={{0,1},{1,0},{2,3},{3,2},{4,5},{5,4},{6,7},{7,6},{8,9},{9,8},{10,11... | collective-permute-start | bytes 3932168 | tf_op jit(solution)/shard_map/ppermute | solution.py:285
  2.4 4.2 %collective-permute-start = (f32[8,256]{1,0:T(8,128)S(1)}, f32[8,256]{1,0:T(8,128)S(1)}, u32[]{:S(2)}, u32[]{:S(2)}) collective-permute-start(f32[8,256]{1,0:T(8,128)S(1)} %get-tuple-element.19.own_sq), channel_id=1, source_target_pairs={{0,2},{2,0},{1,3},{3,1},{4,6},{6,4},{5,7},{7,5},{8,10},{10,8},{9,1... | collective-permute-start | bytes 24584 | tf_op jit(solution)/shard_map/ppermute | solution.py:281
  6.6 1.1 %copy-start.2 = (bf16[256,2560]{1,0:T(8,128)(2,1)}, bf16[256,2560]{1,0:T(8,128)(2,1)S(1)}, u32[]{:S(2)}) copy-start(bf16[256,2560]{1,0:T(8,128)(2,1)S(1)} %collective-permute-done.1.far_hbm) | copy-start | bytes 3932164
  10.9 12.3 %collective-permute-start.2 = (bf16[656,256]{1,0:T(8,128)(2,1)S(1)}, bf16[656,256]{1,0:T(8,128)(2,1)S(1)}, u32[]{:S(2)}, u32[]{:S(2)}) collective-permute-start(bf16[656,256]{1,0:T(8,128)(2,1)S(1)} %attend.4.refs_0_), channel_id=1, source_target_pairs={{0,4},{12,8},{1,5},{13,9},{2,6},{14,10},{3,7},{15,11},{16,20},{28,... | collective-permute-start | bytes 1007624 | tf_op jit(solution)/shard_map/ppermute | solution.py:320
  18.2 16.3 %collective-permute-start.4 = (bf16[656,256]{1,0:T(8,128)(2,1)S(1)}, bf16[656,256]{1,0:T(8,128)(2,1)S(1)}, u32[]{:S(2)}, u32[]{:S(2)}) collective-permute-start(bf16[656,256]{1,0:T(8,128)(2,1)S(1)} %attend.5.refs_0_), channel_id=1, source_target_pairs={{0,4},{12,8},{1,5},{13,9},{2,6},{14,10},{3,7},{15,11},{16,20},{28,... | collective-permute-start | bytes 1007624 | tf_op jit(solution)/shard_map/ppermute | solution.py:320
  23.3 12.0 %collective-permute-start.3 = (bf16[656,256]{1,0:T(8,128)(2,1)S(1)}, bf16[656,256]{1,0:T(8,128)(2,1)S(1)}, u32[]{:S(2)}, u32[]{:S(2)}) collective-permute-start(bf16[656,256]{1,0:T(8,128)(2,1)S(1)} %merge.8.refs_0_), channel_id=1, source_target_pairs={{4,8},{8,4},{5,9},{9,5},{6,10},{10,6},{7,11},{11,7},{20,24},{24,20... | collective-permute-start | bytes 1007624 | tf_op jit(solution)/shard_map/ppermute | solution.py:326
  24.0 13.5 %collective-permute-start.7 = (bf16[656,256]{1,0:T(8,128)(2,1)S(1)}, bf16[656,256]{1,0:T(8,128)(2,1)S(1)}, u32[]{:S(2)}, u32[]{:S(2)}) collective-permute-start(bf16[656,256]{1,0:T(8,128)(2,1)S(1)} %attend.6.refs_0_), channel_id=1, source_target_pairs={{0,4},{12,8},{1,5},{13,9},{2,6},{14,10},{3,7},{15,11},{16,20},{28,... | collective-permute-start | bytes 1007624 | tf_op jit(solution)/shard_map/ppermute | solution.py:320
  34.7 3.7 %collective-permute-start.6 = (bf16[656,256]{1,0:T(8,128)(2,1)S(1)}, bf16[656,256]{1,0:T(8,128)(2,1)S(1)}, u32[]{:S(2)}, u32[]{:S(2)}) collective-permute-start(bf16[656,256]{1,0:T(8,128)(2,1)S(1)} %merge.9.refs_0_), channel_id=1, source_target_pairs={{4,8},{8,4},{5,9},{9,5},{6,10},{10,6},{7,11},{11,7},{20,24},{24,20... | collective-permute-start | bytes 1007624 | tf_op jit(solution)/shard_map/ppermute | solution.py:326
  36.3 9.1 %collective-permute-start.5 = (bf16[656,256]{1,0:T(8,128)(2,1)}, bf16[656,256]{1,0:T(8,128)(2,1)S(1)}, u32[]{:S(2)}, u32[]{:S(2)}) collective-permute-start(bf16[656,256]{1,0:T(8,128)(2,1)} %broadcast_select_fusion), channel_id=1, source_target_pairs={{0,4},{12,8},{4,0},{8,12},{1,5},{13,9},{5,1},{9,13},{2,6},{14,10},... | collective-permute-start | bytes 1007624 | tf_op jit(solution)/shard_map/ppermute | solution.py:345
  37.7 7.9 %collective-permute-start.9 = (bf16[656,256]{1,0:T(8,128)(2,1)S(1)}, bf16[656,256]{1,0:T(8,128)(2,1)S(1)}, u32[]{:S(2)}, u32[]{:S(2)}) collective-permute-start(bf16[656,256]{1,0:T(8,128)(2,1)S(1)} %merge.11.refs_0_), channel_id=1, source_target_pairs={{4,8},{8,4},{5,9},{9,5},{6,10},{10,6},{7,11},{11,7},{20,24},{24,20... | collective-permute-start | bytes 1007624 | tf_op jit(solution)/shard_map/ppermute | solution.py:326
  38.6 15.1 %collective-permute-start.8 = (bf16[640,256]{1,0:T(8,128)(2,1)S(1)}, bf16[640,256]{1,0:T(8,128)(2,1)S(1)}, u32[]{:S(2)}, u32[]{:S(2)}) collective-permute-start(bf16[640,256]{1,0:T(8,128)(2,1)S(1)} %slice.34), channel_id=1, source_target_pairs={{4,0},{8,12},{5,1},{9,13},{6,2},{10,14},{7,3},{11,15},{20,16},{24,... | collective-permute-start | bytes 983048 | tf_op jit(solution)/shard_map/ppermute | solution.py:335
  45.8 13.2 %collective-permute-start.10 = (bf16[640,256]{1,0:T(8,128)(2,1)S(1)}, bf16[640,256]{1,0:T(8,128)(2,1)S(1)}, u32[]{:S(2)}, u32[]{:S(2)}) collective-permute-start(bf16[640,256]{1,0:T(8,128)(2,1)S(1)} %slice.35), channel_id=1, source_target_pairs={{4,0},{8,12},{5,1},{9,13},{6,2},{10,14},{7,3},{11,15},{20,16},{24,... | collective-permute-start | bytes 983048 | tf_op jit(solution)/shard_map/ppermute | solution.py:335
  53.7 5.3 %collective-permute-start.11 = (bf16[656,256]{1,0:T(8,128)(2,1)S(1)}, bf16[656,256]{1,0:T(8,128)(2,1)S(1)}, u32[]{:S(2)}, u32[]{:S(2)}) collective-permute-start(bf16[656,256]{1,0:T(8,128)(2,1)S(1)} %merge.13.refs_0_), channel_id=1, source_target_pairs={{4,8},{8,4},{5,9},{9,5},{6,10},{10,6},{7,11},{11,7},{20,24},{24,20... | collective-permute-start | bytes 1007624 | tf_op jit(solution)/shard_map/ppermute | solution.py:326
  59.2 9.9 %collective-permute-start.12 = (bf16[640,256]{1,0:T(8,128)(2,1)S(1)}, bf16[640,256]{1,0:T(8,128)(2,1)S(1)}, u32[]{:S(2)}, u32[]{:S(2)}) collective-permute-start(bf16[640,256]{1,0:T(8,128)(2,1)S(1)} %slice.36), channel_id=1, source_target_pairs={{4,0},{8,12},{5,1},{9,13},{6,2},{10,14},{7,3},{11,15},{20,16},{24,... | collective-permute-start | bytes 983048 | tf_op jit(solution)/shard_map/ppermute | solution.py:335
  71.4 7.1 %collective-permute-start.13 = (bf16[256,640]{1,0:T(8,128)(2,1)S(1)}, bf16[256,640]{1,0:T(8,128)(2,1)S(1)}, u32[]{:S(2)}, u32[]{:S(2)}) collective-permute-start(bf16[256,640]{1,0:T(8,128)(2,1)S(1)} %select_convert_fusion), channel_id=1, source_target_pairs={{0,2},{2,0},{1,3},{3,1},{4,6},{6,4},{5,7},{7,5},{8,10},{10,8},{9,1... | collective-permute-start | bytes 983048 | tf_op jit(solution)/shard_map/ppermute | solution.py:375

commit v4 on v3

--- a/solution.py
+++ b/solution.py
@@ -18,20 +18,25 @@
 
 
 def chunk_sizes(heads):
-    count = -(-heads // 5) if heads > 5 else 2
+    count = -(-heads // 4) if heads > 4 else 2
     return [heads // count + (c < heads % count) for c in range(count)]
 
 
-def order_of(count):
+def order_of(sizes):
+    count = len(sizes)
     if count < 3:
         steps = [(kind, c) for c in range(count) for kind in "AI"]
         steps += [("F", c) for c in range(count)]
         return steps + [(kind, c) for c in range(count) for kind in "CO"]
-    steps = [(kind, c) for c in range(count - 1) for kind in "AI"]
-    steps += [("F", 0), ("A", count - 1), ("F", 1), ("C", 0), ("X", 0)]
-    for c in range(2, count):
-        steps += [("F", c), ("C", c - 1), ("O", c - 1)]
-    return steps + [("C", count - 1), ("O", count - 1)]
+    steps = [(kind, c) for c in range(3) for kind in "AI"] + [("F", 0)]
+    for c in range(3, count):
+        steps += [("A", c), ("F", c - 2), ("C", c - 3)]
+        steps += [("X", c)] if sizes[c] == sizes[c - 3] else [("I", c), ("O", c - 3)]
+    for c in range(max(count - 3, 0), count):
+        if c + 1 < count:
+            steps += [("F", c + 1)]
+        steps += [("C", c), ("O", c)]
+    return steps
 
 
 def in_order(value, *earlier):
@@ -46,27 +51,38 @@
     return pl.BlockSpec(memory_space=pltpu.HBM)
 
 
+def anywhere():
+    return pl.BlockSpec(memory_space=pl.ANY)
+
+
 def in_hbm(*arrays):
     return [pltpu.with_memory_space_constraint(array, pltpu.HBM) for array in arrays]
 
 
 def prepare_kernel(q_hbm, fk, nk, fv, nv, squares_ref, near_ref, q_ref, sems):
     rows = fk.shape[0]
-    copies = [pltpu.make_async_copy(q_hbm, q_ref, sems.at[0])] + [
-        pltpu.make_async_copy(src, near_ref.at[pl.ds(n * rows, rows), :], sems.at[n + 1])
+    heads = q_ref.shape[1] // HD
+    pieces = [slice(c * 5 * HD, min((c + 1) * 5, heads) * HD) for c in range(-(-heads // 5))]
+    loads = [
+        pltpu.make_async_copy(q_hbm.at[:, piece], q_ref.at[:, piece], sems.at[n + 4])
+        for n, piece in enumerate(pieces)
+    ]
+    copies = [
+        pltpu.make_async_copy(src, near_ref.at[pl.ds(n * rows, rows), :], sems.at[n])
         for n, src in enumerate((fk, nk, fv, nv))
     ]
-    for copy in copies:
+    for copy in loads + copies:
         copy.start()
-    copies[0].wait()
     total = None
-    for h in range(q_ref.shape[1] // HD):
+    for h in range(heads):
+        if h % 5 == 0:
+            loads[h // 5].wait()
         block = q_ref[:, h * HD : (h + 1) * HD].astype(F32)
         term = block * block
         total = term if total is None else total + term
     row = jnp.sum(total.T, axis=0, keepdims=True)
     squares_ref[...] = jnp.broadcast_to(row, squares_ref.shape)
-    for copy in copies[1:]:
+    for copy in copies:
         copy.wait()
 
 
@@ -80,7 +96,7 @@
         ),
         in_specs=[hbm()] * 5,
         out_specs=(vmem(), vmem()),
-        scratch_shapes=[pltpu.VMEM(queries.shape, BF16), pltpu.SemaphoreType.DMA((5,))],
+        scratch_shapes=[pltpu.VMEM(queries.shape, BF16), pltpu.SemaphoreType.DMA((4 + -(-queries.shape[1] // (5 * HD)),))],
         cost_estimate=pl.CostEstimate(
             flops=2 * queries.size, bytes_accessed=8 * queries.size, transcendentals=0
         ),
@@ -209,7 +225,7 @@
     return pl.pallas_call(
         functools.partial(attend_kernel, start, heads, width),
         out_shape=jax.ShapeDtypeStruct((wide + STATS, rows), BF16),
-        in_specs=[pl.BlockSpec(memory_space=pltpu.SMEM)] + [vmem()] * 2 + [hbm()] * 6,
+        in_specs=[pl.BlockSpec(memory_space=pltpu.SMEM)] + [vmem()] * 2 + [hbm()] * 5 + [anywhere()],
         out_specs=vmem(),
         scratch_shapes=[pltpu.VMEM((8, rows), F32)]
         + [pltpu.VMEM((keys, rows), F32)] * 2
@@ -264,6 +280,81 @@
     )(*guard, own, got)
 
 
+def project_kernel(parts, attended_ref, weight_hbm, sum_ref, later_ref, turned, weight, sems):
+    depth, cols = attended_ref.shape[0], sum_ref.shape[1]
+    step = depth // parts
+    copies = [
+        pltpu.make_async_copy(
+            weight_hbm.at[pl.ds(n * step, step), :], weight.at[pl.ds(n * step, step), :], sems.at[n]
+        )
+        for n in range(parts)
+    ]
+    copies.append(
+        pltpu.make_async_copy(
+            weight_hbm.at[pl.ds(depth, later_ref.shape[0]), :], later_ref, sems.at[parts]
+        )
+    )
+    for copy in copies:
+        copy.start()
+    turned[...] = attended_ref[...].T
+    for n in range(parts):
+        copies[n].wait()
+        span = slice(n * step, (n + 1) * step)
+        for low in range(0, cols, 256):
+            tile = slice(low, min(low + 256, cols))
+            term = jnp.dot(turned[:, span], weight[span, tile], preferred_element_type=F32)
+            sum_ref[:, tile] = term if n == 0 else sum_ref[:, tile] + term
+    copies[parts].wait()
+
+
+def project(parts, attended, weight):
+    depth, rows = attended.shape
+    cols = weight.shape[1]
+    return pl.pallas_call(
+        functools.partial(project_kernel, parts),
+        out_shape=(
+            jax.ShapeDtypeStruct((rows, cols), F32),
+            jax.ShapeDtypeStruct((weight.shape[0] - depth, cols), BF16),
+        ),
+        in_specs=[vmem(), hbm()],
+        out_specs=(vmem(), vmem()),
+        scratch_shapes=[
+            pltpu.VMEM((rows, depth), BF16),
+            pltpu.VMEM((depth, cols), BF16),
+            pltpu.SemaphoreType.DMA((parts + 1,)),
+        ],
+        cost_estimate=pl.CostEstimate(
+            flops=2 * depth * rows * cols, bytes_accessed=2 * weight.size, transcendentals=0
+        ),
+        compiler_params=pltpu.CompilerParams(vmem_limit_bytes=16 << 20),
+        name="project",
+    )(attended, weight)
+
+
+def finish_kernel(attended_ref, weight_ref, sum_ref, out_ref):
+    turned = attended_ref[...].T
+    for low in range(0, out_ref.shape[1], 256):
+        tile = slice(low, min(low + 256, out_ref.shape[1]))
+        term = jnp.dot(turned, weight_ref[:, tile], preferred_element_type=F32)
+        out_ref[:, tile] = sum_ref[:, tile] + term
+
+
+def finish(attended, weight, summed):
+    return pl.pallas_call(
+        finish_kernel,
+        out_shape=jax.ShapeDtypeStruct(summed.shape, F32),
+        in_specs=[vmem()] * 3,
+        out_specs=vmem(),
+        cost_estimate=pl.CostEstimate(
+            flops=2 * attended.size * weight.shape[1],
+            bytes_accessed=2 * weight.size,
+            transcendentals=0,
+        ),
+        compiler_params=pltpu.CompilerParams(vmem_limit_bytes=12 << 20),
+        name="finish",
+    )(attended, weight, summed)
+
+
 def local(
     n_slab, n_head, n_seq,
     queries, query_gain, cache_keys, cache_values, finished_keys, finished_values,
@@ -272,6 +363,7 @@
     queries, cache_keys, cache_values, finished_keys, finished_values, new_keys, new_values = in_hbm(
         queries, cache_keys, cache_values, finished_keys, finished_values, new_keys, new_values
     )
+    (out_weight,) = in_hbm(out_weight)
     heads = queries.shape[1] // HD
     width = queries.shape[1] * n_head
     slab = lax.axis_index("slab")
@@ -285,6 +377,7 @@
     far = lax.ppermute(near, "seq", [(0, 1), (1, 0)])
     is_owner = (slab == owner).astype(jnp.int32)
     gain = query_gain[None, :]
+    first_far = far
     gain, near, far = in_hbm(gain, near, far)
 
     sizes = chunk_sizes(heads)
@@ -306,7 +399,7 @@
         own[c] = run(
             attend(
                 starts[c], sizes[c], width, flag, queries, gain, own_sq,
-                far_sq, cache_keys, cache_values, near, far,
+                far_sq, cache_keys, cache_values, near, far if c else first_far,
             )
         )
 
@@ -337,28 +430,21 @@
         final[c] = attended
 
     def send_both(c):
-        if side != 2 or sizes[c] != sizes[-1]:
-            send_in(count - 1)
-            send_out(c)
+        if side != 2:
+            send_in(c)
+            send_out(c - 3)
             return
-        sent = run(jnp.where(outer, own[count - 1], total[c]))
+        sent = run(jnp.where(outer, own[c], total[c - 3]))
         got = lax.ppermute(sent, "slab", inward[0] + outward[0])
-        got_in[count - 1] = got
-        final[c] = jnp.where(outer, got, sent)[: sizes[c] * HD]
+        got_in[c] = got
+        final[c - 3] = jnp.where(outer, got, sent)[: sizes[c - 3] * HD]
 
     steps = {"A": attention, "I": send_in, "F": fold, "C": cross, "O": send_out, "X": send_both}
-    for kind, c in order_of(count):
+    for kind, c in order_of(sizes):
         steps[kind](c)
-    projected = None
-    for first, stop in ((0, count - 1), (count - 1, count)):
-        attended = jnp.concatenate([final[c] for c in range(first, stop)], axis=0)
-        if projected is not None:
-            attended = in_order(attended, projected)
-        at = starts[first] * HD
-        term = lax.dot_general(
-            attended, out_weight[at : at + attended.shape[0]], TN, preferred_element_type=F32
-        )
-        projected = term if projected is None else projected + term
+    early = jnp.concatenate([final[c] for c in range(count - 1)], axis=0)
+    projected, later = project(count - 1, in_order(early, *last), out_weight)
+    projected = finish(in_order(final[count - 1], projected), later, projected)
 
     half = time_weight.shape[0] // 2
     frequency = jnp.exp(-jnp.log(10000.0) * jnp.arange(half, dtype=F32) / half)

time: 79.9 us -> 75.5 us (0.945)
  matrix products: 6.52 us -> 0.43 us
  Pallas kernels: 16.1 us -> 21.8 us
  waiting for transfers between devices: 25.4 us -> 20.4 us
  starting transfers between devices: 25.1 us -> 28.7 us
  other arithmetic: 2.86 us -> 1.25 us
  local copies, waits for them, and re-layouts: 1.76 us -> 0.68 us
    dot_general x2 -> x0, matrix products: 6.09 us -> none  [local(): lax.dot_general(attended, out_weight[at:at + attended.shape[0]], TN, pref...]
    pallas_call x0 -> x2, Pallas kernels: none -> 3.97 us  [the longest x1 3.42 us: project(): pl.pallas_call(functools.partial(project_kernel, parts), out_shape=(jax.S...]
    ppermute x1 -> x2, starting transfers between devices: 1.13 us -> 4.26 us  [send_both(): got = lax.ppermute(sent, 'slab', inward[0] + outward[0])]
    ppermute x1 -> x2, waiting for transfers between devices: 4.76 us -> 1.84 us  [send_both(): got = lax.ppermute(sent, 'slab', inward[0] + outward[0])]
    pallas_call x4 -> x5, Pallas kernels: 13 us -> 14.7 us  [attend(): pl.pallas_call(functools.partial(attend_kernel, start, heads, width), out...]
    select_n x2 -> x4, other arithmetic: 1.79 us -> 0.13 us  [the longest x2 0.07 us: send_both(): sent = run(jnp.where(outer, own[c], total[c - 3]))]
    ppermute x3, waiting for transfers between devices: 14.6 us -> 13 us  [send_out(): got = lax.ppermute(attended, 'slab', outward[j])]
    unnamed x8, local copies, waits for them, and re-layouts: 1.09 us -> 0.02 us
  transfers between devices with their start and end apart: 14 -> 16, of which waited for: 8 -> 5; matrix products, arithmetic and copies ran while one was open for 9% -> 2% of each run, Pallas kernels for 14% -> 22%
where the time goes in v4:
time: 75.5 us; the launch traced here: 75 us
  starting transfers between devices  28.7 us (38%)
  Pallas kernels  21.8 us (29%)
  waiting for transfers between devices  20.4 us (27%)
  between operations  1.77 us (2%)
  other arithmetic  1.25 us (2%)
    pallas_call x5, Pallas kernels, attend(): pl.pallas_call(functools.partial(attend_kernel, start, heads, width), out...  14.7 us
    ppermute x3, waiting for transfers between devices, send_out(): got = lax.ppermute(attended, 'slab', outward[j])  13 us
    ppermute x3, starting transfers between devices, send_in(): lax.ppermute(sent, 'slab', inward[side - 2])  12.3 us
    ppermute x1, waiting for transfers between devices, local(): summed = kept + lax.ppermute(sent, 'head', [(0, 1), (1, 0)]).astype(F32)  5.12 us
    ppermute x2, starting transfers between devices, send_both(): got = lax.ppermute(sent, 'slab', inward[0] + outward[0])  4.26 us
    ppermute x3, starting transfers between devices, send_out(): got = lax.ppermute(attended, 'slab', outward[j])  4.06 us
    pallas_call x1, Pallas kernels, project(): pl.pallas_call(functools.partial(project_kernel, parts), out_shape=(jax.S...  3.42 us
    ppermute x5, starting transfers between devices, fold(): lax.ppermute(folded[c], 'slab', [(side - 1, side), (side, side - 1)])  3.39 us
  transfers between devices with their start and end apart: 16, of which 5 were waited for; matrix products, arithmetic and copies ran while one was open for 2% of the time, Pallas kernels for 22%

profile of v4, /device:TPU:0, one launch (start us, length us, event | category | flops | bytes accessed | tf_op | source)
XLA Modules:
  0.0 75.0 jit_solution(17607011544685453633)
XLA Ops:
  0.0 0.0 copy-start
  0.0 0.0 copy-start.3
  0.0 1.8 %prepare.1 = (f32[8,256]{1,0:T(8,128)S(1)}, bf16[256,2560]{1,0:T(8,128)(2,1)S(1)}) custom-call(bf16[256,2560]{1,0:T(8,128)(2,1)} %q_hbm.11, bf16[64,2560]{1,0:T(8,128)(2,1)} %fk.1, bf16[64,2560]{1,0:T(8,128)(2,1)} %nk.1, bf16[64,2560]{1,0:T(8,128)(2,1)} %fv.1, bf16[64,2560]{1,0:T(8,128)(2,1)} %nv.1), custom_call_target="tpu_custom_call" | custom-call | flops 1310720 | bytes 5242880 | tf_op jit(solution)/shard_map/prepare/pallas_call | solution.py:91
  1.8 0.0 copy-start.1
  1.8 0.6 collective-permute-start.1
  2.4 2.6 %collective-permute-start = (f32[8,256]{1,0:T(8,128)S(1)}, f32[8,256]{1,0:T(8,128)S(1)}, u32[]{:S(2)}, u32[]{:S(2)}) collective-permute-start(f32[8,256]{1,0:T(8,128)S(1)} %get-tuple-element.25.own_sq), channel_id=1, source_target_pairs={{0,2},{2,0},{1,3},{3,1},{4,6},{6,4},{5,7},{7,5},{8,10},{10,8},{9,1... | collective-permute-start | bytes 24584 | tf_op jit(solution)/shard_map/ppermute | solution.py:373
  5.6 0.0 copy-done.3
  5.6 0.6 broadcast_in_dim.4.gain_hbm
  6.2 0.4 collective-permute-done.far_sq
  6.6 0.0 collective-permute-done.1.far_hbm
  6.6 0.0 copy-done.1
  6.6 0.0 copy-start.2
  6.6 3.2 %attend.5.refs_0_ = bf16[528,256]{1,0:T(8,128)(2,1)S(1)} custom-call(s32[1]{0:T(128)S(6)} %convert_element_type.20.owner_ref, f32[8,256]{1,0:T(8,128)S(1)} %get-tuple-element.25.own_sq, f32[8,256]{1,0:T(8,128)S(1)} %collective-permute-done.far_sq, f32[1,2560]{1,0:T(1,128)} %broadcast_in_dim.4.gain_hbm, bf16[256,2560]{1,0:T(8,128)(2,1)} %q_hbm.11, ...), custom_call_target="tpu_custom_call" | custom-call | flops 1610612736 | bytes 1572864 | tf_op jit(solution)/shard_map/attend/pallas_call | solution.py:225
  9.9 0.0 copy-done.2
  9.9 4.0 %collective-permute-start.2 = (bf16[528,256]{1,0:T(8,128)(2,1)S(1)}, bf16[528,256]{1,0:T(8,128)(2,1)S(1)}, u32[]{:S(2)}, u32[]{:S(2)}) collective-permute-start(bf16[528,256]{1,0:T(8,128)(2,1)S(1)} %attend.5.refs_0_), channel_id=1, source_target_pairs={{0,4},{12,8},{1,5},{13,9},{2,6},{14,10},{3,7},{15,11},{16,20},{28,... | collective-permute-start | bytes 811016 | tf_op jit(solution)/shard_map/ppermute | solution.py:413
  13.9 2.9 %attend.6.refs_0_ = bf16[528,256]{1,0:T(8,128)(2,1)S(1)} custom-call(s32[1]{0:T(128)S(6)} %convert_element_type.20.owner_ref, f32[8,256]{1,0:T(8,128)S(1)} %get-tuple-element.25.own_sq, f32[8,256]{1,0:T(8,128)S(1)} %collective-permute-done.far_sq, f32[1,2560]{1,0:T(1,128)} %broadcast_in_dim.4.gain_hbm, bf16[256,2560]{1,0:T(8,128)(2,1)} %q_hbm.11, ...), custom_call_target="tpu_custom_call" | custom-call | flops 1610612736 | bytes 1572864 | tf_op jit(solution)/shard_map/attend/pallas_call | solution.py:225
  16.8 1.3 %collective-permute-start.4 = (bf16[528,256]{1,0:T(8,128)(2,1)S(1)}, bf16[528,256]{1,0:T(8,128)(2,1)S(1)}, u32[]{:S(2)}, u32[]{:S(2)}) collective-permute-start(bf16[528,256]{1,0:T(8,128)(2,1)S(1)} %attend.6.refs_0_), channel_id=1, source_target_pairs={{0,4},{12,8},{1,5},{13,9},{2,6},{14,10},{3,7},{15,11},{16,20},{28,... | collective-permute-start | bytes 811016 | tf_op jit(solution)/shard_map/ppermute | solution.py:413
  18.1 2.9 %attend.7.refs_0_ = bf16[528,256]{1,0:T(8,128)(2,1)S(1)} custom-call(s32[1]{0:T(128)S(6)} %convert_element_type.20.owner_ref, f32[8,256]{1,0:T(8,128)S(1)} %get-tuple-element.25.own_sq, f32[8,256]{1,0:T(8,128)S(1)} %collective-permute-done.far_sq, f32[1,2560]{1,0:T(1,128)} %broadcast_in_dim.4.gain_hbm, bf16[256,2560]{1,0:T(8,128)(2,1)} %q_hbm.11, ...), custom_call_target="tpu_custom_call" | custom-call | flops 1610612736 | bytes 1572864 | tf_op jit(solution)/shard_map/attend/pallas_call | solution.py:225
  21.0 0.0 collective-permute-done.2.refs_1_
  21.0 0.1 merge.10.refs_0_
  21.1 0.7 collective-permute-start.3
  21.8 7.0 %collective-permute-start.6 = (bf16[528,256]{1,0:T(8,128)(2,1)S(1)}, bf16[528,256]{1,0:T(8,128)(2,1)S(1)}, u32[]{:S(2)}, u32[]{:S(2)}) collective-permute-start(bf16[528,256]{1,0:T(8,128)(2,1)S(1)} %attend.7.refs_0_), channel_id=1, source_target_pairs={{0,4},{12,8},{1,5},{13,9},{2,6},{14,10},{3,7},{15,11},{16,20},{28,... | collective-permute-start | bytes 811016 | tf_op jit(solution)/shard_map/ppermute | solution.py:413
  28.8 2.9 %attend.8.refs_0_ = bf16[528,256]{1,0:T(8,128)(2,1)S(1)} custom-call(s32[1]{0:T(128)S(6)} %convert_element_type.20.owner_ref, f32[8,256]{1,0:T(8,128)S(1)} %get-tuple-element.25.own_sq, f32[8,256]{1,0:T(8,128)S(1)} %collective-permute-done.far_sq, f32[1,2560]{1,0:T(1,128)} %broadcast_in_dim.4.gain_hbm, bf16[256,2560]{1,0:T(8,128)(2,1)} %q_hbm.11, ...), custom_call_target="tpu_custom_call" | custom-call | flops 1610612736 | bytes 1572864 | tf_op jit(solution)/shard_map/attend/pallas_call | solution.py:225
  31.7 0.0 collective-permute-done.4.refs_1_
  31.7 0.1 merge.11.refs_0_
  31.8 0.7 collective-permute-start.5
  32.5 0.0 collective-permute-done.3.refs_1_
  32.5 0.1 merge.12
  32.7 1.1 %collective-permute-start.9 = (bf16[528,256]{1,0:T(8,128)(2,1)S(1)}, bf16[528,256]{1,0:T(8,128)(2,1)S(1)}, u32[]{:S(2)}, u32[]{:S(2)}) collective-permute-start(bf16[528,256]{1,0:T(8,128)(2,1)S(1)} %broadcast_select_fusion.1), channel_id=1, source_target_pairs={{0,4},{12,8},{4,0},{8,12},{1,5},{13,9},{5,1},{9,13},{2,6},{14,10},... | collective-permute-start | bytes 811016 | tf_op jit(solution)/shard_map/ppermute | solution.py:438
  33.8 2.9 %attend.9.refs_0_ = bf16[528,256]{1,0:T(8,128)(2,1)S(1)} custom-call(s32[1]{0:T(128)S(6)} %convert_element_type.20.owner_ref, f32[8,256]{1,0:T(8,128)S(1)} %get-tuple-element.25.own_sq, f32[8,256]{1,0:T(8,128)S(1)} %collective-permute-done.far_sq, f32[1,2560]{1,0:T(1,128)} %broadcast_in_dim.4.gain_hbm, bf16[256,2560]{1,0:T(8,128)(2,1)} %q_hbm.11, ...), custom_call_target="tpu_custom_call" | custom-call | flops 1610612736 | bytes 1572864 | tf_op jit(solution)/shard_map/attend/pallas_call | solution.py:225
  36.7 0.0 collective-permute-done.6.refs_1_
  36.7 0.1 merge.13.refs_0_
  36.8 0.7 collective-permute-start.8
  37.5 0.0 collective-permute-done.5.refs_1_
  37.5 0.1 merge.14
  37.7 3.1 %collective-permute-start.7 = (bf16[528,256]{1,0:T(8,128)(2,1)S(1)}, bf16[528,256]{1,0:T(8,128)(2,1)S(1)}, u32[]{:S(2)}, u32[]{:S(2)}) collective-permute-start(bf16[528,256]{1,0:T(8,128)(2,1)S(1)} %broadcast_select_fusion), channel_id=1, source_target_pairs={{0,4},{12,8},{4,0},{8,12},{1,5},{13,9},{5,1},{9,13},{2,6},{14,10},... | collective-permute-start | bytes 811016 | tf_op jit(solution)/shard_map/ppermute | solution.py:438
  41.6 0.0 collective-permute-done.9.refs_1_
  41.6 0.1 merge.15.refs_0_
  41.7 0.7 collective-permute-start.11
  42.4 0.0 collective-permute-done.8.refs_1_
  42.4 0.1 merge.16
  42.6 1.3 %collective-permute-start.13 = (bf16[512,256]{1,0:T(8,128)(2,1)S(1)}, bf16[512,256]{1,0:T(8,128)(2,1)S(1)}, u32[]{:S(2)}, u32[]{:S(2)}) collective-permute-start(bf16[512,256]{1,0:T(8,128)(2,1)S(1)} %slice.33), channel_id=1, source_target_pairs={{4,0},{8,12},{5,1},{9,13},{6,2},{10,14},{7,3},{11,15},{20,16},{24,... | collective-permute-start | bytes 786440 | tf_op jit(solution)/shard_map/ppermute | solution.py:428
  43.9 1.8 %collective-permute-done.7.refs_1_ = bf16[528,256]{1,0:T(8,128)(2,1)S(1)} collective-permute-done((bf16[528,256]{1,0:T(8,128)(2,1)S(1)}, bf16[528,256]{1,0:T(8,128)(2,1)S(1)}, u32[]{:S(2)}, u32[]{:S(2)}) %collective-permute-start.7) | collective-permute-done | bytes 270368 | tf_op jit(solution)/shard_map/ppermute | solution.py:438
  45.7 0.1 merge.17.refs_0_
  45.9 0.7 collective-permute-start.10
  46.6 0.0 collective-permute-done.11.refs_1_
  46.6 0.1 merge.18
  46.8 1.3 %collective-permute-start.14 = (bf16[512,256]{1,0:T(8,128)(2,1)S(1)}, bf16[512,256]{1,0:T(8,128)(2,1)S(1)}, u32[]{:S(2)}, u32[]{:S(2)}) collective-permute-start(bf16[512,256]{1,0:T(8,128)(2,1)S(1)} %slice.34), channel_id=1, source_target_pairs={{4,0},{8,12},{5,1},{9,13},{6,2},{10,14},{7,3},{11,15},{20,16},{24,... | collective-permute-start | bytes 786440 | tf_op jit(solution)/shard_map/ppermute | solution.py:428
  48.1 9.2 %collective-permute-done.13 = bf16[512,256]{1,0:T(8,128)(2,1)S(1)} collective-permute-done((bf16[512,256]{1,0:T(8,128)(2,1)S(1)}, bf16[512,256]{1,0:T(8,128)(2,1)S(1)}, u32[]{:S(2)}, u32[]{:S(2)}) %collective-permute-start.13) | collective-permute-done | bytes 262176 | tf_op jit(solution)/shard_map/ppermute | solution.py:428
  57.4 0.0 collective-permute-done.10.refs_1_
  57.4 0.1 merge.19
  57.5 1.5 %collective-permute-start.12 = (bf16[512,256]{1,0:T(8,128)(2,1)S(1)}, bf16[512,256]{1,0:T(8,128)(2,1)S(1)}, u32[]{:S(2)}, u32[]{:S(2)}) collective-permute-start(bf16[512,256]{1,0:T(8,128)(2,1)S(1)} %slice.28), channel_id=1, source_target_pairs={{4,0},{8,12},{5,1},{9,13},{6,2},{10,14},{7,3},{11,15},{20,16},{24,... | collective-permute-start | bytes 786440 | tf_op jit(solution)/shard_map/ppermute | solution.py:428
  59.0 3.8 %collective-permute-done.14 = bf16[512,256]{1,0:T(8,128)(2,1)S(1)} collective-permute-done((bf16[512,256]{1,0:T(8,128)(2,1)S(1)}, bf16[512,256]{1,0:T(8,128)(2,1)S(1)}, u32[]{:S(2)}, u32[]{:S(2)}) %collective-permute-start.14) | collective-permute-done | bytes 262176 | tf_op jit(solution)/shard_map/ppermute | solution.py:428
  62.9 0.1 pad_maximum_fusion.attended_ref
  62.9 3.4 %project.1 = (f32[256,1280]{1,0:T(8,128)S(1)}, bf16[512,1280]{1,0:T(8,128)(2,1)S(1)}) custom-call(bf16[2048,256]{1,0:T(8,128)(2,1)S(1)} %pad_maximum_fusion.attended_ref, bf16[2560,1280]{1,0:T(8,128)(2,1)} %weight_hbm.1), custom_call_target="tpu_custom_call" | custom-call | flops 1342177280 | bytes 6553600 | tf_op jit(solution)/shard_map/project/pallas_call | solution.py:313
  66.4 0.0 collective-permute-done.12
  66.4 0.5 finish.1
  67.0 0.1 select_convert_fusion
  67.0 1.6 %collective-permute-start.15 = (bf16[256,640]{1,0:T(8,128)(2,1)S(1)}, bf16[256,640]{1,0:T(8,128)(2,1)S(1)}, u32[]{:S(2)}, u32[]{:S(2)}) collective-permute-start(bf16[256,640]{1,0:T(8,128)(2,1)S(1)} %select_convert_fusion), channel_id=1, source_target_pairs={{0,2},{2,0},{1,3},{3,1},{4,6},{6,4},{5,7},{7,5},{8,10},{10,8},{9,1... | collective-permute-start | bytes 983048 | tf_op jit(solution)/shard_map/ppermute | solution.py:461
  68.6 0.0 copy-done
  68.6 0.4 convolution_reduce_fusion
  69.1 5.1 %collective-permute-done.15 = bf16[256,640]{1,0:T(8,128)(2,1)S(1)} collective-permute-done((bf16[256,640]{1,0:T(8,128)(2,1)S(1)}, bf16[256,640]{1,0:T(8,128)(2,1)S(1)}, u32[]{:S(2)}, u32[]{:S(2)}) %collective-permute-start.15) | collective-permute-done | bytes 327712 | tf_op jit(solution)/shard_map/ppermute | solution.py:461
  74.2 0.8 %multiply_convert_fusion = bf16[256,640]{1,0:T(8,128)(2,1)} fusion(bf16[256,640]{1,0:T(8,128)(2,1)S(1)} %collective-permute-done.15, f32[256,1280]{1,0:T(8,128)S(1)} %finish.1, f32[640]{0:T(1024)S(1)} %broadcast_add_fusion, pred[]{:T(512)S(6)} %eq.20), kind=kLoop, calls=%fused_computation.2 | loop fusion | flops 819200 | bytes 1968641 | tf_op jit(solution)/shard_map/convert_element_type | solution.py:464
  (13 shorter events, 0.3 us)
Async XLA Ops:
  0.0 68.6 %copy-start = (f32[256,640]{1,0:T(8,128)S(1)}, f32[256,640]{1,0:T(8,128)}, u32[]{:S(2)}) copy-start(f32[256,640]{1,0:T(8,128)} %param.21) | copy-start | bytes 1966084
  0.0 5.6 %copy-start.3 = (f32[2560]{0:T(1024)S(1)}, f32[2560]{0:T(1024)}, u32[]{:S(2)}) copy-start(f32[2560]{0:T(1024)} %param.13) | copy-start | bytes 30724
  1.8 4.8 %copy-start.1 = (bf16[256,2560]{1,0:T(8,128)(2,1)}, bf16[256,2560]{1,0:T(8,128)(2,1)S(1)}, u32[]{:S(2)}) copy-start(bf16[256,2560]{1,0:T(8,128)(2,1)S(1)} %get-tuple-element.26.near_hbm) | copy-start | bytes 3932164
  1.8 4.7 %collective-permute-start.1 = (bf16[256,2560]{1,0:T(8,128)(2,1)S(1)}, bf16[256,2560]{1,0:T(8,128)(2,1)S(1)}, u32[]{:S(2)}, u32[]{:S(2)}) collective-permute-start(bf16[256,2560]{1,0:T(8,128)(2,1)S(1)} %get-tuple-element.26.near_hbm), channel_id=1, source_target_pairs={{0,1},{1,0},{2,3},{3,2},{4,5},{5,4},{6,7},{7,6},{8,9},{9,8},{10,11... | collective-permute-start | bytes 3932168 | tf_op jit(solution)/shard_map/ppermute | solution.py:377
  2.4 4.2 %collective-permute-start = (f32[8,256]{1,0:T(8,128)S(1)}, f32[8,256]{1,0:T(8,128)S(1)}, u32[]{:S(2)}, u32[]{:S(2)}) collective-permute-start(f32[8,256]{1,0:T(8,128)S(1)} %get-tuple-element.25.own_sq), channel_id=1, source_target_pairs={{0,2},{2,0},{1,3},{3,1},{4,6},{6,4},{5,7},{7,5},{8,10},{10,8},{9,1... | collective-permute-start | bytes 24584 | tf_op jit(solution)/shard_map/ppermute | solution.py:373
  6.6 3.3 %copy-start.2 = (bf16[256,2560]{1,0:T(8,128)(2,1)}, bf16[256,2560]{1,0:T(8,128)(2,1)S(1)}, u32[]{:S(2)}) copy-start(bf16[256,2560]{1,0:T(8,128)(2,1)S(1)} %collective-permute-done.1.far_hbm) | copy-start | bytes 3932164
  9.9 11.1 %collective-permute-start.2 = (bf16[528,256]{1,0:T(8,128)(2,1)S(1)}, bf16[528,256]{1,0:T(8,128)(2,1)S(1)}, u32[]{:S(2)}, u32[]{:S(2)}) collective-permute-start(bf16[528,256]{1,0:T(8,128)(2,1)S(1)} %attend.5.refs_0_), channel_id=1, source_target_pairs={{0,4},{12,8},{1,5},{13,9},{2,6},{14,10},{3,7},{15,11},{16,20},{28,... | collective-permute-start | bytes 811016 | tf_op jit(solution)/shard_map/ppermute | solution.py:413
  16.8 14.9 %collective-permute-start.4 = (bf16[528,256]{1,0:T(8,128)(2,1)S(1)}, bf16[528,256]{1,0:T(8,128)(2,1)S(1)}, u32[]{:S(2)}, u32[]{:S(2)}) collective-permute-start(bf16[528,256]{1,0:T(8,128)(2,1)S(1)} %attend.6.refs_0_), channel_id=1, source_target_pairs={{0,4},{12,8},{1,5},{13,9},{2,6},{14,10},{3,7},{15,11},{16,20},{28,... | collective-permute-start | bytes 811016 | tf_op jit(solution)/shard_map/ppermute | solution.py:413
  21.1 11.4 %collective-permute-start.3 = (bf16[528,256]{1,0:T(8,128)(2,1)S(1)}, bf16[528,256]{1,0:T(8,128)(2,1)S(1)}, u32[]{:S(2)}, u32[]{:S(2)}) collective-permute-start(bf16[528,256]{1,0:T(8,128)(2,1)S(1)} %merge.10.refs_0_), channel_id=1, source_target_pairs={{4,8},{8,4},{5,9},{9,5},{6,10},{10,6},{7,11},{11,7},{20,24},{24,20... | collective-permute-start | bytes 811016 | tf_op jit(solution)/shard_map/ppermute | solution.py:419
  21.8 14.9 %collective-permute-start.6 = (bf16[528,256]{1,0:T(8,128)(2,1)S(1)}, bf16[528,256]{1,0:T(8,128)(2,1)S(1)}, u32[]{:S(2)}, u32[]{:S(2)}) collective-permute-start(bf16[528,256]{1,0:T(8,128)(2,1)S(1)} %attend.7.refs_0_), channel_id=1, source_target_pairs={{0,4},{12,8},{1,5},{13,9},{2,6},{14,10},{3,7},{15,11},{16,20},{28,... | collective-permute-start | bytes 811016 | tf_op jit(solution)/shard_map/ppermute | solution.py:413
  31.8 5.7 %collective-permute-start.5 = (bf16[528,256]{1,0:T(8,128)(2,1)S(1)}, bf16[528,256]{1,0:T(8,128)(2,1)S(1)}, u32[]{:S(2)}, u32[]{:S(2)}) collective-permute-start(bf16[528,256]{1,0:T(8,128)(2,1)S(1)} %merge.11.refs_0_), channel_id=1, source_target_pairs={{4,8},{8,4},{5,9},{9,5},{6,10},{10,6},{7,11},{11,7},{20,24},{24,20... | collective-permute-start | bytes 811016 | tf_op jit(solution)/shard_map/ppermute | solution.py:419
  32.7 8.9 %collective-permute-start.9 = (bf16[528,256]{1,0:T(8,128)(2,1)S(1)}, bf16[528,256]{1,0:T(8,128)(2,1)S(1)}, u32[]{:S(2)}, u32[]{:S(2)}) collective-permute-start(bf16[528,256]{1,0:T(8,128)(2,1)S(1)} %broadcast_select_fusion.1), channel_id=1, source_target_pairs={{0,4},{12,8},{4,0},{8,12},{1,5},{13,9},{5,1},{9,13},{2,6},{14,10},... | collective-permute-start | bytes 811016 | tf_op jit(solution)/shard_map/ppermute | solution.py:438
  36.8 5.6 %collective-permute-start.8 = (bf16[528,256]{1,0:T(8,128)(2,1)S(1)}, bf16[528,256]{1,0:T(8,128)(2,1)S(1)}, u32[]{:S(2)}, u32[]{:S(2)}) collective-permute-start(bf16[528,256]{1,0:T(8,128)(2,1)S(1)} %merge.13.refs_0_), channel_id=1, source_target_pairs={{4,8},{8,4},{5,9},{9,5},{6,10},{10,6},{7,11},{11,7},{20,24},{24,20... | collective-permute-start | bytes 811016 | tf_op jit(solution)/shard_map/ppermute | solution.py:419
  37.7 8.0 %collective-permute-start.7 = (bf16[528,256]{1,0:T(8,128)(2,1)S(1)}, bf16[528,256]{1,0:T(8,128)(2,1)S(1)}, u32[]{:S(2)}, u32[]{:S(2)}) collective-permute-start(bf16[528,256]{1,0:T(8,128)(2,1)S(1)} %broadcast_select_fusion), channel_id=1, source_target_pairs={{0,4},{12,8},{4,0},{8,12},{1,5},{13,9},{5,1},{9,13},{2,6},{14,10},... | collective-permute-start | bytes 811016 | tf_op jit(solution)/shard_map/ppermute | solution.py:438
  41.7 4.9 %collective-permute-start.11 = (bf16[528,256]{1,0:T(8,128)(2,1)S(1)}, bf16[528,256]{1,0:T(8,128)(2,1)S(1)}, u32[]{:S(2)}, u32[]{:S(2)}) collective-permute-start(bf16[528,256]{1,0:T(8,128)(2,1)S(1)} %merge.15.refs_0_), channel_id=1, source_target_pairs={{4,8},{8,4},{5,9},{9,5},{6,10},{10,6},{7,11},{11,7},{20,24},{24,20... | collective-permute-start | bytes 811016 | tf_op jit(solution)/shard_map/ppermute | solution.py:419
  42.6 14.7 %collective-permute-start.13 = (bf16[512,256]{1,0:T(8,128)(2,1)S(1)}, bf16[512,256]{1,0:T(8,128)(2,1)S(1)}, u32[]{:S(2)}, u32[]{:S(2)}) collective-permute-start(bf16[512,256]{1,0:T(8,128)(2,1)S(1)} %slice.33), channel_id=1, source_target_pairs={{4,0},{8,12},{5,1},{9,13},{6,2},{10,14},{7,3},{11,15},{20,16},{24,... | collective-permute-start | bytes 786440 | tf_op jit(solution)/shard_map/ppermute | solution.py:428
  45.9 11.5 %collective-permute-start.10 = (bf16[528,256]{1,0:T(8,128)(2,1)S(1)}, bf16[528,256]{1,0:T(8,128)(2,1)S(1)}, u32[]{:S(2)}, u32[]{:S(2)}) collective-permute-start(bf16[528,256]{1,0:T(8,128)(2,1)S(1)} %merge.17.refs_0_), channel_id=1, source_target_pairs={{4,8},{8,4},{5,9},{9,5},{6,10},{10,6},{7,11},{11,7},{20,24},{24,20... | collective-permute-start | bytes 811016 | tf_op jit(solution)/shard_map/ppermute | solution.py:419
  46.8 16.1 %collective-permute-start.14 = (bf16[512,256]{1,0:T(8,128)(2,1)S(1)}, bf16[512,256]{1,0:T(8,128)(2,1)S(1)}, u32[]{:S(2)}, u32[]{:S(2)}) collective-permute-start(bf16[512,256]{1,0:T(8,128)(2,1)S(1)} %slice.34), channel_id=1, source_target_pairs={{4,0},{8,12},{5,1},{9,13},{6,2},{10,14},{7,3},{11,15},{20,16},{24,... | collective-permute-start | bytes 786440 | tf_op jit(solution)/shard_map/ppermute | solution.py:428
  57.5 8.8 %collective-permute-start.12 = (bf16[512,256]{1,0:T(8,128)(2,1)S(1)}, bf16[512,256]{1,0:T(8,128)(2,1)S(1)}, u32[]{:S(2)}, u32[]{:S(2)}) collective-permute-start(bf16[512,256]{1,0:T(8,128)(2,1)S(1)} %slice.28), channel_id=1, source_target_pairs={{4,0},{8,12},{5,1},{9,13},{6,2},{10,14},{7,3},{11,15},{20,16},{24,... | collective-permute-start | bytes 786440 | tf_op jit(solution)/shard_map/ppermute | solution.py:428
  67.0 7.1 %collective-permute-start.15 = (bf16[256,640]{1,0:T(8,128)(2,1)S(1)}, bf16[256,640]{1,0:T(8,128)(2,1)S(1)}, u32[]{:S(2)}, u32[]{:S(2)}) collective-permute-start(bf16[256,640]{1,0:T(8,128)(2,1)S(1)} %select_convert_fusion), channel_id=1, source_target_pairs={{0,2},{2,0},{1,3},{3,1},{4,6},{6,4},{5,7},{7,5},{8,10},{10,8},{9,1... | collective-permute-start | bytes 983048 | tf_op jit(solution)/shard_map/ppermute | solution.py:461

commit v5 on v4

--- a/solution.py
+++ b/solution.py
@@ -19,7 +19,10 @@
 
 def chunk_sizes(heads):
     count = -(-heads // 4) if heads > 4 else 2
-    return [heads // count + (c < heads % count) for c in range(count)]
+    sizes = [heads // count + (c < heads % count) for c in range(count)]
+    if count > 3:
+        sizes[0], sizes[1] = sizes[0] - 1, sizes[1] + 1
+    return sizes
 
 
 def order_of(sizes):
@@ -31,7 +34,7 @@
     steps = [(kind, c) for c in range(3) for kind in "AI"] + [("F", 0)]
     for c in range(3, count):
         steps += [("A", c), ("F", c - 2), ("C", c - 3)]
-        steps += [("X", c)] if sizes[c] == sizes[c - 3] else [("I", c), ("O", c - 3)]
+        steps += [("X", c)]
     for c in range(max(count - 3, 0), count):
         if c + 1 < count:
             steps += [("F", c + 1)]
@@ -280,14 +283,13 @@
     )(*guard, own, got)
 
 
-def project_kernel(parts, attended_ref, weight_hbm, sum_ref, later_ref, turned, weight, sems):
+def project_kernel(bounds, attended_ref, weight_hbm, sum_ref, later_ref, turned, weight, sems):
     depth, cols = attended_ref.shape[0], sum_ref.shape[1]
-    step = depth // parts
+    parts = len(bounds) - 1
+    spans = [slice(low, high) for low, high in zip(bounds[:-1], bounds[1:])]
     copies = [
-        pltpu.make_async_copy(
-            weight_hbm.at[pl.ds(n * step, step), :], weight.at[pl.ds(n * step, step), :], sems.at[n]
-        )
-        for n in range(parts)
+        pltpu.make_async_copy(weight_hbm.at[span, :], weight.at[span, :], sems.at[n])
+        for n, span in enumerate(spans)
     ]
     copies.append(
         pltpu.make_async_copy(
@@ -299,7 +301,7 @@
     turned[...] = attended_ref[...].T
     for n in range(parts):
         copies[n].wait()
-        span = slice(n * step, (n + 1) * step)
+        span = spans[n]
         for low in range(0, cols, 256):
             tile = slice(low, min(low + 256, cols))
             term = jnp.dot(turned[:, span], weight[span, tile], preferred_element_type=F32)
@@ -307,11 +309,11 @@
     copies[parts].wait()
 
 
-def project(parts, attended, weight):
+def project(bounds, attended, weight):
     depth, rows = attended.shape
     cols = weight.shape[1]
     return pl.pallas_call(
-        functools.partial(project_kernel, parts),
+        functools.partial(project_kernel, bounds),
         out_shape=(
             jax.ShapeDtypeStruct((rows, cols), F32),
             jax.ShapeDtypeStruct((weight.shape[0] - depth, cols), BF16),
@@ -321,7 +323,7 @@
         scratch_shapes=[
             pltpu.VMEM((rows, depth), BF16),
             pltpu.VMEM((depth, cols), BF16),
-            pltpu.SemaphoreType.DMA((parts + 1,)),
+            pltpu.SemaphoreType.DMA((len(bounds),)),
         ],
         cost_estimate=pl.CostEstimate(
             flops=2 * depth * rows * cols, bytes_accessed=2 * weight.size, transcendentals=0
@@ -434,16 +436,21 @@
             send_in(c)
             send_out(c - 3)
             return
-        sent = run(jnp.where(outer, own[c], total[c - 3]))
+        rows = max(own[c].shape[0], total[c - 3].shape[0])
+        going, coming = (
+            jnp.pad(m, ((0, rows - m.shape[0]), (0, 0))) for m in (own[c], total[c - 3])
+        )
+        sent = run(jnp.where(outer, going, coming))
         got = lax.ppermute(sent, "slab", inward[0] + outward[0])
-        got_in[c] = got
+        got_in[c] = got[: own[c].shape[0]]
         final[c - 3] = jnp.where(outer, got, sent)[: sizes[c - 3] * HD]
 
     steps = {"A": attention, "I": send_in, "F": fold, "C": cross, "O": send_out, "X": send_both}
     for kind, c in order_of(sizes):
         steps[kind](c)
     early = jnp.concatenate([final[c] for c in range(count - 1)], axis=0)
-    projected, later = project(count - 1, in_order(early, *last), out_weight)
+    bounds = tuple(start * HD for start in starts)
+    projected, later = project(bounds, in_order(early, *last), out_weight)
     projected = finish(in_order(final[count - 1], projected), later, projected)
 
     half = time_weight.shape[0] // 2

time: 75.5 us -> 77.1 us (1.021)
  waiting for transfers between devices: 20.4 us -> 21.9 us
    ppermute x3, starting transfers between devices: 12.3 us -> 9.42 us  [send_in(): lax.ppermute(sent, 'slab', inward[side - 2])]
    ppermute x2, starting transfers between devices: 4.26 us -> 6.71 us  [send_both(): got = lax.ppermute(sent, 'slab', inward[0] + outward[0])]
    ppermute x2, waiting for transfers between devices: 1.84 us -> 2.83 us  [send_both(): got = lax.ppermute(sent, 'slab', inward[0] + outward[0])]
  transfers between devices with their start and end apart: 16 -> 16, of which waited for: 5 -> 6; matrix products, arithmetic and copies ran while one was open for 2% -> 2% of each run, Pallas kernels for 22% -> 22%
where the time goes in v5:
time: 77.1 us; the launch traced here: 76.6 us
  starting transfers between devices  28.3 us (37%)
  Pallas kernels  22.2 us (29%)
  waiting for transfers between devices  21.9 us (28%)
  between operations  1.74 us (2%)
  other arithmetic  1.35 us (2%)
    pallas_call x5, Pallas kernels, attend(): pl.pallas_call(functools.partial(attend_kernel, start, heads, width), out...  14.8 us
    ppermute x3, waiting for transfers between devices, send_out(): got = lax.ppermute(attended, 'slab', outward[j])  13.6 us
    ppermute x3, starting transfers between devices, send_in(): lax.ppermute(sent, 'slab', inward[side - 2])  9.42 us
    ppermute x2, starting transfers between devices, send_both(): got = lax.ppermute(sent, 'slab', inward[0] + outward[0])  6.71 us
    ppermute x1, waiting for transfers between devices, local(): summed = kept + lax.ppermute(sent, 'head', [(0, 1), (1, 0)]).astype(F32)  5.1 us
    ppermute x3, starting transfers between devices, send_out(): got = lax.ppermute(attended, 'slab', outward[j])  4.06 us
    pallas_call x1, Pallas kernels, project(): pl.pallas_call(functools.partial(project_kernel, bounds), out_shape=(jax....  3.7 us
    ppermute x5, starting transfers between devices, fold(): lax.ppermute(folded[c], 'slab', [(side - 1, side), (side, side - 1)])  3.39 us
  transfers between devices with their start and end apart: 16, of which 6 were waited for; matrix products, arithmetic and copies ran while one was open for 2% of the time, Pallas kernels for 22%

profile of v5, /device:TPU:0, one launch (start us, length us, event | category | flops | bytes accessed | tf_op | source)
XLA Modules:
  0.0 76.6 jit_solution(15762002550883881521)
XLA Ops:
  0.0 0.0 copy-start
  0.0 1.8 %prepare.1 = (f32[8,256]{1,0:T(8,128)S(1)}, bf16[256,2560]{1,0:T(8,128)(2,1)S(1)}) custom-call(bf16[256,2560]{1,0:T(8,128)(2,1)} %q_hbm.11, bf16[64,2560]{1,0:T(8,128)(2,1)} %fk.1, bf16[64,2560]{1,0:T(8,128)(2,1)} %nk.1, bf16[64,2560]{1,0:T(8,128)(2,1)} %fv.1, bf16[64,2560]{1,0:T(8,128)(2,1)} %nv.1), custom_call_target="tpu_custom_call" | custom-call | flops 1310720 | bytes 5242880 | tf_op jit(solution)/shard_map/prepare/pallas_call | solution.py:94
  1.8 0.0 copy-start.1
  1.8 0.6 collective-permute-start.1
  2.4 2.6 %collective-permute-start = (f32[8,256]{1,0:T(8,128)S(1)}, f32[8,256]{1,0:T(8,128)S(1)}, u32[]{:S(2)}, u32[]{:S(2)}) collective-permute-start(f32[8,256]{1,0:T(8,128)S(1)} %get-tuple-element.25.own_sq), channel_id=1, source_target_pairs={{0,2},{2,0},{1,3},{3,1},{4,6},{6,4},{5,7},{7,5},{8,10},{10,8},{9,1... | collective-permute-start | bytes 24584 | tf_op jit(solution)/shard_map/ppermute | solution.py:375
  5.6 0.0 copy-done.3
  5.6 0.6 broadcast_in_dim.4.gain_hbm
  6.2 0.4 collective-permute-done.far_sq
  6.6 0.0 collective-permute-done.1.far_hbm
  6.6 0.0 copy-done.1
  6.6 2.9 %attend.5.refs_0_ = bf16[400,256]{1,0:T(8,128)(2,1)S(1)} custom-call(s32[1]{0:T(128)S(6)} %convert_element_type.24.owner_ref, f32[8,256]{1,0:T(8,128)S(1)} %get-tuple-element.25.own_sq, f32[8,256]{1,0:T(8,128)S(1)} %collective-permute-done.far_sq, f32[1,2560]{1,0:T(1,128)} %broadcast_in_dim.4.gain_hbm, bf16[256,2560]{1,0:T(8,128)(2,1)} %q_hbm.11, ...), custom_call_target="tpu_custom_call" | custom-call | flops 1207959552 | bytes 1179648 | tf_op jit(solution)/shard_map/attend/pallas_call | solution.py:228
  9.5 0.0 copy-done.2
  9.5 4.0 %collective-permute-start.2 = (bf16[400,256]{1,0:T(8,128)(2,1)S(1)}, bf16[400,256]{1,0:T(8,128)(2,1)S(1)}, u32[]{:S(2)}, u32[]{:S(2)}) collective-permute-start(bf16[400,256]{1,0:T(8,128)(2,1)S(1)} %attend.5.refs_0_), channel_id=1, source_target_pairs={{0,4},{12,8},{1,5},{13,9},{2,6},{14,10},{3,7},{15,11},{16,20},{28,... | collective-permute-start | bytes 614408 | tf_op jit(solution)/shard_map/ppermute | solution.py:415
  13.6 3.3 %attend.6.refs_0_ = bf16[656,256]{1,0:T(8,128)(2,1)S(1)} custom-call(s32[1]{0:T(128)S(6)} %convert_element_type.24.owner_ref, f32[8,256]{1,0:T(8,128)S(1)} %get-tuple-element.25.own_sq, f32[8,256]{1,0:T(8,128)S(1)} %collective-permute-done.far_sq, f32[1,2560]{1,0:T(1,128)} %broadcast_in_dim.4.gain_hbm, bf16[256,2560]{1,0:T(8,128)(2,1)} %q_hbm.11, ...), custom_call_target="tpu_custom_call" | custom-call | flops 2013265920 | bytes 1966080 | tf_op jit(solution)/shard_map/attend/pallas_call | solution.py:228
  16.8 1.3 %collective-permute-start.4 = (bf16[656,256]{1,0:T(8,128)(2,1)S(1)}, bf16[656,256]{1,0:T(8,128)(2,1)S(1)}, u32[]{:S(2)}, u32[]{:S(2)}) collective-permute-start(bf16[656,256]{1,0:T(8,128)(2,1)S(1)} %attend.6.refs_0_), channel_id=1, source_target_pairs={{0,4},{12,8},{1,5},{13,9},{2,6},{14,10},{3,7},{15,11},{16,20},{28,... | collective-permute-start | bytes 1007624 | tf_op jit(solution)/shard_map/ppermute | solution.py:415
  18.1 2.9 %attend.7.refs_0_ = bf16[528,256]{1,0:T(8,128)(2,1)S(1)} custom-call(s32[1]{0:T(128)S(6)} %convert_element_type.24.owner_ref, f32[8,256]{1,0:T(8,128)S(1)} %get-tuple-element.25.own_sq, f32[8,256]{1,0:T(8,128)S(1)} %collective-permute-done.far_sq, f32[1,2560]{1,0:T(1,128)} %broadcast_in_dim.4.gain_hbm, bf16[256,2560]{1,0:T(8,128)(2,1)} %q_hbm.11, ...), custom_call_target="tpu_custom_call" | custom-call | flops 1610612736 | bytes 1572864 | tf_op jit(solution)/shard_map/attend/pallas_call | solution.py:228
  21.0 0.0 collective-permute-done.2.refs_1_
  21.0 0.1 merge.10.refs_0_
  21.2 0.7 collective-permute-start.3
  22.5 4.1 %collective-permute-start.6 = (bf16[528,256]{1,0:T(8,128)(2,1)S(1)}, bf16[528,256]{1,0:T(8,128)(2,1)S(1)}, u32[]{:S(2)}, u32[]{:S(2)}) collective-permute-start(bf16[528,256]{1,0:T(8,128)(2,1)S(1)} %attend.7.refs_0_), channel_id=1, source_target_pairs={{0,4},{12,8},{1,5},{13,9},{2,6},{14,10},{3,7},{15,11},{16,20},{28,... | collective-permute-start | bytes 811016 | tf_op jit(solution)/shard_map/ppermute | solution.py:415
  26.6 2.9 %attend.8.refs_0_ = bf16[528,256]{1,0:T(8,128)(2,1)S(1)} custom-call(s32[1]{0:T(128)S(6)} %convert_element_type.24.owner_ref, f32[8,256]{1,0:T(8,128)S(1)} %get-tuple-element.25.own_sq, f32[8,256]{1,0:T(8,128)S(1)} %collective-permute-done.far_sq, f32[1,2560]{1,0:T(1,128)} %broadcast_in_dim.4.gain_hbm, bf16[256,2560]{1,0:T(8,128)(2,1)} %q_hbm.11, ...), custom_call_target="tpu_custom_call" | custom-call | flops 1610612736 | bytes 1572864 | tf_op jit(solution)/shard_map/attend/pallas_call | solution.py:228
  29.5 0.0 collective-permute-done.4.refs_1_
  29.5 0.2 merge.11.refs_0_
  29.6 0.7 collective-permute-start.5
  30.3 0.0 collective-permute-done.3.refs_1_
  30.3 0.1 merge.12
  30.5 0.1 pad_select_fusion.1
  30.5 1.1 %collective-permute-start.9 = (bf16[528,256]{1,0:T(8,128)(2,1)S(1)}, bf16[528,256]{1,0:T(8,128)(2,1)S(1)}, u32[]{:S(2)}, u32[]{:S(2)}) collective-permute-start(bf16[528,256]{1,0:T(8,128)(2,1)S(1)} %pad_select_fusion.1), channel_id=1, source_target_pairs={{0,4},{12,8},{4,0},{8,12},{1,5},{13,9},{5,1},{9,13},{2,6},{14,10},... | collective-permute-start | bytes 811016 | tf_op jit(solution)/shard_map/ppermute | solution.py:444
  31.6 2.9 %attend.9.refs_0_ = bf16[528,256]{1,0:T(8,128)(2,1)S(1)} custom-call(s32[1]{0:T(128)S(6)} %convert_element_type.24.owner_ref, f32[8,256]{1,0:T(8,128)S(1)} %get-tuple-element.25.own_sq, f32[8,256]{1,0:T(8,128)S(1)} %collective-permute-done.far_sq, f32[1,2560]{1,0:T(1,128)} %broadcast_in_dim.4.gain_hbm, bf16[256,2560]{1,0:T(8,128)(2,1)} %q_hbm.11, ...), custom_call_target="tpu_custom_call" | custom-call | flops 1610612736 | bytes 1572864 | tf_op jit(solution)/shard_map/attend/pallas_call | solution.py:228
  34.5 0.0 collective-permute-done.6.refs_1_
  34.5 0.1 merge.13.refs_0_
  34.7 0.7 collective-permute-start.8
  35.3 0.1 fusion
  35.4 0.0 collective-permute-done.5.refs_1_
  35.4 0.2 merge.14
  35.6 0.1 pad_select_fusion
  35.7 5.6 %collective-permute-start.7 = (bf16[656,256]{1,0:T(8,128)(2,1)S(1)}, bf16[656,256]{1,0:T(8,128)(2,1)S(1)}, u32[]{:S(2)}, u32[]{:S(2)}) collective-permute-start(bf16[656,256]{1,0:T(8,128)(2,1)S(1)} %pad_select_fusion), channel_id=1, source_target_pairs={{0,4},{12,8},{4,0},{8,12},{1,5},{13,9},{5,1},{9,13},{2,6},{14,10},... | collective-permute-start | bytes 1007624 | tf_op jit(solution)/shard_map/ppermute | solution.py:444
  41.3 0.0 collective-permute-done.9.refs_1_
  41.3 0.1 merge.15.refs_0_
  41.4 0.7 collective-permute-start.11
  42.1 0.0 collective-permute-done.8.refs_1_
  42.1 0.1 merge.16
  42.3 1.3 %collective-permute-start.13 = (bf16[512,256]{1,0:T(8,128)(2,1)S(1)}, bf16[512,256]{1,0:T(8,128)(2,1)S(1)}, u32[]{:S(2)}, u32[]{:S(2)}) collective-permute-start(bf16[512,256]{1,0:T(8,128)(2,1)S(1)} %slice.38), channel_id=1, source_target_pairs={{4,0},{8,12},{5,1},{9,13},{6,2},{10,14},{7,3},{11,15},{20,16},{24,... | collective-permute-start | bytes 786440 | tf_op jit(solution)/shard_map/ppermute | solution.py:430
  43.6 2.8 %collective-permute-done.7 = bf16[656,256]{1,0:T(8,128)(2,1)S(1)} collective-permute-done((bf16[656,256]{1,0:T(8,128)(2,1)S(1)}, bf16[656,256]{1,0:T(8,128)(2,1)S(1)}, u32[]{:S(2)}, u32[]{:S(2)}) %collective-permute-start.7) | collective-permute-done | bytes 335904 | tf_op jit(solution)/shard_map/ppermute | solution.py:444
  46.5 0.1 merge.17.refs_0_
  46.6 0.0 collective-permute-done.11.refs_1_
  46.6 0.1 merge.18
  46.8 1.3 %collective-permute-start.14 = (bf16[512,256]{1,0:T(8,128)(2,1)S(1)}, bf16[512,256]{1,0:T(8,128)(2,1)S(1)}, u32[]{:S(2)}, u32[]{:S(2)}) collective-permute-start(bf16[512,256]{1,0:T(8,128)(2,1)S(1)} %slice.39), channel_id=1, source_target_pairs={{4,0},{8,12},{5,1},{9,13},{6,2},{10,14},{7,3},{11,15},{20,16},{24,... | collective-permute-start | bytes 786440 | tf_op jit(solution)/shard_map/ppermute | solution.py:430
  48.1 4.7 %collective-permute-done.13 = bf16[512,256]{1,0:T(8,128)(2,1)S(1)} collective-permute-done((bf16[512,256]{1,0:T(8,128)(2,1)S(1)}, bf16[512,256]{1,0:T(8,128)(2,1)S(1)}, u32[]{:S(2)}, u32[]{:S(2)}) %collective-permute-start.13) | collective-permute-done | bytes 262176 | tf_op jit(solution)/shard_map/ppermute | solution.py:430
  52.9 0.7 collective-permute-start.10
  53.6 4.7 %collective-permute-done.14 = bf16[512,256]{1,0:T(8,128)(2,1)S(1)} collective-permute-done((bf16[512,256]{1,0:T(8,128)(2,1)S(1)}, bf16[512,256]{1,0:T(8,128)(2,1)S(1)}, u32[]{:S(2)}, u32[]{:S(2)}) %collective-permute-start.14) | collective-permute-done | bytes 262176 | tf_op jit(solution)/shard_map/ppermute | solution.py:430
  58.3 0.0 collective-permute-done.10.refs_1_
  58.3 0.1 merge.19
  58.5 1.5 %collective-permute-start.12 = (bf16[512,256]{1,0:T(8,128)(2,1)S(1)}, bf16[512,256]{1,0:T(8,128)(2,1)S(1)}, u32[]{:S(2)}, u32[]{:S(2)}) collective-permute-start(bf16[512,256]{1,0:T(8,128)(2,1)S(1)} %slice.33), channel_id=1, source_target_pairs={{4,0},{8,12},{5,1},{9,13},{6,2},{10,14},{7,3},{11,15},{20,16},{24,... | collective-permute-start | bytes 786440 | tf_op jit(solution)/shard_map/ppermute | solution.py:430
  60.0 0.1 pad_maximum_fusion.attended_ref
  60.1 3.7 %project.1 = (f32[256,1280]{1,0:T(8,128)S(1)}, bf16[512,1280]{1,0:T(8,128)(2,1)S(1)}) custom-call(bf16[2048,256]{1,0:T(8,128)(2,1)S(1)} %pad_maximum_fusion.attended_ref, bf16[2560,1280]{1,0:T(8,128)(2,1)} %weight_hbm.1), custom_call_target="tpu_custom_call" | custom-call | flops 1342177280 | bytes 6553600 | tf_op jit(solution)/shard_map/project/pallas_call | solution.py:315
  63.8 4.2 %collective-permute-done.12 = bf16[512,256]{1,0:T(8,128)(2,1)S(1)} collective-permute-done((bf16[512,256]{1,0:T(8,128)(2,1)S(1)}, bf16[512,256]{1,0:T(8,128)(2,1)S(1)}, u32[]{:S(2)}, u32[]{:S(2)}) %collective-permute-start.12) | collective-permute-done | bytes 262176 | tf_op jit(solution)/shard_map/ppermute | solution.py:430
  68.0 0.5 finish.1
  68.5 0.1 select_convert_fusion
  68.6 1.6 %collective-permute-start.15 = (bf16[256,640]{1,0:T(8,128)(2,1)S(1)}, bf16[256,640]{1,0:T(8,128)(2,1)S(1)}, u32[]{:S(2)}, u32[]{:S(2)}) collective-permute-start(bf16[256,640]{1,0:T(8,128)(2,1)S(1)} %select_convert_fusion), channel_id=1, source_target_pairs={{0,2},{2,0},{1,3},{3,1},{4,6},{6,4},{5,7},{7,5},{8,10},{10,8},{9,1... | collective-permute-start | bytes 983048 | tf_op jit(solution)/shard_map/ppermute | solution.py:468
  70.2 0.0 copy-done
  70.2 0.4 convolution_reduce_fusion
  70.6 5.1 %collective-permute-done.15 = bf16[256,640]{1,0:T(8,128)(2,1)S(1)} collective-permute-done((bf16[256,640]{1,0:T(8,128)(2,1)S(1)}, bf16[256,640]{1,0:T(8,128)(2,1)S(1)}, u32[]{:S(2)}, u32[]{:S(2)}) %collective-permute-start.15) | collective-permute-done | bytes 327712 | tf_op jit(solution)/shard_map/ppermute | solution.py:468
  75.7 0.8 %multiply_convert_fusion = bf16[256,640]{1,0:T(8,128)(2,1)} fusion(bf16[256,640]{1,0:T(8,128)(2,1)S(1)} %collective-permute-done.15, f32[256,1280]{1,0:T(8,128)S(1)} %finish.1, f32[640]{0:T(1024)S(1)} %broadcast_add_fusion, pred[]{:T(512)S(6)} %eq.20), kind=kLoop, calls=%fused_computation.2 | loop fusion | flops 819200 | bytes 1968641 | tf_op jit(solution)/shard_map/convert_element_type | solution.py:471
  (13 shorter events, 0.3 us)
Async XLA Ops:
  0.0 70.2 %copy-start = (f32[256,640]{1,0:T(8,128)S(1)}, f32[256,640]{1,0:T(8,128)}, u32[]{:S(2)}) copy-start(f32[256,640]{1,0:T(8,128)} %param.21) | copy-start | bytes 1966084
  0.0 5.6 %copy-start.3 = (f32[2560]{0:T(1024)S(1)}, f32[2560]{0:T(1024)}, u32[]{:S(2)}) copy-start(f32[2560]{0:T(1024)} %param.13) | copy-start | bytes 30724
  1.8 4.8 %copy-start.1 = (bf16[256,2560]{1,0:T(8,128)(2,1)}, bf16[256,2560]{1,0:T(8,128)(2,1)S(1)}, u32[]{:S(2)}) copy-start(bf16[256,2560]{1,0:T(8,128)(2,1)S(1)} %get-tuple-element.26.near_hbm) | copy-start | bytes 3932164
  1.8 4.7 %collective-permute-start.1 = (bf16[256,2560]{1,0:T(8,128)(2,1)S(1)}, bf16[256,2560]{1,0:T(8,128)(2,1)S(1)}, u32[]{:S(2)}, u32[]{:S(2)}) collective-permute-start(bf16[256,2560]{1,0:T(8,128)(2,1)S(1)} %get-tuple-element.26.near_hbm), channel_id=1, source_target_pairs={{0,1},{1,0},{2,3},{3,2},{4,5},{5,4},{6,7},{7,6},{8,9},{9,8},{10,11... | collective-permute-start | bytes 3932168 | tf_op jit(solution)/shard_map/ppermute | solution.py:379
  2.4 4.2 %collective-permute-start = (f32[8,256]{1,0:T(8,128)S(1)}, f32[8,256]{1,0:T(8,128)S(1)}, u32[]{:S(2)}, u32[]{:S(2)}) collective-permute-start(f32[8,256]{1,0:T(8,128)S(1)} %get-tuple-element.25.own_sq), channel_id=1, source_target_pairs={{0,2},{2,0},{1,3},{3,1},{4,6},{6,4},{5,7},{7,5},{8,10},{10,8},{9,1... | collective-permute-start | bytes 24584 | tf_op jit(solution)/shard_map/ppermute | solution.py:375
  6.6 2.9 %copy-start.2 = (bf16[256,2560]{1,0:T(8,128)(2,1)}, bf16[256,2560]{1,0:T(8,128)(2,1)S(1)}, u32[]{:S(2)}) copy-start(bf16[256,2560]{1,0:T(8,128)(2,1)S(1)} %collective-permute-done.1.far_hbm) | copy-start | bytes 3932164
  9.5 11.5 %collective-permute-start.2 = (bf16[400,256]{1,0:T(8,128)(2,1)S(1)}, bf16[400,256]{1,0:T(8,128)(2,1)S(1)}, u32[]{:S(2)}, u32[]{:S(2)}) collective-permute-start(bf16[400,256]{1,0:T(8,128)(2,1)S(1)} %attend.5.refs_0_), channel_id=1, source_target_pairs={{0,4},{12,8},{1,5},{13,9},{2,6},{14,10},{3,7},{15,11},{16,20},{28,... | collective-permute-start | bytes 614408 | tf_op jit(solution)/shard_map/ppermute | solution.py:415
  16.8 12.6 %collective-permute-start.4 = (bf16[656,256]{1,0:T(8,128)(2,1)S(1)}, bf16[656,256]{1,0:T(8,128)(2,1)S(1)}, u32[]{:S(2)}, u32[]{:S(2)}) collective-permute-start(bf16[656,256]{1,0:T(8,128)(2,1)S(1)} %attend.6.refs_0_), channel_id=1, source_target_pairs={{0,4},{12,8},{1,5},{13,9},{2,6},{14,10},{3,7},{15,11},{16,20},{28,... | collective-permute-start | bytes 1007624 | tf_op jit(solution)/shard_map/ppermute | solution.py:415
  21.2 9.2 %collective-permute-start.3 = (bf16[400,256]{1,0:T(8,128)(2,1)S(1)}, bf16[400,256]{1,0:T(8,128)(2,1)S(1)}, u32[]{:S(2)}, u32[]{:S(2)}) collective-permute-start(bf16[400,256]{1,0:T(8,128)(2,1)S(1)} %merge.10.refs_0_), channel_id=1, source_target_pairs={{4,8},{8,4},{5,9},{9,5},{6,10},{10,6},{7,11},{11,7},{20,24},{24,20... | collective-permute-start | bytes 614408 | tf_op jit(solution)/shard_map/ppermute | solution.py:421
  22.5 12.0 %collective-permute-start.6 = (bf16[528,256]{1,0:T(8,128)(2,1)S(1)}, bf16[528,256]{1,0:T(8,128)(2,1)S(1)}, u32[]{:S(2)}, u32[]{:S(2)}) collective-permute-start(bf16[528,256]{1,0:T(8,128)(2,1)S(1)} %attend.7.refs_0_), channel_id=1, source_target_pairs={{0,4},{12,8},{1,5},{13,9},{2,6},{14,10},{3,7},{15,11},{16,20},{28,... | collective-permute-start | bytes 811016 | tf_op jit(solution)/shard_map/ppermute | solution.py:415
  29.6 5.8 %collective-permute-start.5 = (bf16[656,256]{1,0:T(8,128)(2,1)S(1)}, bf16[656,256]{1,0:T(8,128)(2,1)S(1)}, u32[]{:S(2)}, u32[]{:S(2)}) collective-permute-start(bf16[656,256]{1,0:T(8,128)(2,1)S(1)} %merge.11.refs_0_), channel_id=1, source_target_pairs={{4,8},{8,4},{5,9},{9,5},{6,10},{10,6},{7,11},{11,7},{20,24},{24,20... | collective-permute-start | bytes 1007624 | tf_op jit(solution)/shard_map/ppermute | solution.py:421
  30.5 10.7 %collective-permute-start.9 = (bf16[528,256]{1,0:T(8,128)(2,1)S(1)}, bf16[528,256]{1,0:T(8,128)(2,1)S(1)}, u32[]{:S(2)}, u32[]{:S(2)}) collective-permute-start(bf16[528,256]{1,0:T(8,128)(2,1)S(1)} %pad_select_fusion.1), channel_id=1, source_target_pairs={{0,4},{12,8},{4,0},{8,12},{1,5},{13,9},{5,1},{9,13},{2,6},{14,10},... | collective-permute-start | bytes 811016 | tf_op jit(solution)/shard_map/ppermute | solution.py:444
  34.7 7.4 %collective-permute-start.8 = (bf16[528,256]{1,0:T(8,128)(2,1)S(1)}, bf16[528,256]{1,0:T(8,128)(2,1)S(1)}, u32[]{:S(2)}, u32[]{:S(2)}) collective-permute-start(bf16[528,256]{1,0:T(8,128)(2,1)S(1)} %merge.13.refs_0_), channel_id=1, source_target_pairs={{4,8},{8,4},{5,9},{9,5},{6,10},{10,6},{7,11},{11,7},{20,24},{24,20... | collective-permute-start | bytes 811016 | tf_op jit(solution)/shard_map/ppermute | solution.py:421
  35.7 10.8 %collective-permute-start.7 = (bf16[656,256]{1,0:T(8,128)(2,1)S(1)}, bf16[656,256]{1,0:T(8,128)(2,1)S(1)}, u32[]{:S(2)}, u32[]{:S(2)}) collective-permute-start(bf16[656,256]{1,0:T(8,128)(2,1)S(1)} %pad_select_fusion), channel_id=1, source_target_pairs={{0,4},{12,8},{4,0},{8,12},{1,5},{13,9},{5,1},{9,13},{2,6},{14,10},... | collective-permute-start | bytes 1007624 | tf_op jit(solution)/shard_map/ppermute | solution.py:444
  41.4 5.2 %collective-permute-start.11 = (bf16[528,256]{1,0:T(8,128)(2,1)S(1)}, bf16[528,256]{1,0:T(8,128)(2,1)S(1)}, u32[]{:S(2)}, u32[]{:S(2)}) collective-permute-start(bf16[528,256]{1,0:T(8,128)(2,1)S(1)} %merge.15.refs_0_), channel_id=1, source_target_pairs={{4,8},{8,4},{5,9},{9,5},{6,10},{10,6},{7,11},{11,7},{20,24},{24,20... | collective-permute-start | bytes 811016 | tf_op jit(solution)/shard_map/ppermute | solution.py:421
  42.3 10.5 %collective-permute-start.13 = (bf16[512,256]{1,0:T(8,128)(2,1)S(1)}, bf16[512,256]{1,0:T(8,128)(2,1)S(1)}, u32[]{:S(2)}, u32[]{:S(2)}) collective-permute-start(bf16[512,256]{1,0:T(8,128)(2,1)S(1)} %slice.38), channel_id=1, source_target_pairs={{4,0},{8,12},{5,1},{9,13},{6,2},{10,14},{7,3},{11,15},{20,16},{24,... | collective-permute-start | bytes 786440 | tf_op jit(solution)/shard_map/ppermute | solution.py:430
  46.8 11.5 %collective-permute-start.14 = (bf16[512,256]{1,0:T(8,128)(2,1)S(1)}, bf16[512,256]{1,0:T(8,128)(2,1)S(1)}, u32[]{:S(2)}, u32[]{:S(2)}) collective-permute-start(bf16[512,256]{1,0:T(8,128)(2,1)S(1)} %slice.39), channel_id=1, source_target_pairs={{4,0},{8,12},{5,1},{9,13},{6,2},{10,14},{7,3},{11,15},{20,16},{24,... | collective-permute-start | bytes 786440 | tf_op jit(solution)/shard_map/ppermute | solution.py:430
  52.9 5.5 %collective-permute-start.10 = (bf16[528,256]{1,0:T(8,128)(2,1)S(1)}, bf16[528,256]{1,0:T(8,128)(2,1)S(1)}, u32[]{:S(2)}, u32[]{:S(2)}) collective-permute-start(bf16[528,256]{1,0:T(8,128)(2,1)S(1)} %merge.17.refs_0_), channel_id=1, source_target_pairs={{4,8},{8,4},{5,9},{9,5},{6,10},{10,6},{7,11},{11,7},{20,24},{24,20... | collective-permute-start | bytes 811016 | tf_op jit(solution)/shard_map/ppermute | solution.py:421
  58.5 9.4 %collective-permute-start.12 = (bf16[512,256]{1,0:T(8,128)(2,1)S(1)}, bf16[512,256]{1,0:T(8,128)(2,1)S(1)}, u32[]{:S(2)}, u32[]{:S(2)}) collective-permute-start(bf16[512,256]{1,0:T(8,128)(2,1)S(1)} %slice.33), channel_id=1, source_target_pairs={{4,0},{8,12},{5,1},{9,13},{6,2},{10,14},{7,3},{11,15},{20,16},{24,... | collective-permute-start | bytes 786440 | tf_op jit(solution)/shard_map/ppermute | solution.py:430
  68.6 7.1 %collective-permute-start.15 = (bf16[256,640]{1,0:T(8,128)(2,1)S(1)}, bf16[256,640]{1,0:T(8,128)(2,1)S(1)}, u32[]{:S(2)}, u32[]{:S(2)}) collective-permute-start(bf16[256,640]{1,0:T(8,128)(2,1)S(1)} %select_convert_fusion), channel_id=1, source_target_pairs={{0,2},{2,0},{1,3},{3,1},{4,6},{6,4},{5,7},{7,5},{8,10},{10,8},{9,1... | collective-permute-start | bytes 983048 | tf_op jit(solution)/shard_map/ppermute | solution.py:468

commit v6 on v5

--- a/solution.py
+++ b/solution.py
@@ -39,6 +39,7 @@
         if c + 1 < count:
             steps += [("F", c + 1)]
         steps += [("C", c), ("O", c)]
+    steps += [("P", count - 3)]
     return steps
 
 
@@ -283,78 +284,85 @@
     )(*guard, own, got)
 
 
-def project_kernel(bounds, attended_ref, weight_hbm, sum_ref, later_ref, turned, weight, sems):
-    depth, cols = attended_ref.shape[0], sum_ref.shape[1]
-    parts = len(bounds) - 1
+def project_kernel(bounds, before, more, *refs):
+    attended_ref, weight_hbm = refs[:2]
+    sum_ref, turned, weight, sems = refs[2 + before], *refs[-3:]
+    first, cols = bounds[0], sum_ref.shape[1]
     spans = [slice(low, high) for low, high in zip(bounds[:-1], bounds[1:])]
+    places = [slice(span.start - first, span.stop - first) for span in spans]
     copies = [
-        pltpu.make_async_copy(weight_hbm.at[span, :], weight.at[span, :], sems.at[n])
-        for n, span in enumerate(spans)
+        pltpu.make_async_copy(weight_hbm.at[span, :], weight.at[place, :], sems.at[n])
+        for n, (span, place) in enumerate(zip(spans, places))
     ]
-    copies.append(
-        pltpu.make_async_copy(
-            weight_hbm.at[pl.ds(depth, later_ref.shape[0]), :], later_ref, sems.at[parts]
+    if more:
+        later_ref = refs[3 + before]
+        copies.append(
+            pltpu.make_async_copy(
+                weight_hbm.at[bounds[-1] : bounds[-1] + more, :], later_ref, sems.at[len(spans)]
+            )
         )
-    )
     for copy in copies:
         copy.start()
     turned[...] = attended_ref[...].T
-    for n in range(parts):
+    for n, place in enumerate(places):
         copies[n].wait()
-        span = spans[n]
         for low in range(0, cols, 256):
             tile = slice(low, min(low + 256, cols))
-            term = jnp.dot(turned[:, span], weight[span, tile], preferred_element_type=F32)
-            sum_ref[:, tile] = term if n == 0 else sum_ref[:, tile] + term
-    copies[parts].wait()
-
-
-def project(bounds, attended, weight):
+            term = jnp.dot(turned[:, place], weight[place, tile], preferred_element_type=F32)
+            if n or before:
+                term = term + (sum_ref if n else refs[2])[:, tile]
+            sum_ref[:, tile] = term
+    if more:
+        copies[-1].wait()
+
+
+def project(bounds, more, attended, weight, before):
     depth, rows = attended.shape
     cols = weight.shape[1]
+    before = [] if before is None else [before]
+    shapes = [jax.ShapeDtypeStruct((rows, cols), F32)]
+    if more:
+        shapes.append(jax.ShapeDtypeStruct((more, cols), BF16))
     return pl.pallas_call(
-        functools.partial(project_kernel, bounds),
-        out_shape=(
-            jax.ShapeDtypeStruct((rows, cols), F32),
-            jax.ShapeDtypeStruct((weight.shape[0] - depth, cols), BF16),
-        ),
-        in_specs=[vmem(), hbm()],
-        out_specs=(vmem(), vmem()),
+        functools.partial(project_kernel, bounds, len(before), more),
+        out_shape=shapes,
+        in_specs=[vmem(), hbm()] + [vmem()] * len(before),
+        out_specs=[vmem()] * len(shapes),
         scratch_shapes=[
             pltpu.VMEM((rows, depth), BF16),
             pltpu.VMEM((depth, cols), BF16),
             pltpu.SemaphoreType.DMA((len(bounds),)),
         ],
         cost_estimate=pl.CostEstimate(
-            flops=2 * depth * rows * cols, bytes_accessed=2 * weight.size, transcendentals=0
+            flops=2 * depth * rows * cols, bytes_accessed=2 * depth * cols, transcendentals=0
         ),
         compiler_params=pltpu.CompilerParams(vmem_limit_bytes=16 << 20),
         name="project",
-    )(attended, weight)
-
-
-def finish_kernel(attended_ref, weight_ref, sum_ref, out_ref):
+    )(attended, weight, *before)
+
+
+def finish_kernel(at_ref, attended_ref, weight_ref, sum_ref, out_ref):
     turned = attended_ref[...].T
-    for low in range(0, out_ref.shape[1], 256):
-        tile = slice(low, min(low + 256, out_ref.shape[1]))
+    cols = out_ref.shape[1]
+    for low in range(0, cols, 256):
+        wide = min(256, cols - low)
+        tile = pl.ds(pl.multiple_of(at_ref[0] * HD + low, HD), wide)
         term = jnp.dot(turned, weight_ref[:, tile], preferred_element_type=F32)
-        out_ref[:, tile] = sum_ref[:, tile] + term
-
-
-def finish(attended, weight, summed):
+        out_ref[:, low : low + wide] = (sum_ref[:, tile] + term).astype(out_ref.dtype)
+
+
+def finish(at, cols, dtype, attended, weight, summed):
     return pl.pallas_call(
         finish_kernel,
-        out_shape=jax.ShapeDtypeStruct(summed.shape, F32),
-        in_specs=[vmem()] * 3,
+        out_shape=jax.ShapeDtypeStruct((summed.shape[0], cols), dtype),
+        in_specs=[pl.BlockSpec(memory_space=pltpu.SMEM)] + [vmem()] * 3,
         out_specs=vmem(),
         cost_estimate=pl.CostEstimate(
-            flops=2 * attended.size * weight.shape[1],
-            bytes_accessed=2 * weight.size,
-            transcendentals=0,
+            flops=2 * attended.size * cols, bytes_accessed=2 * weight.size, transcendentals=0
         ),
         compiler_params=pltpu.CompilerParams(vmem_limit_bytes=12 << 20),
         name="finish",
-    )(attended, weight, summed)
+    )(at, attended, weight, summed)
 
 
 def local(
@@ -390,7 +398,7 @@
     inward = [[(j, j + 1), (n_slab - 1 - j, n_slab - 2 - j)] for j in range(side - 1)]
     outward = [[(b, a) for a, b in pairs] for pairs in inward]
     own, got_in, folded, crossed, total, final = {}, {}, {}, {}, {}, {}
-    last = []
+    last, early_sum, arrived = [], [], []
 
     def run(value):
         last[:] = [value]
@@ -428,8 +436,18 @@
         attended = total[c][: sizes[c] * HD]
         for j in range(side - 2, -1, -1):
             got = lax.ppermute(attended, "slab", outward[j])
-            attended = jnp.where((slab == j) | (slab == n_slab - 1 - j), got, attended)
+            if c == count - 1 and j == 0:
+                arrived.append(got)
+            else:
+                attended = jnp.where((slab == j) | (slab == n_slab - 1 - j), got, attended)
         final[c] = attended
+
+    def project_early(c):
+        parts = range(c + 1)
+        bounds = tuple(start * HD for start in starts[: c + 2])
+        early = jnp.concatenate([final[p] for p in parts], axis=0)
+        (summed,) = project(bounds, 0, in_order(early, *last), out_weight, None)
+        early_sum.append(run(summed))
 
     def send_both(c):
         if side != 2:
@@ -446,12 +464,18 @@
         final[c - 3] = jnp.where(outer, got, sent)[: sizes[c - 3] * HD]
 
     steps = {"A": attention, "I": send_in, "F": fold, "C": cross, "O": send_out, "X": send_both}
+    steps["P"] = project_early
     for kind, c in order_of(sizes):
         steps[kind](c)
-    early = jnp.concatenate([final[c] for c in range(count - 1)], axis=0)
-    bounds = tuple(start * HD for start in starts)
-    projected, later = project(bounds, in_order(early, *last), out_weight)
-    projected = finish(in_order(final[count - 1], projected), later, projected)
+    bounds = tuple(start * HD for start in starts[count - 2 :])
+    projected, later = project(
+        bounds, sizes[-1] * HD, in_order(final[count - 2], *last), out_weight,
+        early_sum[0] if early_sum else None,
+    )
+    attended = final[count - 1]
+    if arrived:
+        got = in_order(arrived[0], projected)
+        attended = jnp.where((slab == 0) | (slab == n_slab - 1), got, attended)
 
     half = time_weight.shape[0] // 2
     frequency = jnp.exp(-jnp.log(10000.0) * jnp.arange(half, dtype=F32) / half)
@@ -460,14 +484,17 @@
     time_gate = 1.0 + jnp.dot(embedding, time_weight, precision=lax.Precision.HIGHEST)
 
     cols = time_weight.shape[1]
-    if n_head == 2:
-        me = lax.axis_index("head")
-        left, right = projected[:, :cols], projected[:, cols:]
-        kept = jnp.where(me == 0, left, right)
-        sent = jnp.where(me == 0, right, left).astype(BF16)
-        summed = kept + lax.ppermute(sent, "head", [(0, 1), (1, 0)]).astype(F32)
+    if n_head == 2 and cols % HD == 0:
+        mine = lax.axis_index("head") * (cols // HD)
+        other = (cols // HD) - mine
+        sent = finish(other[None], cols, BF16, attended, later, projected)
+        got = lax.ppermute(sent, "head", [(0, 1), (1, 0)])
+        kept = finish(mine[None], cols, F32, in_order(attended, sent), later, projected)
+        summed = kept + got.astype(F32)
     else:
-        summed = lax.psum_scatter(projected, "head", scatter_dimension=1, tiled=True)
+        zero = jnp.zeros((1,), jnp.int32)
+        ready = finish(zero, projected.shape[1], F32, attended, later, projected)
+        summed = lax.psum_scatter(ready, "head", scatter_dimension=1, tiled=True)
     return (time_gate * summed).astype(BF16)
 
 

time: 77.1 us -> 84.4 us (1.095)
  waiting for transfers between devices: 21.9 us -> 25.6 us
  starting transfers between devices: 28.3 us -> 30.4 us
  Pallas kernels: 22.2 us -> 23.7 us
    ppermute x2, waiting for transfers between devices: 2.83 us -> 7.47 us  [send_both(): got = lax.ppermute(sent, 'slab', inward[0] + outward[0])]
    ppermute x2, starting transfers between devices: 6.71 us -> 8.83 us  [send_both(): got = lax.ppermute(sent, 'slab', inward[0] + outward[0])]
    pallas_call x2 -> x4, Pallas kernels: 4.25 us -> 5.75 us  [the longest x2 4.94 us: project(): pl.pallas_call(functools.partial(project_kernel, bounds, len(before), mor...]
where the time goes in v6:
time: 84.4 us; the launch traced here: 83.8 us
  starting transfers between devices  30.4 us (36%)
  waiting for transfers between devices  25.6 us (30%)
  Pallas kernels  23.7 us (28%)
  between operations  1.76 us (2%)
  other arithmetic  1.25 us (1%)
    pallas_call x5, Pallas kernels, attend(): pl.pallas_call(functools.partial(attend_kernel, start, heads, width), out...  14.8 us
    ppermute x3, waiting for transfers between devices, send_out(): got = lax.ppermute(attended, 'slab', outward[j])  13.1 us
    ppermute x3, starting transfers between devices, send_in(): lax.ppermute(sent, 'slab', inward[side - 2])  9.42 us
    ppermute x2, starting transfers between devices, send_both(): got = lax.ppermute(sent, 'slab', inward[0] + outward[0])  8.83 us
    ppermute x2, waiting for transfers between devices, send_both(): got = lax.ppermute(sent, 'slab', inward[0] + outward[0])  7.47 us
    pallas_call x2, Pallas kernels, project(): pl.pallas_call(functools.partial(project_kernel, bounds, len(before), mor...  4.94 us
    ppermute x1, waiting for transfers between devices, local(): got = lax.ppermute(sent, 'head', [(0, 1), (1, 0)])  4.69 us
    ppermute x3, starting transfers between devices, send_out(): got = lax.ppermute(attended, 'slab', outward[j])  4.06 us
  transfers between devices with their start and end apart: 16, of which 6 were waited for; matrix products, arithmetic and copies ran while one was open for 2% of the time, Pallas kernels for 22%

profile of v6, /device:TPU:0, one launch (start us, length us, event | category | flops | bytes accessed | tf_op | source)
XLA Modules:
  0.0 83.8 jit_solution(8773566240635234263)
XLA Ops:
  0.0 0.0 copy-start
  0.0 1.8 %prepare.1 = (f32[8,256]{1,0:T(8,128)S(1)}, bf16[256,2560]{1,0:T(8,128)(2,1)S(1)}) custom-call(bf16[256,2560]{1,0:T(8,128)(2,1)} %q_hbm.11, bf16[64,2560]{1,0:T(8,128)(2,1)} %fk.1, bf16[64,2560]{1,0:T(8,128)(2,1)} %nk.1, bf16[64,2560]{1,0:T(8,128)(2,1)} %fv.1, bf16[64,2560]{1,0:T(8,128)(2,1)} %nv.1), custom_call_target="tpu_custom_call" | custom-call | flops 1310720 | bytes 5242880 | tf_op jit(solution)/shard_map/prepare/pallas_call | solution.py:95
  1.8 0.0 copy-start.1
  1.8 0.6 collective-permute-start.1
  2.4 2.6 %collective-permute-start = (f32[8,256]{1,0:T(8,128)S(1)}, f32[8,256]{1,0:T(8,128)S(1)}, u32[]{:S(2)}, u32[]{:S(2)}) collective-permute-start(f32[8,256]{1,0:T(8,128)S(1)} %get-tuple-element.27.own_sq), channel_id=1, source_target_pairs={{0,2},{2,0},{1,3},{3,1},{4,6},{6,4},{5,7},{7,5},{8,10},{10,8},{9,1... | collective-permute-start | bytes 24584 | tf_op jit(solution)/shard_map/ppermute | solution.py:383
  5.6 0.0 copy-done.3
  5.6 0.6 broadcast_in_dim.11.gain_hbm
  6.2 0.4 collective-permute-done.far_sq
  6.6 0.0 collective-permute-done.1.far_hbm
  6.6 0.0 copy-done.1
  6.6 2.9 %attend.5.refs_0_ = bf16[400,256]{1,0:T(8,128)(2,1)S(1)} custom-call(s32[1]{0:T(128)S(6)} %convert_element_type.21.owner_ref, f32[8,256]{1,0:T(8,128)S(1)} %get-tuple-element.27.own_sq, f32[8,256]{1,0:T(8,128)S(1)} %collective-permute-done.far_sq, f32[1,2560]{1,0:T(1,128)} %broadcast_in_dim.11.gain_hbm, bf16[256,2560]{1,0:T(8,128)(2,1)} %q_hbm.11, ...), custom_call_target="tpu_custom_call" | custom-call | flops 1207959552 | bytes 1179648 | tf_op jit(solution)/shard_map/attend/pallas_call | solution.py:229
  9.5 4.0 %collective-permute-start.2 = (bf16[400,256]{1,0:T(8,128)(2,1)S(1)}, bf16[400,256]{1,0:T(8,128)(2,1)S(1)}, u32[]{:S(2)}, u32[]{:S(2)}) collective-permute-start(bf16[400,256]{1,0:T(8,128)(2,1)S(1)} %attend.5.refs_0_), channel_id=1, source_target_pairs={{0,4},{12,8},{1,5},{13,9},{2,6},{14,10},{3,7},{15,11},{16,20},{28,... | collective-permute-start | bytes 614408 | tf_op jit(solution)/shard_map/ppermute | solution.py:423
  13.6 3.3 %attend.6.refs_0_ = bf16[656,256]{1,0:T(8,128)(2,1)S(1)} custom-call(s32[1]{0:T(128)S(6)} %convert_element_type.21.owner_ref, f32[8,256]{1,0:T(8,128)S(1)} %get-tuple-element.27.own_sq, f32[8,256]{1,0:T(8,128)S(1)} %collective-permute-done.far_sq, f32[1,2560]{1,0:T(1,128)} %broadcast_in_dim.11.gain_hbm, bf16[256,2560]{1,0:T(8,128)(2,1)} %q_hbm.11, ...), custom_call_target="tpu_custom_call" | custom-call | flops 2013265920 | bytes 1966080 | tf_op jit(solution)/shard_map/attend/pallas_call | solution.py:229
  16.8 1.3 %collective-permute-start.4 = (bf16[656,256]{1,0:T(8,128)(2,1)S(1)}, bf16[656,256]{1,0:T(8,128)(2,1)S(1)}, u32[]{:S(2)}, u32[]{:S(2)}) collective-permute-start(bf16[656,256]{1,0:T(8,128)(2,1)S(1)} %attend.6.refs_0_), channel_id=1, source_target_pairs={{0,4},{12,8},{1,5},{13,9},{2,6},{14,10},{3,7},{15,11},{16,20},{28,... | collective-permute-start | bytes 1007624 | tf_op jit(solution)/shard_map/ppermute | solution.py:423
  18.1 2.9 %attend.7.refs_0_ = bf16[528,256]{1,0:T(8,128)(2,1)S(1)} custom-call(s32[1]{0:T(128)S(6)} %convert_element_type.21.owner_ref, f32[8,256]{1,0:T(8,128)S(1)} %get-tuple-element.27.own_sq, f32[8,256]{1,0:T(8,128)S(1)} %collective-permute-done.far_sq, f32[1,2560]{1,0:T(1,128)} %broadcast_in_dim.11.gain_hbm, bf16[256,2560]{1,0:T(8,128)(2,1)} %q_hbm.11, ...), custom_call_target="tpu_custom_call" | custom-call | flops 1610612736 | bytes 1572864 | tf_op jit(solution)/shard_map/attend/pallas_call | solution.py:229
  21.0 0.0 collective-permute-done.2.refs_1_
  21.0 0.1 merge.10.refs_0_
  21.2 0.7 collective-permute-start.3
  22.5 4.1 %collective-permute-start.6 = (bf16[528,256]{1,0:T(8,128)(2,1)S(1)}, bf16[528,256]{1,0:T(8,128)(2,1)S(1)}, u32[]{:S(2)}, u32[]{:S(2)}) collective-permute-start(bf16[528,256]{1,0:T(8,128)(2,1)S(1)} %attend.7.refs_0_), channel_id=1, source_target_pairs={{0,4},{12,8},{1,5},{13,9},{2,6},{14,10},{3,7},{15,11},{16,20},{28,... | collective-permute-start | bytes 811016 | tf_op jit(solution)/shard_map/ppermute | solution.py:423
  26.6 2.9 %attend.8.refs_0_ = bf16[528,256]{1,0:T(8,128)(2,1)S(1)} custom-call(s32[1]{0:T(128)S(6)} %convert_element_type.21.owner_ref, f32[8,256]{1,0:T(8,128)S(1)} %get-tuple-element.27.own_sq, f32[8,256]{1,0:T(8,128)S(1)} %collective-permute-done.far_sq, f32[1,2560]{1,0:T(1,128)} %broadcast_in_dim.11.gain_hbm, bf16[256,2560]{1,0:T(8,128)(2,1)} %q_hbm.11, ...), custom_call_target="tpu_custom_call" | custom-call | flops 1610612736 | bytes 1572864 | tf_op jit(solution)/shard_map/attend/pallas_call | solution.py:229
  29.5 0.0 collective-permute-done.4.refs_1_
  29.5 0.2 merge.11.refs_0_
  29.6 0.7 collective-permute-start.5
  30.3 0.0 collective-permute-done.3.refs_1_
  30.3 0.1 merge.12
  30.5 0.1 pad_select_fusion.1
  30.5 1.1 %collective-permute-start.9 = (bf16[528,256]{1,0:T(8,128)(2,1)S(1)}, bf16[528,256]{1,0:T(8,128)(2,1)S(1)}, u32[]{:S(2)}, u32[]{:S(2)}) collective-permute-start(bf16[528,256]{1,0:T(8,128)(2,1)S(1)} %pad_select_fusion.1), channel_id=1, source_target_pairs={{0,4},{12,8},{4,0},{8,12},{1,5},{13,9},{5,1},{9,13},{2,6},{14,10},... | collective-permute-start | bytes 811016 | tf_op jit(solution)/shard_map/ppermute | solution.py:462
  31.6 2.9 %attend.9.refs_0_ = bf16[528,256]{1,0:T(8,128)(2,1)S(1)} custom-call(s32[1]{0:T(128)S(6)} %convert_element_type.21.owner_ref, f32[8,256]{1,0:T(8,128)S(1)} %get-tuple-element.27.own_sq, f32[8,256]{1,0:T(8,128)S(1)} %collective-permute-done.far_sq, f32[1,2560]{1,0:T(1,128)} %broadcast_in_dim.11.gain_hbm, bf16[256,2560]{1,0:T(8,128)(2,1)} %q_hbm.11, ...), custom_call_target="tpu_custom_call" | custom-call | flops 1610612736 | bytes 1572864 | tf_op jit(solution)/shard_map/attend/pallas_call | solution.py:229
  34.5 0.0 collective-permute-done.6.refs_1_
  34.5 0.1 merge.13.refs_0_
  34.7 0.7 collective-permute-start.8
  35.3 0.1 fusion
  35.4 0.0 collective-permute-done.5.refs_1_
  35.4 0.2 merge.14
  35.6 0.1 pad_select_fusion
  35.7 2.2 %collective-permute-done.9.refs_1_ = bf16[528,256]{1,0:T(8,128)(2,1)S(1)} collective-permute-done((bf16[528,256]{1,0:T(8,128)(2,1)S(1)}, bf16[528,256]{1,0:T(8,128)(2,1)S(1)}, u32[]{:S(2)}, u32[]{:S(2)}) %collective-permute-start.9) | collective-permute-done | bytes 270368 | tf_op jit(solution)/shard_map/ppermute | solution.py:462
  37.8 0.1 merge.15.refs_0_
  38.0 0.0 collective-permute-done.8.refs_1_
  38.0 0.1 merge.16
  38.1 1.3 %collective-permute-start.14 = (bf16[512,256]{1,0:T(8,128)(2,1)S(1)}, bf16[512,256]{1,0:T(8,128)(2,1)S(1)}, u32[]{:S(2)}, u32[]{:S(2)}) collective-permute-start(bf16[512,256]{1,0:T(8,128)(2,1)S(1)} %slice.31), channel_id=1, source_target_pairs={{4,0},{8,12},{5,1},{9,13},{6,2},{10,14},{7,3},{11,15},{20,16},{24,... | collective-permute-start | bytes 786440 | tf_op jit(solution)/shard_map/ppermute | solution.py:438
  39.5 7.7 %collective-permute-start.7 = (bf16[656,256]{1,0:T(8,128)(2,1)S(1)}, bf16[656,256]{1,0:T(8,128)(2,1)S(1)}, u32[]{:S(2)}, u32[]{:S(2)}) collective-permute-start(bf16[656,256]{1,0:T(8,128)(2,1)S(1)} %pad_select_fusion), channel_id=1, source_target_pairs={{0,4},{12,8},{4,0},{8,12},{1,5},{13,9},{5,1},{9,13},{2,6},{14,10},... | collective-permute-start | bytes 1007624 | tf_op jit(solution)/shard_map/ppermute | solution.py:462
  47.2 0.7 collective-permute-start.11
  47.9 6.3 %collective-permute-done.14 = bf16[512,256]{1,0:T(8,128)(2,1)S(1)} collective-permute-done((bf16[512,256]{1,0:T(8,128)(2,1)S(1)}, bf16[512,256]{1,0:T(8,128)(2,1)S(1)}, u32[]{:S(2)}, u32[]{:S(2)}) %collective-permute-start.14) | collective-permute-done | bytes 262176 | tf_op jit(solution)/shard_map/ppermute | solution.py:438
  54.3 5.3 %collective-permute-done.7 = bf16[656,256]{1,0:T(8,128)(2,1)S(1)} collective-permute-done((bf16[656,256]{1,0:T(8,128)(2,1)S(1)}, bf16[656,256]{1,0:T(8,128)(2,1)S(1)}, u32[]{:S(2)}, u32[]{:S(2)}) %collective-permute-start.7) | collective-permute-done | bytes 335904 | tf_op jit(solution)/shard_map/ppermute | solution.py:462
  59.6 0.1 merge.17.refs_0_
  59.7 0.7 collective-permute-start.10
  60.4 0.0 collective-permute-done.11.refs_1_
  60.4 0.1 merge.18
  60.6 1.3 %collective-permute-start.13 = (bf16[512,256]{1,0:T(8,128)(2,1)S(1)}, bf16[512,256]{1,0:T(8,128)(2,1)S(1)}, u32[]{:S(2)}, u32[]{:S(2)}) collective-permute-start(bf16[512,256]{1,0:T(8,128)(2,1)S(1)} %slice.26), channel_id=1, source_target_pairs={{4,0},{8,12},{5,1},{9,13},{6,2},{10,14},{7,3},{11,15},{20,16},{24,... | collective-permute-start | bytes 786440 | tf_op jit(solution)/shard_map/ppermute | solution.py:438
  61.9 0.1 pad_maximum_fusion.refs_0_
  62.0 0.0 collective-permute-done.10.refs_1_
  62.0 0.1 merge.19
  62.2 1.5 %collective-permute-start.12 = (bf16[512,256]{1,0:T(8,128)(2,1)S(1)}, bf16[512,256]{1,0:T(8,128)(2,1)S(1)}, u32[]{:S(2)}, u32[]{:S(2)}) collective-permute-start(bf16[512,256]{1,0:T(8,128)(2,1)S(1)} %slice.25), channel_id=1, source_target_pairs={{4,0},{8,12},{5,1},{9,13},{6,2},{10,14},{7,3},{11,15},{20,16},{24,... | collective-permute-start | bytes 786440 | tf_op jit(solution)/shard_map/ppermute | solution.py:438
  63.7 6.7 %collective-permute-done.13 = bf16[512,256]{1,0:T(8,128)(2,1)S(1)} collective-permute-done((bf16[512,256]{1,0:T(8,128)(2,1)S(1)}, bf16[512,256]{1,0:T(8,128)(2,1)S(1)}, u32[]{:S(2)}, u32[]{:S(2)}) %collective-permute-start.13) | collective-permute-done | bytes 262176 | tf_op jit(solution)/shard_map/ppermute | solution.py:438
  70.4 3.1 %project.2.refs_2_ = f32[256,1280]{1,0:T(8,128)S(1)} custom-call(bf16[1536,256]{1,0:T(8,128)(2,1)S(1)} %pad_maximum_fusion.refs_0_, bf16[2560,1280]{1,0:T(8,128)(2,1)} %refs_1_.3), custom_call_target="tpu_custom_call" | custom-call | flops 1006632960 | bytes 3932160 | tf_op jit(solution)/shard_map/project/pallas_call | solution.py:326
  73.5 1.9 %project.3 = (f32[256,1280]{1,0:T(8,128)S(1)}, bf16[512,1280]{1,0:T(8,128)(2,1)S(1)}) custom-call(bf16[512,256]{1,0:T(8,128)(2,1)S(1)} %broadcast_select_fusion.2.refs_0_, bf16[2560,1280]{1,0:T(8,128)(2,1)} %refs_1_.3, f32[256,1280]{1,0:T(8,128)S(1)} %project.2.refs_2_), custom_call_target="tpu_custom_call" | custom-call | flops 335544320 | bytes 1310720 | tf_op jit(solution)/shard_map/project/pallas_call | solution.py:326
  75.4 0.0 collective-permute-done.12
  75.4 0.4 finish.2
  75.9 1.6 %collective-permute-start.15 = (bf16[256,640]{1,0:T(8,128)(2,1)S(1)}, bf16[256,640]{1,0:T(8,128)(2,1)S(1)}, u32[]{:S(2)}, u32[]{:S(2)}) collective-permute-start(bf16[256,640]{1,0:T(8,128)(2,1)S(1)} %finish.2), channel_id=1, source_target_pairs={{0,2},{2,0},{1,3},{3,1},{4,6},{6,4},{5,7},{7,5},{8,10},{10,8},{9,1... | collective-permute-start | bytes 983048 | tf_op jit(solution)/shard_map/ppermute | solution.py:491
  77.4 0.0 copy-done
  77.5 0.4 convolution_reduce_fusion
  77.9 0.4 finish.3
  78.3 4.7 %collective-permute-done.15 = bf16[256,640]{1,0:T(8,128)(2,1)S(1)} collective-permute-done((bf16[256,640]{1,0:T(8,128)(2,1)S(1)}, bf16[256,640]{1,0:T(8,128)(2,1)S(1)}, u32[]{:S(2)}, u32[]{:S(2)}) %collective-permute-start.15) | collective-permute-done | bytes 327712 | tf_op jit(solution)/shard_map/ppermute | solution.py:491
  83.0 0.8 multiply_convert_fusion
  (14 shorter events, 0.3 us)
Async XLA Ops:
  0.0 77.5 %copy-start = (f32[256,640]{1,0:T(8,128)S(1)}, f32[256,640]{1,0:T(8,128)}, u32[]{:S(2)}) copy-start(f32[256,640]{1,0:T(8,128)} %param.21) | copy-start | bytes 1966084
  0.0 5.6 %copy-start.3 = (f32[2560]{0:T(1024)S(1)}, f32[2560]{0:T(1024)}, u32[]{:S(2)}) copy-start(f32[2560]{0:T(1024)} %param.13) | copy-start | bytes 30724
  1.8 4.8 %copy-start.1 = (bf16[256,2560]{1,0:T(8,128)(2,1)}, bf16[256,2560]{1,0:T(8,128)(2,1)S(1)}, u32[]{:S(2)}) copy-start(bf16[256,2560]{1,0:T(8,128)(2,1)S(1)} %get-tuple-element.28.near_hbm) | copy-start | bytes 3932164
  1.8 4.7 %collective-permute-start.1 = (bf16[256,2560]{1,0:T(8,128)(2,1)S(1)}, bf16[256,2560]{1,0:T(8,128)(2,1)S(1)}, u32[]{:S(2)}, u32[]{:S(2)}) collective-permute-start(bf16[256,2560]{1,0:T(8,128)(2,1)S(1)} %get-tuple-element.28.near_hbm), channel_id=1, source_target_pairs={{0,1},{1,0},{2,3},{3,2},{4,5},{5,4},{6,7},{7,6},{8,9},{9,8},{10,11... | collective-permute-start | bytes 3932168 | tf_op jit(solution)/shard_map/ppermute | solution.py:387
  2.4 4.2 %collective-permute-start = (f32[8,256]{1,0:T(8,128)S(1)}, f32[8,256]{1,0:T(8,128)S(1)}, u32[]{:S(2)}, u32[]{:S(2)}) collective-permute-start(f32[8,256]{1,0:T(8,128)S(1)} %get-tuple-element.27.own_sq), channel_id=1, source_target_pairs={{0,2},{2,0},{1,3},{3,1},{4,6},{6,4},{5,7},{7,5},{8,10},{10,8},{9,1... | collective-permute-start | bytes 24584 | tf_op jit(solution)/shard_map/ppermute | solution.py:383
  6.6 2.9 %copy-start.2 = (bf16[256,2560]{1,0:T(8,128)(2,1)}, bf16[256,2560]{1,0:T(8,128)(2,1)S(1)}, u32[]{:S(2)}) copy-start(bf16[256,2560]{1,0:T(8,128)(2,1)S(1)} %collective-permute-done.1.far_hbm) | copy-start | bytes 3932164
  9.5 11.5 %collective-permute-start.2 = (bf16[400,256]{1,0:T(8,128)(2,1)S(1)}, bf16[400,256]{1,0:T(8,128)(2,1)S(1)}, u32[]{:S(2)}, u32[]{:S(2)}) collective-permute-start(bf16[400,256]{1,0:T(8,128)(2,1)S(1)} %attend.5.refs_0_), channel_id=1, source_target_pairs={{0,4},{12,8},{1,5},{13,9},{2,6},{14,10},{3,7},{15,11},{16,20},{28,... | collective-permute-start | bytes 614408 | tf_op jit(solution)/shard_map/ppermute | solution.py:423
  16.8 12.6 %collective-permute-start.4 = (bf16[656,256]{1,0:T(8,128)(2,1)S(1)}, bf16[656,256]{1,0:T(8,128)(2,1)S(1)}, u32[]{:S(2)}, u32[]{:S(2)}) collective-permute-start(bf16[656,256]{1,0:T(8,128)(2,1)S(1)} %attend.6.refs_0_), channel_id=1, source_target_pairs={{0,4},{12,8},{1,5},{13,9},{2,6},{14,10},{3,7},{15,11},{16,20},{28,... | collective-permute-start | bytes 1007624 | tf_op jit(solution)/shard_map/ppermute | solution.py:423
  21.2 9.2 %collective-permute-start.3 = (bf16[400,256]{1,0:T(8,128)(2,1)S(1)}, bf16[400,256]{1,0:T(8,128)(2,1)S(1)}, u32[]{:S(2)}, u32[]{:S(2)}) collective-permute-start(bf16[400,256]{1,0:T(8,128)(2,1)S(1)} %merge.10.refs_0_), channel_id=1, source_target_pairs={{4,8},{8,4},{5,9},{9,5},{6,10},{10,6},{7,11},{11,7},{20,24},{24,20... | collective-permute-start | bytes 614408 | tf_op jit(solution)/shard_map/ppermute | solution.py:429
  22.5 12.0 %collective-permute-start.6 = (bf16[528,256]{1,0:T(8,128)(2,1)S(1)}, bf16[528,256]{1,0:T(8,128)(2,1)S(1)}, u32[]{:S(2)}, u32[]{:S(2)}) collective-permute-start(bf16[528,256]{1,0:T(8,128)(2,1)S(1)} %attend.7.refs_0_), channel_id=1, source_target_pairs={{0,4},{12,8},{1,5},{13,9},{2,6},{14,10},{3,7},{15,11},{16,20},{28,... | collective-permute-start | bytes 811016 | tf_op jit(solution)/shard_map/ppermute | solution.py:423
  29.6 5.8 %collective-permute-start.5 = (bf16[656,256]{1,0:T(8,128)(2,1)S(1)}, bf16[656,256]{1,0:T(8,128)(2,1)S(1)}, u32[]{:S(2)}, u32[]{:S(2)}) collective-permute-start(bf16[656,256]{1,0:T(8,128)(2,1)S(1)} %merge.11.refs_0_), channel_id=1, source_target_pairs={{4,8},{8,4},{5,9},{9,5},{6,10},{10,6},{7,11},{11,7},{20,24},{24,20... | collective-permute-start | bytes 1007624 | tf_op jit(solution)/shard_map/ppermute | solution.py:429
  30.5 7.3 %collective-permute-start.9 = (bf16[528,256]{1,0:T(8,128)(2,1)S(1)}, bf16[528,256]{1,0:T(8,128)(2,1)S(1)}, u32[]{:S(2)}, u32[]{:S(2)}) collective-permute-start(bf16[528,256]{1,0:T(8,128)(2,1)S(1)} %pad_select_fusion.1), channel_id=1, source_target_pairs={{0,4},{12,8},{4,0},{8,12},{1,5},{13,9},{5,1},{9,13},{2,6},{14,10},... | collective-permute-start | bytes 811016 | tf_op jit(solution)/shard_map/ppermute | solution.py:462
  34.7 3.3 %collective-permute-start.8 = (bf16[528,256]{1,0:T(8,128)(2,1)S(1)}, bf16[528,256]{1,0:T(8,128)(2,1)S(1)}, u32[]{:S(2)}, u32[]{:S(2)}) collective-permute-start(bf16[528,256]{1,0:T(8,128)(2,1)S(1)} %merge.13.refs_0_), channel_id=1, source_target_pairs={{4,8},{8,4},{5,9},{9,5},{6,10},{10,6},{7,11},{11,7},{20,24},{24,20... | collective-permute-start | bytes 811016 | tf_op jit(solution)/shard_map/ppermute | solution.py:429
  38.1 16.1 %collective-permute-start.14 = (bf16[512,256]{1,0:T(8,128)(2,1)S(1)}, bf16[512,256]{1,0:T(8,128)(2,1)S(1)}, u32[]{:S(2)}, u32[]{:S(2)}) collective-permute-start(bf16[512,256]{1,0:T(8,128)(2,1)S(1)} %slice.31), channel_id=1, source_target_pairs={{4,0},{8,12},{5,1},{9,13},{6,2},{10,14},{7,3},{11,15},{20,16},{24,... | collective-permute-start | bytes 786440 | tf_op jit(solution)/shard_map/ppermute | solution.py:438
  39.5 20.1 %collective-permute-start.7 = (bf16[656,256]{1,0:T(8,128)(2,1)S(1)}, bf16[656,256]{1,0:T(8,128)(2,1)S(1)}, u32[]{:S(2)}, u32[]{:S(2)}) collective-permute-start(bf16[656,256]{1,0:T(8,128)(2,1)S(1)} %pad_select_fusion), channel_id=1, source_target_pairs={{0,4},{12,8},{4,0},{8,12},{1,5},{13,9},{5,1},{9,13},{2,6},{14,10},... | collective-permute-start | bytes 1007624 | tf_op jit(solution)/shard_map/ppermute | solution.py:462
  47.2 13.2 %collective-permute-start.11 = (bf16[528,256]{1,0:T(8,128)(2,1)S(1)}, bf16[528,256]{1,0:T(8,128)(2,1)S(1)}, u32[]{:S(2)}, u32[]{:S(2)}) collective-permute-start(bf16[528,256]{1,0:T(8,128)(2,1)S(1)} %merge.15.refs_0_), channel_id=1, source_target_pairs={{4,8},{8,4},{5,9},{9,5},{6,10},{10,6},{7,11},{11,7},{20,24},{24,20... | collective-permute-start | bytes 811016 | tf_op jit(solution)/shard_map/ppermute | solution.py:429
  59.7 2.3 %collective-permute-start.10 = (bf16[528,256]{1,0:T(8,128)(2,1)S(1)}, bf16[528,256]{1,0:T(8,128)(2,1)S(1)}, u32[]{:S(2)}, u32[]{:S(2)}) collective-permute-start(bf16[528,256]{1,0:T(8,128)(2,1)S(1)} %merge.17.refs_0_), channel_id=1, source_target_pairs={{4,8},{8,4},{5,9},{9,5},{6,10},{10,6},{7,11},{11,7},{20,24},{24,20... | collective-permute-start | bytes 811016 | tf_op jit(solution)/shard_map/ppermute | solution.py:429
  60.6 9.8 %collective-permute-start.13 = (bf16[512,256]{1,0:T(8,128)(2,1)S(1)}, bf16[512,256]{1,0:T(8,128)(2,1)S(1)}, u32[]{:S(2)}, u32[]{:S(2)}) collective-permute-start(bf16[512,256]{1,0:T(8,128)(2,1)S(1)} %slice.26), channel_id=1, source_target_pairs={{4,0},{8,12},{5,1},{9,13},{6,2},{10,14},{7,3},{11,15},{20,16},{24,... | collective-permute-start | bytes 786440 | tf_op jit(solution)/shard_map/ppermute | solution.py:438
  62.2 13.2 %collective-permute-start.12 = (bf16[512,256]{1,0:T(8,128)(2,1)S(1)}, bf16[512,256]{1,0:T(8,128)(2,1)S(1)}, u32[]{:S(2)}, u32[]{:S(2)}) collective-permute-start(bf16[512,256]{1,0:T(8,128)(2,1)S(1)} %slice.25), channel_id=1, source_target_pairs={{4,0},{8,12},{5,1},{9,13},{6,2},{10,14},{7,3},{11,15},{20,16},{24,... | collective-permute-start | bytes 786440 | tf_op jit(solution)/shard_map/ppermute | solution.py:438
  75.9 7.1 %collective-permute-start.15 = (bf16[256,640]{1,0:T(8,128)(2,1)S(1)}, bf16[256,640]{1,0:T(8,128)(2,1)S(1)}, u32[]{:S(2)}, u32[]{:S(2)}) collective-permute-start(bf16[256,640]{1,0:T(8,128)(2,1)S(1)} %finish.2), channel_id=1, source_target_pairs={{0,2},{2,0},{1,3},{3,1},{4,6},{6,4},{5,7},{7,5},{8,10},{10,8},{9,1... | collective-permute-start | bytes 983048 | tf_op jit(solution)/shard_map/ppermute | solution.py:491

commit v7 on v5

--- a/solution.py
+++ b/solution.py
@@ -333,28 +333,28 @@
     )(attended, weight)
 
 
-def finish_kernel(attended_ref, weight_ref, sum_ref, out_ref):
+def finish_kernel(at_ref, attended_ref, weight_ref, sum_ref, out_ref):
     turned = attended_ref[...].T
-    for low in range(0, out_ref.shape[1], 256):
-        tile = slice(low, min(low + 256, out_ref.shape[1]))
+    cols = out_ref.shape[1]
+    for low in range(0, cols, 256):
+        wide = min(256, cols - low)
+        tile = pl.ds(pl.multiple_of(at_ref[0] * HD + low, HD), wide)
         term = jnp.dot(turned, weight_ref[:, tile], preferred_element_type=F32)
-        out_ref[:, tile] = sum_ref[:, tile] + term
-
-
-def finish(attended, weight, summed):
+        out_ref[:, low : low + wide] = (sum_ref[:, tile] + term).astype(out_ref.dtype)
+
+
+def finish(at, cols, dtype, attended, weight, summed):
     return pl.pallas_call(
         finish_kernel,
-        out_shape=jax.ShapeDtypeStruct(summed.shape, F32),
-        in_specs=[vmem()] * 3,
+        out_shape=jax.ShapeDtypeStruct((summed.shape[0], cols), dtype),
+        in_specs=[pl.BlockSpec(memory_space=pltpu.SMEM)] + [vmem()] * 3,
         out_specs=vmem(),
         cost_estimate=pl.CostEstimate(
-            flops=2 * attended.size * weight.shape[1],
-            bytes_accessed=2 * weight.size,
-            transcendentals=0,
+            flops=2 * attended.size * cols, bytes_accessed=2 * weight.size, transcendentals=0
         ),
         compiler_params=pltpu.CompilerParams(vmem_limit_bytes=12 << 20),
         name="finish",
-    )(attended, weight, summed)
+    )(at, attended, weight, summed)
 
 
 def local(
@@ -451,7 +451,7 @@
     early = jnp.concatenate([final[c] for c in range(count - 1)], axis=0)
     bounds = tuple(start * HD for start in starts)
     projected, later = project(bounds, in_order(early, *last), out_weight)
-    projected = finish(in_order(final[count - 1], projected), later, projected)
+    attended = in_order(final[count - 1], projected)
 
     half = time_weight.shape[0] // 2
     frequency = jnp.exp(-jnp.log(10000.0) * jnp.arange(half, dtype=F32) / half)
@@ -460,14 +460,17 @@
     time_gate = 1.0 + jnp.dot(embedding, time_weight, precision=lax.Precision.HIGHEST)
 
     cols = time_weight.shape[1]
-    if n_head == 2:
-        me = lax.axis_index("head")
-        left, right = projected[:, :cols], projected[:, cols:]
-        kept = jnp.where(me == 0, left, right)
-        sent = jnp.where(me == 0, right, left).astype(BF16)
-        summed = kept + lax.ppermute(sent, "head", [(0, 1), (1, 0)]).astype(F32)
+    if n_head == 2 and cols % HD == 0:
+        mine = lax.axis_index("head") * (cols // HD)
+        other = (cols // HD) - mine
+        sent = finish(other[None], cols, BF16, attended, later, projected)
+        got = lax.ppermute(sent, "head", [(0, 1), (1, 0)])
+        kept = finish(mine[None], cols, F32, in_order(attended, sent), later, projected)
+        summed = kept + got.astype(F32)
     else:
-        summed = lax.psum_scatter(projected, "head", scatter_dimension=1, tiled=True)
+        zero = jnp.zeros((1,), jnp.int32)
+        ready = finish(zero, projected.shape[1], F32, attended, later, projected)
+        summed = lax.psum_scatter(ready, "head", scatter_dimension=1, tiled=True)
     return (time_gate * summed).astype(BF16)
 
 

time: 77.1 us -> 76.9 us (level)
  no operation moved by 1% of the time
where the time goes in v7:
time: 76.9 us; the launch traced here: 76.4 us
  starting transfers between devices  28.3 us (37%)
  Pallas kernels  22.4 us (29%)
  waiting for transfers between devices  21.5 us (28%)
  between operations  1.73 us (2%)
  other arithmetic  1.28 us (2%)
    pallas_call x5, Pallas kernels, attend(): pl.pallas_call(functools.partial(attend_kernel, start, heads, width), out...  14.8 us
    ppermute x3, waiting for transfers between devices, send_out(): got = lax.ppermute(attended, 'slab', outward[j])  13.6 us
    ppermute x3, starting transfers between devices, send_in(): lax.ppermute(sent, 'slab', inward[side - 2])  9.42 us
    ppermute x2, starting transfers between devices, send_both(): got = lax.ppermute(sent, 'slab', inward[0] + outward[0])  6.71 us
    ppermute x1, waiting for transfers between devices, local(): got = lax.ppermute(sent, 'head', [(0, 1), (1, 0)])  4.71 us
    ppermute x3, starting transfers between devices, send_out(): got = lax.ppermute(attended, 'slab', outward[j])  4.06 us
    pallas_call x1, Pallas kernels, project(): pl.pallas_call(functools.partial(project_kernel, bounds), out_shape=(jax....  3.7 us
    ppermute x5, starting transfers between devices, fold(): lax.ppermute(folded[c], 'slab', [(side - 1, side), (side, side - 1)])  3.39 us
  transfers between devices with their start and end apart: 16, of which 6 were waited for; matrix products, arithmetic and copies ran while one was open for 2% of the time, Pallas kernels for 22%

profile of v7, /device:TPU:0, one launch (start us, length us, event | category | flops | bytes accessed | tf_op | source)
XLA Modules:
  0.0 76.4 jit_solution(11928907773783328208)
XLA Ops:
  0.0 0.0 copy-start
  0.0 1.8 %prepare.1 = (f32[8,256]{1,0:T(8,128)S(1)}, bf16[256,2560]{1,0:T(8,128)(2,1)S(1)}) custom-call(bf16[256,2560]{1,0:T(8,128)(2,1)} %q_hbm.11, bf16[64,2560]{1,0:T(8,128)(2,1)} %fk.1, bf16[64,2560]{1,0:T(8,128)(2,1)} %nk.1, bf16[64,2560]{1,0:T(8,128)(2,1)} %fv.1, bf16[64,2560]{1,0:T(8,128)(2,1)} %nv.1), custom_call_target="tpu_custom_call" | custom-call | flops 1310720 | bytes 5242880 | tf_op jit(solution)/shard_map/prepare/pallas_call | solution.py:94
  1.8 0.0 copy-start.1
  1.8 0.6 collective-permute-start.1
  2.4 2.6 %collective-permute-start = (f32[8,256]{1,0:T(8,128)S(1)}, f32[8,256]{1,0:T(8,128)S(1)}, u32[]{:S(2)}, u32[]{:S(2)}) collective-permute-start(f32[8,256]{1,0:T(8,128)S(1)} %get-tuple-element.26.own_sq), channel_id=1, source_target_pairs={{0,2},{2,0},{1,3},{3,1},{4,6},{6,4},{5,7},{7,5},{8,10},{10,8},{9,1... | collective-permute-start | bytes 24584 | tf_op jit(solution)/shard_map/ppermute | solution.py:375
  5.6 0.0 copy-done.3
  5.6 0.6 broadcast_in_dim.11.gain_hbm
  6.2 0.4 collective-permute-done.far_sq
  6.6 0.0 collective-permute-done.1.far_hbm
  6.6 0.0 copy-done.1
  6.6 2.9 %attend.5.refs_0_ = bf16[400,256]{1,0:T(8,128)(2,1)S(1)} custom-call(s32[1]{0:T(128)S(6)} %convert_element_type.21.owner_ref, f32[8,256]{1,0:T(8,128)S(1)} %get-tuple-element.26.own_sq, f32[8,256]{1,0:T(8,128)S(1)} %collective-permute-done.far_sq, f32[1,2560]{1,0:T(1,128)} %broadcast_in_dim.11.gain_hbm, bf16[256,2560]{1,0:T(8,128)(2,1)} %q_hbm.11, ...), custom_call_target="tpu_custom_call" | custom-call | flops 1207959552 | bytes 1179648 | tf_op jit(solution)/shard_map/attend/pallas_call | solution.py:228
  9.5 0.0 copy-done.2
  9.5 4.0 %collective-permute-start.2 = (bf16[400,256]{1,0:T(8,128)(2,1)S(1)}, bf16[400,256]{1,0:T(8,128)(2,1)S(1)}, u32[]{:S(2)}, u32[]{:S(2)}) collective-permute-start(bf16[400,256]{1,0:T(8,128)(2,1)S(1)} %attend.5.refs_0_), channel_id=1, source_target_pairs={{0,4},{12,8},{1,5},{13,9},{2,6},{14,10},{3,7},{15,11},{16,20},{28,... | collective-permute-start | bytes 614408 | tf_op jit(solution)/shard_map/ppermute | solution.py:415
  13.6 3.3 %attend.6.refs_0_ = bf16[656,256]{1,0:T(8,128)(2,1)S(1)} custom-call(s32[1]{0:T(128)S(6)} %convert_element_type.21.owner_ref, f32[8,256]{1,0:T(8,128)S(1)} %get-tuple-element.26.own_sq, f32[8,256]{1,0:T(8,128)S(1)} %collective-permute-done.far_sq, f32[1,2560]{1,0:T(1,128)} %broadcast_in_dim.11.gain_hbm, bf16[256,2560]{1,0:T(8,128)(2,1)} %q_hbm.11, ...), custom_call_target="tpu_custom_call" | custom-call | flops 2013265920 | bytes 1966080 | tf_op jit(solution)/shard_map/attend/pallas_call | solution.py:228
  16.8 1.3 %collective-permute-start.4 = (bf16[656,256]{1,0:T(8,128)(2,1)S(1)}, bf16[656,256]{1,0:T(8,128)(2,1)S(1)}, u32[]{:S(2)}, u32[]{:S(2)}) collective-permute-start(bf16[656,256]{1,0:T(8,128)(2,1)S(1)} %attend.6.refs_0_), channel_id=1, source_target_pairs={{0,4},{12,8},{1,5},{13,9},{2,6},{14,10},{3,7},{15,11},{16,20},{28,... | collective-permute-start | bytes 1007624 | tf_op jit(solution)/shard_map/ppermute | solution.py:415
  18.1 2.9 %attend.7.refs_0_ = bf16[528,256]{1,0:T(8,128)(2,1)S(1)} custom-call(s32[1]{0:T(128)S(6)} %convert_element_type.21.owner_ref, f32[8,256]{1,0:T(8,128)S(1)} %get-tuple-element.26.own_sq, f32[8,256]{1,0:T(8,128)S(1)} %collective-permute-done.far_sq, f32[1,2560]{1,0:T(1,128)} %broadcast_in_dim.11.gain_hbm, bf16[256,2560]{1,0:T(8,128)(2,1)} %q_hbm.11, ...), custom_call_target="tpu_custom_call" | custom-call | flops 1610612736 | bytes 1572864 | tf_op jit(solution)/shard_map/attend/pallas_call | solution.py:228
  21.0 0.0 collective-permute-done.2.refs_1_
  21.0 0.1 merge.10.refs_0_
  21.2 0.7 collective-permute-start.3
  22.5 4.1 %collective-permute-start.6 = (bf16[528,256]{1,0:T(8,128)(2,1)S(1)}, bf16[528,256]{1,0:T(8,128)(2,1)S(1)}, u32[]{:S(2)}, u32[]{:S(2)}) collective-permute-start(bf16[528,256]{1,0:T(8,128)(2,1)S(1)} %attend.7.refs_0_), channel_id=1, source_target_pairs={{0,4},{12,8},{1,5},{13,9},{2,6},{14,10},{3,7},{15,11},{16,20},{28,... | collective-permute-start | bytes 811016 | tf_op jit(solution)/shard_map/ppermute | solution.py:415
  26.6 2.9 %attend.8.refs_0_ = bf16[528,256]{1,0:T(8,128)(2,1)S(1)} custom-call(s32[1]{0:T(128)S(6)} %convert_element_type.21.owner_ref, f32[8,256]{1,0:T(8,128)S(1)} %get-tuple-element.26.own_sq, f32[8,256]{1,0:T(8,128)S(1)} %collective-permute-done.far_sq, f32[1,2560]{1,0:T(1,128)} %broadcast_in_dim.11.gain_hbm, bf16[256,2560]{1,0:T(8,128)(2,1)} %q_hbm.11, ...), custom_call_target="tpu_custom_call" | custom-call | flops 1610612736 | bytes 1572864 | tf_op jit(solution)/shard_map/attend/pallas_call | solution.py:228
  29.5 0.0 collective-permute-done.4.refs_1_
  29.5 0.2 merge.11.refs_0_
  29.6 0.7 collective-permute-start.5
  30.3 0.0 collective-permute-done.3.refs_1_
  30.3 0.1 merge.12
  30.5 0.1 pad_select_fusion.1
  30.5 1.1 %collective-permute-start.9 = (bf16[528,256]{1,0:T(8,128)(2,1)S(1)}, bf16[528,256]{1,0:T(8,128)(2,1)S(1)}, u32[]{:S(2)}, u32[]{:S(2)}) collective-permute-start(bf16[528,256]{1,0:T(8,128)(2,1)S(1)} %pad_select_fusion.1), channel_id=1, source_target_pairs={{0,4},{12,8},{4,0},{8,12},{1,5},{13,9},{5,1},{9,13},{2,6},{14,10},... | collective-permute-start | bytes 811016 | tf_op jit(solution)/shard_map/ppermute | solution.py:444
  31.6 2.9 %attend.9.refs_0_ = bf16[528,256]{1,0:T(8,128)(2,1)S(1)} custom-call(s32[1]{0:T(128)S(6)} %convert_element_type.21.owner_ref, f32[8,256]{1,0:T(8,128)S(1)} %get-tuple-element.26.own_sq, f32[8,256]{1,0:T(8,128)S(1)} %collective-permute-done.far_sq, f32[1,2560]{1,0:T(1,128)} %broadcast_in_dim.11.gain_hbm, bf16[256,2560]{1,0:T(8,128)(2,1)} %q_hbm.11, ...), custom_call_target="tpu_custom_call" | custom-call | flops 1610612736 | bytes 1572864 | tf_op jit(solution)/shard_map/attend/pallas_call | solution.py:228
  34.5 0.0 collective-permute-done.6.refs_1_
  34.5 0.1 merge.13.refs_0_
  34.7 0.7 collective-permute-start.8
  35.3 0.1 fusion
  35.4 0.0 collective-permute-done.5.refs_1_
  35.4 0.2 merge.14
  35.6 0.1 pad_select_fusion
  35.7 5.6 %collective-permute-start.7 = (bf16[656,256]{1,0:T(8,128)(2,1)S(1)}, bf16[656,256]{1,0:T(8,128)(2,1)S(1)}, u32[]{:S(2)}, u32[]{:S(2)}) collective-permute-start(bf16[656,256]{1,0:T(8,128)(2,1)S(1)} %pad_select_fusion), channel_id=1, source_target_pairs={{0,4},{12,8},{4,0},{8,12},{1,5},{13,9},{5,1},{9,13},{2,6},{14,10},... | collective-permute-start | bytes 1007624 | tf_op jit(solution)/shard_map/ppermute | solution.py:444
  41.3 0.0 collective-permute-done.9.refs_1_
  41.3 0.1 merge.15.refs_0_
  41.4 0.7 collective-permute-start.11
  42.1 0.0 collective-permute-done.8.refs_1_
  42.1 0.1 merge.16
  42.3 1.3 %collective-permute-start.13 = (bf16[512,256]{1,0:T(8,128)(2,1)S(1)}, bf16[512,256]{1,0:T(8,128)(2,1)S(1)}, u32[]{:S(2)}, u32[]{:S(2)}) collective-permute-start(bf16[512,256]{1,0:T(8,128)(2,1)S(1)} %slice.30), channel_id=1, source_target_pairs={{4,0},{8,12},{5,1},{9,13},{6,2},{10,14},{7,3},{11,15},{20,16},{24,... | collective-permute-start | bytes 786440 | tf_op jit(solution)/shard_map/ppermute | solution.py:430
  43.6 2.8 %collective-permute-done.7 = bf16[656,256]{1,0:T(8,128)(2,1)S(1)} collective-permute-done((bf16[656,256]{1,0:T(8,128)(2,1)S(1)}, bf16[656,256]{1,0:T(8,128)(2,1)S(1)}, u32[]{:S(2)}, u32[]{:S(2)}) %collective-permute-start.7) | collective-permute-done | bytes 335904 | tf_op jit(solution)/shard_map/ppermute | solution.py:444
  46.5 0.1 merge.17.refs_0_
  46.6 0.0 collective-permute-done.11.refs_1_
  46.6 0.1 merge.18
  46.8 1.3 %collective-permute-start.14 = (bf16[512,256]{1,0:T(8,128)(2,1)S(1)}, bf16[512,256]{1,0:T(8,128)(2,1)S(1)}, u32[]{:S(2)}, u32[]{:S(2)}) collective-permute-start(bf16[512,256]{1,0:T(8,128)(2,1)S(1)} %slice.31), channel_id=1, source_target_pairs={{4,0},{8,12},{5,1},{9,13},{6,2},{10,14},{7,3},{11,15},{20,16},{24,... | collective-permute-start | bytes 786440 | tf_op jit(solution)/shard_map/ppermute | solution.py:430
  48.1 4.7 %collective-permute-done.13 = bf16[512,256]{1,0:T(8,128)(2,1)S(1)} collective-permute-done((bf16[512,256]{1,0:T(8,128)(2,1)S(1)}, bf16[512,256]{1,0:T(8,128)(2,1)S(1)}, u32[]{:S(2)}, u32[]{:S(2)}) %collective-permute-start.13) | collective-permute-done | bytes 262176 | tf_op jit(solution)/shard_map/ppermute | solution.py:430
  52.9 0.7 collective-permute-start.10
  53.6 4.7 %collective-permute-done.14 = bf16[512,256]{1,0:T(8,128)(2,1)S(1)} collective-permute-done((bf16[512,256]{1,0:T(8,128)(2,1)S(1)}, bf16[512,256]{1,0:T(8,128)(2,1)S(1)}, u32[]{:S(2)}, u32[]{:S(2)}) %collective-permute-start.14) | collective-permute-done | bytes 262176 | tf_op jit(solution)/shard_map/ppermute | solution.py:430
  58.3 0.0 collective-permute-done.10.refs_1_
  58.3 0.1 merge.19
  58.5 1.5 %collective-permute-start.12 = (bf16[512,256]{1,0:T(8,128)(2,1)S(1)}, bf16[512,256]{1,0:T(8,128)(2,1)S(1)}, u32[]{:S(2)}, u32[]{:S(2)}) collective-permute-start(bf16[512,256]{1,0:T(8,128)(2,1)S(1)} %slice.25), channel_id=1, source_target_pairs={{4,0},{8,12},{5,1},{9,13},{6,2},{10,14},{7,3},{11,15},{20,16},{24,... | collective-permute-start | bytes 786440 | tf_op jit(solution)/shard_map/ppermute | solution.py:430
  60.0 0.1 pad_maximum_fusion.attended_ref
  60.1 3.7 %project.1 = (f32[256,1280]{1,0:T(8,128)S(1)}, bf16[512,1280]{1,0:T(8,128)(2,1)S(1)}) custom-call(bf16[2048,256]{1,0:T(8,128)(2,1)S(1)} %pad_maximum_fusion.attended_ref, bf16[2560,1280]{1,0:T(8,128)(2,1)} %weight_hbm.1), custom_call_target="tpu_custom_call" | custom-call | flops 1342177280 | bytes 6553600 | tf_op jit(solution)/shard_map/project/pallas_call | solution.py:315
  63.8 4.2 %collective-permute-done.12 = bf16[512,256]{1,0:T(8,128)(2,1)S(1)} collective-permute-done((bf16[512,256]{1,0:T(8,128)(2,1)S(1)}, bf16[512,256]{1,0:T(8,128)(2,1)S(1)}, u32[]{:S(2)}, u32[]{:S(2)}) %collective-permute-start.12) | collective-permute-done | bytes 262176 | tf_op jit(solution)/shard_map/ppermute | solution.py:430
  68.0 0.4 finish.2
  68.4 1.6 %collective-permute-start.15 = (bf16[256,640]{1,0:T(8,128)(2,1)S(1)}, bf16[256,640]{1,0:T(8,128)(2,1)S(1)}, u32[]{:S(2)}, u32[]{:S(2)}) collective-permute-start(bf16[256,640]{1,0:T(8,128)(2,1)S(1)} %finish.2), channel_id=1, source_target_pairs={{0,2},{2,0},{1,3},{3,1},{4,6},{6,4},{5,7},{7,5},{8,10},{10,8},{9,1... | collective-permute-start | bytes 983048 | tf_op jit(solution)/shard_map/ppermute | solution.py:467
  70.0 0.0 copy-done
  70.0 0.4 convolution_reduce_fusion
  70.4 0.4 finish.3
  70.8 4.7 %collective-permute-done.15 = bf16[256,640]{1,0:T(8,128)(2,1)S(1)} collective-permute-done((bf16[256,640]{1,0:T(8,128)(2,1)S(1)}, bf16[256,640]{1,0:T(8,128)(2,1)S(1)}, u32[]{:S(2)}, u32[]{:S(2)}) %collective-permute-start.15) | collective-permute-done | bytes 327712 | tf_op jit(solution)/shard_map/ppermute | solution.py:467
  75.5 0.8 %multiply_convert_fusion = bf16[256,640]{1,0:T(8,128)(2,1)} fusion(f32[256,640]{1,0:T(8,128)S(1)} %finish.3, bf16[256,640]{1,0:T(8,128)(2,1)S(1)} %collective-permute-done.15, f32[640]{0:T(1024)S(1)} %broadcast_add_fusion), kind=kLoop, calls=%fused_computation.2 | loop fusion | flops 655360 | bytes 1313280 | tf_op jit(solution)/shard_map/convert_element_type | solution.py:474
  (13 shorter events, 0.3 us)
Async XLA Ops:
  0.0 70.0 %copy-start = (f32[256,640]{1,0:T(8,128)S(1)}, f32[256,640]{1,0:T(8,128)}, u32[]{:S(2)}) copy-start(f32[256,640]{1,0:T(8,128)} %param.21) | copy-start | bytes 1966084
  0.0 5.6 %copy-start.3 = (f32[2560]{0:T(1024)S(1)}, f32[2560]{0:T(1024)}, u32[]{:S(2)}) copy-start(f32[2560]{0:T(1024)} %param.13) | copy-start | bytes 30724
  1.8 4.8 %copy-start.1 = (bf16[256,2560]{1,0:T(8,128)(2,1)}, bf16[256,2560]{1,0:T(8,128)(2,1)S(1)}, u32[]{:S(2)}) copy-start(bf16[256,2560]{1,0:T(8,128)(2,1)S(1)} %get-tuple-element.27.near_hbm) | copy-start | bytes 3932164
  1.8 4.7 %collective-permute-start.1 = (bf16[256,2560]{1,0:T(8,128)(2,1)S(1)}, bf16[256,2560]{1,0:T(8,128)(2,1)S(1)}, u32[]{:S(2)}, u32[]{:S(2)}) collective-permute-start(bf16[256,2560]{1,0:T(8,128)(2,1)S(1)} %get-tuple-element.27.near_hbm), channel_id=1, source_target_pairs={{0,1},{1,0},{2,3},{3,2},{4,5},{5,4},{6,7},{7,6},{8,9},{9,8},{10,11... | collective-permute-start | bytes 3932168 | tf_op jit(solution)/shard_map/ppermute | solution.py:379
  2.4 4.2 %collective-permute-start = (f32[8,256]{1,0:T(8,128)S(1)}, f32[8,256]{1,0:T(8,128)S(1)}, u32[]{:S(2)}, u32[]{:S(2)}) collective-permute-start(f32[8,256]{1,0:T(8,128)S(1)} %get-tuple-element.26.own_sq), channel_id=1, source_target_pairs={{0,2},{2,0},{1,3},{3,1},{4,6},{6,4},{5,7},{7,5},{8,10},{10,8},{9,1... | collective-permute-start | bytes 24584 | tf_op jit(solution)/shard_map/ppermute | solution.py:375
  6.6 2.9 %copy-start.2 = (bf16[256,2560]{1,0:T(8,128)(2,1)}, bf16[256,2560]{1,0:T(8,128)(2,1)S(1)}, u32[]{:S(2)}) copy-start(bf16[256,2560]{1,0:T(8,128)(2,1)S(1)} %collective-permute-done.1.far_hbm) | copy-start | bytes 3932164
  9.5 11.5 %collective-permute-start.2 = (bf16[400,256]{1,0:T(8,128)(2,1)S(1)}, bf16[400,256]{1,0:T(8,128)(2,1)S(1)}, u32[]{:S(2)}, u32[]{:S(2)}) collective-permute-start(bf16[400,256]{1,0:T(8,128)(2,1)S(1)} %attend.5.refs_0_), channel_id=1, source_target_pairs={{0,4},{12,8},{1,5},{13,9},{2,6},{14,10},{3,7},{15,11},{16,20},{28,... | collective-permute-start | bytes 614408 | tf_op jit(solution)/shard_map/ppermute | solution.py:415
  16.8 12.6 %collective-permute-start.4 = (bf16[656,256]{1,0:T(8,128)(2,1)S(1)}, bf16[656,256]{1,0:T(8,128)(2,1)S(1)}, u32[]{:S(2)}, u32[]{:S(2)}) collective-permute-start(bf16[656,256]{1,0:T(8,128)(2,1)S(1)} %attend.6.refs_0_), channel_id=1, source_target_pairs={{0,4},{12,8},{1,5},{13,9},{2,6},{14,10},{3,7},{15,11},{16,20},{28,... | collective-permute-start | bytes 1007624 | tf_op jit(solution)/shard_map/ppermute | solution.py:415
  21.2 9.2 %collective-permute-start.3 = (bf16[400,256]{1,0:T(8,128)(2,1)S(1)}, bf16[400,256]{1,0:T(8,128)(2,1)S(1)}, u32[]{:S(2)}, u32[]{:S(2)}) collective-permute-start(bf16[400,256]{1,0:T(8,128)(2,1)S(1)} %merge.10.refs_0_), channel_id=1, source_target_pairs={{4,8},{8,4},{5,9},{9,5},{6,10},{10,6},{7,11},{11,7},{20,24},{24,20... | collective-permute-start | bytes 614408 | tf_op jit(solution)/shard_map/ppermute | solution.py:421
  22.5 12.0 %collective-permute-start.6 = (bf16[528,256]{1,0:T(8,128)(2,1)S(1)}, bf16[528,256]{1,0:T(8,128)(2,1)S(1)}, u32[]{:S(2)}, u32[]{:S(2)}) collective-permute-start(bf16[528,256]{1,0:T(8,128)(2,1)S(1)} %attend.7.refs_0_), channel_id=1, source_target_pairs={{0,4},{12,8},{1,5},{13,9},{2,6},{14,10},{3,7},{15,11},{16,20},{28,... | collective-permute-start | bytes 811016 | tf_op jit(solution)/shard_map/ppermute | solution.py:415
  29.6 5.8 %collective-permute-start.5 = (bf16[656,256]{1,0:T(8,128)(2,1)S(1)}, bf16[656,256]{1,0:T(8,128)(2,1)S(1)}, u32[]{:S(2)}, u32[]{:S(2)}) collective-permute-start(bf16[656,256]{1,0:T(8,128)(2,1)S(1)} %merge.11.refs_0_), channel_id=1, source_target_pairs={{4,8},{8,4},{5,9},{9,5},{6,10},{10,6},{7,11},{11,7},{20,24},{24,20... | collective-permute-start | bytes 1007624 | tf_op jit(solution)/shard_map/ppermute | solution.py:421
  30.5 10.7 %collective-permute-start.9 = (bf16[528,256]{1,0:T(8,128)(2,1)S(1)}, bf16[528,256]{1,0:T(8,128)(2,1)S(1)}, u32[]{:S(2)}, u32[]{:S(2)}) collective-permute-start(bf16[528,256]{1,0:T(8,128)(2,1)S(1)} %pad_select_fusion.1), channel_id=1, source_target_pairs={{0,4},{12,8},{4,0},{8,12},{1,5},{13,9},{5,1},{9,13},{2,6},{14,10},... | collective-permute-start | bytes 811016 | tf_op jit(solution)/shard_map/ppermute | solution.py:444
  34.7 7.4 %collective-permute-start.8 = (bf16[528,256]{1,0:T(8,128)(2,1)S(1)}, bf16[528,256]{1,0:T(8,128)(2,1)S(1)}, u32[]{:S(2)}, u32[]{:S(2)}) collective-permute-start(bf16[528,256]{1,0:T(8,128)(2,1)S(1)} %merge.13.refs_0_), channel_id=1, source_target_pairs={{4,8},{8,4},{5,9},{9,5},{6,10},{10,6},{7,11},{11,7},{20,24},{24,20... | collective-permute-start | bytes 811016 | tf_op jit(solution)/shard_map/ppermute | solution.py:421
  35.7 10.8 %collective-permute-start.7 = (bf16[656,256]{1,0:T(8,128)(2,1)S(1)}, bf16[656,256]{1,0:T(8,128)(2,1)S(1)}, u32[]{:S(2)}, u32[]{:S(2)}) collective-permute-start(bf16[656,256]{1,0:T(8,128)(2,1)S(1)} %pad_select_fusion), channel_id=1, source_target_pairs={{0,4},{12,8},{4,0},{8,12},{1,5},{13,9},{5,1},{9,13},{2,6},{14,10},... | collective-permute-start | bytes 1007624 | tf_op jit(solution)/shard_map/ppermute | solution.py:444
  41.4 5.2 %collective-permute-start.11 = (bf16[528,256]{1,0:T(8,128)(2,1)S(1)}, bf16[528,256]{1,0:T(8,128)(2,1)S(1)}, u32[]{:S(2)}, u32[]{:S(2)}) collective-permute-start(bf16[528,256]{1,0:T(8,128)(2,1)S(1)} %merge.15.refs_0_), channel_id=1, source_target_pairs={{4,8},{8,4},{5,9},{9,5},{6,10},{10,6},{7,11},{11,7},{20,24},{24,20... | collective-permute-start | bytes 811016 | tf_op jit(solution)/shard_map/ppermute | solution.py:421
  42.3 10.5 %collective-permute-start.13 = (bf16[512,256]{1,0:T(8,128)(2,1)S(1)}, bf16[512,256]{1,0:T(8,128)(2,1)S(1)}, u32[]{:S(2)}, u32[]{:S(2)}) collective-permute-start(bf16[512,256]{1,0:T(8,128)(2,1)S(1)} %slice.30), channel_id=1, source_target_pairs={{4,0},{8,12},{5,1},{9,13},{6,2},{10,14},{7,3},{11,15},{20,16},{24,... | collective-permute-start | bytes 786440 | tf_op jit(solution)/shard_map/ppermute | solution.py:430
  46.8 11.5 %collective-permute-start.14 = (bf16[512,256]{1,0:T(8,128)(2,1)S(1)}, bf16[512,256]{1,0:T(8,128)(2,1)S(1)}, u32[]{:S(2)}, u32[]{:S(2)}) collective-permute-start(bf16[512,256]{1,0:T(8,128)(2,1)S(1)} %slice.31), channel_id=1, source_target_pairs={{4,0},{8,12},{5,1},{9,13},{6,2},{10,14},{7,3},{11,15},{20,16},{24,... | collective-permute-start | bytes 786440 | tf_op jit(solution)/shard_map/ppermute | solution.py:430
  52.9 5.5 %collective-permute-start.10 = (bf16[528,256]{1,0:T(8,128)(2,1)S(1)}, bf16[528,256]{1,0:T(8,128)(2,1)S(1)}, u32[]{:S(2)}, u32[]{:S(2)}) collective-permute-start(bf16[528,256]{1,0:T(8,128)(2,1)S(1)} %merge.17.refs_0_), channel_id=1, source_target_pairs={{4,8},{8,4},{5,9},{9,5},{6,10},{10,6},{7,11},{11,7},{20,24},{24,20... | collective-permute-start | bytes 811016 | tf_op jit(solution)/shard_map/ppermute | solution.py:421
  58.5 9.4 %collective-permute-start.12 = (bf16[512,256]{1,0:T(8,128)(2,1)S(1)}, bf16[512,256]{1,0:T(8,128)(2,1)S(1)}, u32[]{:S(2)}, u32[]{:S(2)}) collective-permute-start(bf16[512,256]{1,0:T(8,128)(2,1)S(1)} %slice.25), channel_id=1, source_target_pairs={{4,0},{8,12},{5,1},{9,13},{6,2},{10,14},{7,3},{11,15},{20,16},{24,... | collective-permute-start | bytes 786440 | tf_op jit(solution)/shard_map/ppermute | solution.py:430
  68.4 7.1 %collective-permute-start.15 = (bf16[256,640]{1,0:T(8,128)(2,1)S(1)}, bf16[256,640]{1,0:T(8,128)(2,1)S(1)}, u32[]{:S(2)}, u32[]{:S(2)}) collective-permute-start(bf16[256,640]{1,0:T(8,128)(2,1)S(1)} %finish.2), channel_id=1, source_target_pairs={{0,2},{2,0},{1,3},{3,1},{4,6},{6,4},{5,7},{7,5},{8,10},{10,8},{9,1... | collective-permute-start | bytes 983048 | tf_op jit(solution)/shard_map/ppermute | solution.py:467
